TPU v7x, 32 devices: a whole 2x2x4 slice. The times are simulated.
32 devices in a mesh: pair: 2 (over x), day: 4 (over z), lag: 4 (over y, core).
Axes of the slice: x: 2, y: 2, z: 4, core: 2. Of those that a mesh axis runs over, the one named last changes fastest.
Arguments:
- corr: bfloat16 [2048, 16, 2048], P('pair', 'day', 'lag'), may hold values from -150 to 150
Outputs:
- pws_stack: float32 [2048, 2048], P('pair', 'lag')
- robust_stack: float32 [2048, 2048], P('pair', 'lag')
- day_weights: float32 [2048, 16], P('pair', 'day')
All inputs are finite; a program needn't handle non-finite values.
Results may differ from a plain program's by a relative error of at most 0.00049.
Values may be sent and summed in bfloat16 or wider, within the bound.
No kernel may reach another device: no remote copies, remote signals or barrier semaphores. Data moves between devices by JAX's collectives and lax.ppermute only.
A program may use at most 128 MiB of HBM per device.

v0:
```python
import jax
import jax.numpy as jnp
from jax import lax
from jax.sharding import PartitionSpec as P

ITERS = 3


epsilon = 1e-06


def kernel_block(rows, cols, lags):
    offset = (cols[None, :] - rows[:, None]) % lags
    odd = offset % 2 == 1
    angle = jnp.pi * offset.astype(jnp.float32) / lags
    value = jnp.where(odd, 2.0 / lags * jnp.cos(angle) / jnp.where(odd, jnp.sin(angle), 1.0), 0.0)
    return value.astype(jnp.bfloat16)


def per_device(corr):
    width_in = corr.shape[2]
    lags = width_in * lax.axis_size("lag")
    pairs, days_here, width = corr.shape
    days = days_here * lax.axis_size("day")
    data = corr.astype(jnp.float32)
    squares = jnp.sum(data * data, axis=2)
    norm2 = lax.psum(squares, "lag")
    rms = jnp.sqrt(norm2 / lags + epsilon)
    xn = data / rms[:, :, None]
    local_lags = lax.axis_index("lag") * width + jnp.arange(width, dtype=jnp.int32)
    piece = lax.all_gather(corr, "lag", axis=2, tiled=True)
    count = piece.shape[2]
    rows = jnp.arange(count, dtype=jnp.int32)
    block = kernel_block(rows, local_lags, lags)
    quad = jnp.dot(
        piece.reshape(pairs * days_here, count), block, preferred_element_type=jnp.float32
    )
    quad = quad.reshape(pairs, days_here, width)
    den = jnp.maximum(jnp.sqrt(data * data + quad * quad), 0.1 * rms[:, :, None])
    cosine = data / den
    sine = quad / den
    linear, csum, ssum = lax.psum(
        (jnp.sum(xn, axis=1), jnp.sum(cosine, axis=1), jnp.sum(sine, axis=1)), "day"
    )
    pws = linear / days * ((csum * csum + ssum * ssum) / (days * days))
    stack = pws
    for step in range(ITERS):
        energy = jnp.sum(stack * stack, axis=1)
        msq = lax.psum(energy, "lag") / lags
        normed = stack / jnp.sqrt(msq + epsilon)[:, None]
        inner = jnp.sum(xn * normed[:, None, :], axis=2)
        coh = lax.psum(inner, "lag") / lags
        mean_data = norm2 / lags / (norm2 / lags + epsilon)
        mean_stack = msq / (msq + epsilon)
        res = mean_data - 2.0 * coh * coh + coh * coh * mean_stack[:, None]
        rbar = lax.psum(jnp.sum(res, axis=1), "day") / days
        weight = (0.1 + jnp.abs(coh)) / (res + rbar[:, None] + epsilon)
        stack, total = lax.psum(
            (jnp.sum(weight[:, :, None] * xn, axis=1), jnp.sum(weight, axis=1)), "day"
        )
    robust = stack / total[:, None]
    shares = weight / total[:, None]
    return (pws, robust, shares)


def solution(mesh):
    return jax.shard_map(
        per_device,
        mesh=mesh,
        in_specs=(P("pair", "day", "lag"),),
        out_specs=(P("pair", "lag"), P("pair", "lag"), P("pair", "day")),
        check_vma=False,
    )
```

profile of v0, /device:TPU:0, one launch (start us, length us, event | category | flops | bytes accessed | tf_op | source)
XLA Modules:
  0.0 833.6 jit_solution(3083666384770448746)
XLA Ops:
  12.6 12.7 %psum.119 = f32[1024,4]{0,1:T(4,128)S(1)} all-reduce(f32[1024,4]{0,1:T(4,128)S(1)} %copy.20), channel_id=1, replica_groups=mesh['pair'=2,'day'=4,'lag'=4] {'lag'}, use_global_device_ids=true, to_apply=%region_1.0 | all-reduce | flops 4096 | bytes 32768 | tf_op jit(solution)/shard_map/psum | solution.py:27
  25.8 20.1 %select_convert_fusion.4 = bf16[2048,512]{1,0:T(8,128)(2,1)} fusion(s32[512]{0:T(512)S(1)} %iota_add_fusion), kind=kLoop, calls=%fused_computation.25.clone.clone.1 | loop fusion | flops 32505856 | bytes 2099200 | tf_op jit(solution)/shard_map/dot_general | solution.py:35
  46.0 74.5 %all-gather.2.cloned.1.call-done = bf16[1024,4,2048]{2,1,0:T(4,128)(2,1)} async-done(((bf16[1024,4,512]{2,1,0:T(4,128)(2,1)}), bf16[1024,4,2048]{2,1,0:T(4,128)(2,1)}) %all-gather.2.cloned.1.call-update) | async-done | bytes 16777232 | tf_op jit(solution)/shard_map/all_gather | solution.py:31
  120.4 23.7 %reshape.35 = bf16[4096,2048]{1,0:T(8,128)(2,1)} reshape(bf16[1024,4,2048]{2,1,0:T(4,128)(2,1)} %all-gather.2.cloned.1.call-done) | data formatting | bytes 33554432 | tf_op jit(solution)/shard_map/reshape | solution.py:36
  144.1 15.1 %convolution_bitcast_fusion = f32[4096,512]{0,1:T(8,128)} fusion(bf16[4096,2048]{1,0:T(8,128)(2,1)} %reshape.35, bf16[2048,512]{1,0:T(8,128)(2,1)} %select_convert_fusion.4), kind=kOutput, calls=%fused_computation.15 | convolution fusion | flops 8589934592 | bytes 27262976 | tf_op jit(solution)/shard_map/dot_general | solution.py:35
  159.2 9.0 %copy.22 = f32[4096,512]{1,0:T(8,128)} copy(f32[4096,512]{0,1:T(8,128)} %convolution_bitcast_fusion) | data formatting | bytes 16777216 | tf_op jit(solution)/shard_map/dot_general | solution.py:35
  168.2 9.8 %reshape.36 = f32[1024,4,512]{2,1,0:T(4,128)} reshape(f32[4096,512]{1,0:T(8,128)} %copy.22) | data formatting | bytes 16777216 | tf_op jit(solution)/shard_map/reshape | solution.py:38
  178.0 32.5 %fusion.37 = (f32[1024,512]{1,0:T(8,128)}, f32[1024,4,512]{2,1,0:T(4,128)}, f32[1024,512]{1,0:T(8,128)}, f32[1024,512]{1,0:T(8,128)}) fusion(f32[1024,4]{1,0:T(8,128)S(1)} %copy.21, bf16[1024,4,512]{2,1,0:T(4,128)(2,1)} %param.1, f32[1024,4,512]{2,1,0:T(4,128)} %reshape.36, f32[1024,4]{1,0:T(8,128)S(1)} %copy.23), kind=kLoop, calls=%fused_computation.83 | loop fusion | flops 21495808 | bytes 27295744 | tf_op jit(solution)/shard_map/reduce_sum | solution.py:43
  210.6 222.9 %all-reduce.12.cloned.1.call-done = (f32[1024,512]{1,0:T(8,128)}, f32[1024,512]{1,0:T(8,128)}, f32[1024,512]{1,0:T(8,128)}) async-done(((f32[1024,512]{1,0:T(8,128)}, f32[1024,512]{1,0:T(8,128)}, f32[1024,512]{1,0:T(8,128)}), (f32[1024,512]{1,0:T(8,128)}, f32[1024,512]{1,0:T(8,128)}, f32[1024,512]{1,0:T(8,128)})) %all-reduce.12.cloned.1.call-update) | async-done | bytes 6291472 | tf_op jit(solution)/shard_map/psum | solution.py:42
  437.0 6.4 psum.123
  445.0 6.3 multiply_reduce_fusion.5
  451.4 10.2 %psum.124 = f32[1024,4]{0,1:T(4,128)S(1)} all-reduce(f32[1024,4]{0,1:T(4,128)S(1)} %copy.24), channel_id=1, replica_groups=mesh['pair'=2,'day'=4,'lag'=4] {'lag'}, use_global_device_ids=true, to_apply=%region_11.12 | all-reduce | flops 4096 | bytes 32768 | tf_op jit(solution)/shard_map/psum | solution.py:52
  461.6 10.0 %psum.125 = f32[1024]{0:T(1024)S(1)} all-reduce(f32[1024]{0:T(1024)S(1)} %fusion.23), channel_id=1, replica_groups=mesh['pair'=2,'day'=4,'lag'=4] {'day'}, use_global_device_ids=true, to_apply=%region_13.14 | all-reduce | flops 1024 | bytes 8192 | tf_op jit(solution)/shard_map/psum | solution.py:56
  471.9 9.3 %multiply_reduce_fusion.4 = f32[1024,512]{1,0:T(8,128)} fusion(f32[1024,4,512]{2,1,0:T(4,128)} %get-tuple-element.16, f32[1024,4]{1,0:T(8,128)S(1)} %copy.25), kind=kLoop, calls=%fused_computation.11 | loop fusion | flops 3670016 | bytes 10502144 | tf_op jit(solution)/shard_map/reduce_sum | solution.py:59
  481.3 83.7 %all-reduce.6.cloned.1.call-done = f32[1024,512]{1,0:T(8,128)} async-done(((f32[1024,512]{1,0:T(8,128)}), f32[1024,512]{1,0:T(8,128)}) %all-reduce.6.cloned.1.call-update) | async-done | bytes 2097168 | tf_op jit(solution)/shard_map/psum | solution.py:58
  580.7 10.4 %psum.128 = f32[1024,4]{0,1:T(4,128)S(1)} all-reduce(f32[1024,4]{0,1:T(4,128)S(1)} %copy.26), channel_id=1, replica_groups=mesh['pair'=2,'day'=4,'lag'=4] {'lag'}, use_global_device_ids=true, to_apply=%region_19.20 | all-reduce | flops 4096 | bytes 32768 | tf_op jit(solution)/shard_map/psum | solution.py:52
  591.0 10.1 %psum.129 = f32[1024]{0:T(1024)S(1)} all-reduce(f32[1024]{0:T(1024)S(1)} %fusion.24), channel_id=1, replica_groups=mesh['pair'=2,'day'=4,'lag'=4] {'day'}, use_global_device_ids=true, to_apply=%region_21.22 | all-reduce | flops 1024 | bytes 8192 | tf_op jit(solution)/shard_map/psum | solution.py:56
  601.5 9.3 %multiply_reduce_fusion.2 = f32[1024,512]{1,0:T(8,128)} fusion(f32[1024,4,512]{2,1,0:T(4,128)} %get-tuple-element.16, f32[1024,4]{1,0:T(8,128)S(1)} %copy.27), kind=kLoop, calls=%fused_computation.9 | loop fusion | flops 3670016 | bytes 10502144 | tf_op jit(solution)/shard_map/reduce_sum | solution.py:59
  610.8 83.6 %all-reduce.8.cloned.1.call-done = f32[1024,512]{1,0:T(8,128)} async-done(((f32[1024,512]{1,0:T(8,128)}), f32[1024,512]{1,0:T(8,128)}) %all-reduce.8.cloned.1.call-update) | async-done | bytes 2097168 | tf_op jit(solution)/shard_map/psum | solution.py:58
  710.1 10.4 %psum.132 = f32[1024,4]{0,1:T(4,128)S(1)} all-reduce(f32[1024,4]{0,1:T(4,128)S(1)} %copy.28), channel_id=1, replica_groups=mesh['pair'=2,'day'=4,'lag'=4] {'lag'}, use_global_device_ids=true, to_apply=%region_27.28 | all-reduce | flops 4096 | bytes 32768 | tf_op jit(solution)/shard_map/psum | solution.py:52
  720.5 10.1 %psum.133 = f32[1024]{0:T(1024)S(1)} all-reduce(f32[1024]{0:T(1024)S(1)} %fusion.34), channel_id=1, replica_groups=mesh['pair'=2,'day'=4,'lag'=4] {'day'}, use_global_device_ids=true, to_apply=%region_29.30 | all-reduce | flops 1024 | bytes 8192 | tf_op jit(solution)/shard_map/psum | solution.py:56
  730.9 9.3 %multiply_reduce_fusion = f32[1024,512]{1,0:T(8,128)} fusion(f32[1024,4,512]{2,1,0:T(4,128)} %get-tuple-element.16, f32[1024,4]{1,0:T(8,128)S(1)} %copy.29), kind=kLoop, calls=%fused_computation.7 | loop fusion | flops 3670016 | bytes 10502144 | tf_op jit(solution)/shard_map/reduce_sum | solution.py:59
  740.3 9.0 %psum.135 = f32[1024]{0:T(1024)S(1)} all-reduce(f32[1024]{0:T(1024)S(1)} %get-tuple-element.11), channel_id=1, replica_groups=mesh['pair'=2,'day'=4,'lag'=4] {'day'}, use_global_device_ids=true, to_apply=%region_33.34 | all-reduce | flops 1024 | bytes 8192 | tf_op jit(solution)/shard_map/psum | solution.py:58
  749.9 74.0 %all-reduce.10.cloned.1.call-done = f32[1024,512]{1,0:T(8,128)} async-done(((f32[1024,512]{1,0:T(8,128)}), f32[1024,512]{1,0:T(8,128)}) %all-reduce.10.cloned.1.call-update) | async-done | bytes 2097168 | tf_op jit(solution)/shard_map/psum | solution.py:58
  (48 shorter events, 47.3 us)
Async XLA Ops:
  7.2 113.3 %all-gather.2.cloned.1.call-start = ((), (), s32[]{:S(2)}) async-start(), calls=%async_computation | async-start | bytes 20971520 | tf_op jit(solution)/shard_map/all_gather | solution.py:31
  7.9 425.6 %all-reduce.12.cloned.1.call-start = ((), (), s32[]{:S(2)}) async-start(), calls=%async_computation.4 | async-start | bytes 12582912 | tf_op jit(solution)/shard_map/psum | solution.py:42
  210.5 354.4 %all-reduce.6.cloned.1.call-start = ((), (), s32[]{:S(2)}) async-start(), calls=%async_computation.1 | async-start | bytes 4194304 | tf_op jit(solution)/shard_map/psum | solution.py:58
  437.0 14.2 %copy-start = (f32[1024,512]{1,0:T(8,128)}, f32[1024,512]{1,0:T(8,128)S(1)}, u32[]{:S(2)}) copy-start(f32[1024,512]{1,0:T(8,128)S(1)} %get-tuple-element.14) | copy-start | bytes 6291460
  481.2 213.2 %all-reduce.8.cloned.1.call-start = ((), (), s32[]{:S(2)}) async-start(), calls=%async_computation.2 | async-start | bytes 4194304 | tf_op jit(solution)/shard_map/psum | solution.py:58
  610.8 213.2 %all-reduce.10.cloned.1.call-start = ((), (), s32[]{:S(2)}) async-start(), calls=%async_computation.3 | async-start | bytes 4194304 | tf_op jit(solution)/shard_map/psum | solution.py:58
Sparse Core Ops, SparseCore 0:
  9.5 110.8 all-gather.1
  210.7 222.8 all-reduce.11
  481.3 83.5 all-reduce.5
  610.9 83.4 all-reduce.7
  740.4 83.5 all-reduce.9
where the time goes:
time: 835 us; the launch traced here: 834 us
  waiting for transfers between devices  539 us (65%)
  other arithmetic  119 us (14%)
  blocking collectives  102 us (12%)
  local copies, waits for them, and re-layouts  44.3 us (5%)
  matrix products  15.1 us (2%)
  between operations  13.9 us (2%)
    psum x3, waiting for transfers between devices, per_device(): lax.psum((jnp.sum(weight[:, :, None] * xn, axis=1), jnp.sum(weight, axis=...  241 us
    psum x1, waiting for transfers between devices, per_device(): lax.psum((jnp.sum(xn, axis=1), jnp.sum(cosine, axis=1), jnp.sum(sine, axi...  223 us
    all_gather x1, waiting for transfers between devices, per_device(): piece = lax.all_gather(corr, 'lag', axis=2, tiled=True)  74.5 us
    reduce_sum x1, other arithmetic, per_device(): jnp.sum(xn, axis=1)  32.5 us
    psum x3, blocking collectives, per_device(): coh = lax.psum(inner, 'lag') / lags  30.9 us
    psum x3, blocking collectives, per_device(): rbar = lax.psum(jnp.sum(res, axis=1), 'day') / days  30.2 us
    reduce_sum x3, other arithmetic, per_device(): jnp.sum(weight[:, :, None] * xn, axis=1)  27.9 us
    reshape x1, local copies, waits for them, and re-layouts, per_device(): piece.reshape(pairs * days_here, count)  23.7 us
  transfers between devices with their start and end apart: 5, of which 5 were waited for; matrix products, arithmetic and copies ran while one was open for 3% of the time, Pallas kernels for 0%

commit v1 on v0

v1 whole, which is shorter than its diff:
```python
import functools

import jax
import jax.numpy as jnp
from jax import lax
from jax.experimental import pallas as pl
from jax.experimental.pallas import tpu as pltpu
from jax.sharding import PartitionSpec as P

ITERS = 3
LANES = 128
epsilon = 1e-06


def kernel_rows(rows, lags):
    row = jnp.arange(rows, dtype=jnp.int32)
    col = jnp.arange(lags, dtype=jnp.int32)
    offset = (col[None, :] - row[:, None]) % lags
    odd = offset % 2 == 1
    angle = jnp.pi * offset.astype(jnp.float32) / lags
    value = jnp.where(odd, 2.0 / lags * jnp.cos(angle) / jnp.where(odd, jnp.sin(angle), 1.0), 0.0)
    return value.astype(jnp.bfloat16)


def stack_kernel(sizes, top_ref, *refs):
    n_src, lag_groups, days_here, group, lags = sizes
    ins = refs[:n_src]
    pws_ref, robust_ref, share_ref = refs[n_src:n_src + 3]
    matrix, rows32, data, data16, quad, normed, stack = refs[n_src + 3:]
    days = n_src // lag_groups * days_here
    width = lags // lag_groups
    tiles = width // LANES
    top_rows = top_ref.shape[0]
    pitch = tiles * days_here

    @pl.when(pl.program_id(0) == 0)
    def _():
        for a in range(lags // top_rows):
            cut = a * top_rows
            if cut:
                matrix[cut:cut + top_rows, :cut] = top_ref[:, lags - cut:]
            matrix[cut:cut + top_rows, cut:] = top_ref[:, :lags - cut]

    for s in range(n_src):
        block, part = divmod(s, lag_groups)
        rows32[...] = ins[s][...].astype(jnp.float32)
        for d in range(days_here):
            day = block * days_here + d
            for t in range(tiles):
                lane = part * width + t * LANES
                x = rows32[pl.ds(t * days_here + d, group, stride=pitch), :]
                data[day, :, lane:lane + LANES] = x
                data16[day * group:(day + 1) * group, lane:lane + LANES] = x.astype(jnp.bfloat16)

    quad[...] = jnp.dot(data16[...], matrix[...], preferred_element_type=jnp.float32)

    scale = []
    for day in range(days):
        x = data[day]
        norm2 = jnp.sum(x * x, axis=1, keepdims=True)
        scale.append(1.0 / jnp.sqrt(norm2 / lags + epsilon))

    chunk = min(512, lags)
    for c in range(0, lags, chunk):
        linear = csum = ssum = None
        for day in range(days):
            x = data[day, :, c:c + chunk]
            q = quad[day * group:(day + 1) * group, c:c + chunk]
            inv = jnp.minimum(lax.rsqrt(x * x + q * q), 10.0 * scale[day])
            xn = x * scale[day]
            data[day, :, c:c + chunk] = xn
            if day == 0:
                linear, csum, ssum = xn, x * inv, q * inv
            else:
                linear, csum, ssum = linear + xn, csum + x * inv, ssum + q * inv
        pws = linear / days * ((csum * csum + ssum * ssum) / (days * days))
        stack[:, c:c + chunk] = pws
    pws_ref[...] = stack[...]

    total = None
    weights = None
    for step in range(ITERS):
        s = stack[...]
        msq = jnp.sum(s * s, axis=1, keepdims=True) / lags
        normed[...] = s * (1.0 / jnp.sqrt(msq + epsilon))
        cohs, ress = [], []
        for day in range(days):
            coh = jnp.sum(data[day] * normed[...], axis=1, keepdims=True) / lags
            cohs.append(coh)
        for day in range(days):
            gap = data[day] - cohs[day] * normed[...]
            ress.append(jnp.sum(gap * gap, axis=1, keepdims=True) / lags)
        rbar = sum(ress[1:], ress[0]) / days
        weights = [(0.1 + jnp.abs(c)) / (r + rbar + epsilon) for c, r in zip(cohs, ress)]
        total = sum(weights[1:], weights[0])
        last = step == ITERS - 1
        if last:
            weights = [w / total for w in weights]
        for c in range(0, lags, chunk):
            acc = weights[0] * data[0, :, c:c + chunk]
            for day in range(1, days):
                acc = acc + weights[day] * data[day, :, c:c + chunk]
            if last:
                robust_ref[:, c:c + chunk] = acc
            else:
                stack[:, c:c + chunk] = acc
    share_ref[...] = jnp.concatenate(weights, axis=1)


def stack_pairs(pieces, top, lag_groups, days_here, pairs, group):
    n_src = len(pieces)
    lags = top.shape[1]
    days = n_src // lag_groups * days_here
    pitch = lags // lag_groups // LANES * days_here
    sizes = (n_src, lag_groups, days_here, group, lags)
    cost = pl.CostEstimate(
        flops=2 * pairs * days * lags * lags, bytes_accessed=pairs * days * lags * 2, transcendentals=pairs * days * lags
    )
    return pl.pallas_call(
        functools.partial(stack_kernel, sizes),
        grid=(pairs // group,),
        in_specs=[pl.BlockSpec(top.shape, lambda i: (0, 0))]
        + [pl.BlockSpec((group * pitch, LANES), lambda i: (i, 0))] * n_src,
        out_specs=[
            pl.BlockSpec((group, lags), lambda i: (i, 0)),
            pl.BlockSpec((group, lags), lambda i: (i, 0)),
            pl.BlockSpec((group, days), lambda i: (i, 0)),
        ],
        out_shape=[
            jax.ShapeDtypeStruct((pairs, lags), jnp.float32),
            jax.ShapeDtypeStruct((pairs, lags), jnp.float32),
            jax.ShapeDtypeStruct((pairs, days), jnp.float32),
        ],
        scratch_shapes=[
            pltpu.VMEM((lags, lags), jnp.bfloat16),
            pltpu.VMEM((group * pitch, LANES), jnp.float32),
            pltpu.VMEM((days, group, lags), jnp.float32),
            pltpu.VMEM((days * group, lags), jnp.bfloat16),
            pltpu.VMEM((days * group, lags), jnp.float32),
            pltpu.VMEM((group, lags), jnp.float32),
            pltpu.VMEM((group, lags), jnp.float32),
        ],
        cost_estimate=cost,
        name="stack_pairs",
    )(top, *pieces)


def per_device(corr):
    pairs, days_here, width = corr.shape
    lag_groups = lax.axis_size("lag")
    day_groups = lax.axis_size("day")
    n = lag_groups * day_groups
    lags = width * lag_groups
    mine = pairs // n
    tiles = width // LANES
    top = kernel_rows(min(256, lags), lags)
    moved = lax.all_to_all(corr, ("day", "lag"), 0, 0, tiled=True)
    moved = moved.reshape(n, mine, days_here, tiles, LANES).transpose(0, 1, 3, 2, 4)
    moved = moved.reshape(n, mine * tiles * days_here, LANES)
    pieces = [moved[s] for s in range(n)]
    pws, robust, shares = stack_pairs(pieces, top, lag_groups, days_here, mine, 16)
    both = jnp.stack([pws, robust])
    peak = jnp.maximum(jnp.max(jnp.abs(both), axis=2), 1e-30)
    both = (both * (1024.0 / peak)[:, :, None]).astype(jnp.float16)
    both = both.reshape(2, mine, lag_groups, width).transpose(2, 0, 1, 3)
    both = jnp.broadcast_to(both[None], (day_groups,) + both.shape).reshape((n,) + both.shape[1:])
    both = lax.all_to_all(both, ("day", "lag"), 0, 0, tiled=True)
    side = jnp.concatenate([shares, peak.T / 1024.0], axis=1)
    side = lax.all_gather(side, ("day", "lag"), axis=0, tiled=True)
    days = days_here * day_groups
    both = both.transpose(1, 0, 2, 3).reshape(2, pairs, width).astype(jnp.float32)
    first = lax.axis_index("day") * days_here
    return (
        both[0] * side[:, days:days + 1],
        both[1] * side[:, days + 1:],
        lax.dynamic_slice_in_dim(side, first, days_here, 1),
    )


def solution(mesh):
    return jax.shard_map(
        per_device,
        mesh=mesh,
        in_specs=(P("pair", "day", "lag"),),
        out_specs=(P("pair", "lag"), P("pair", "lag"), P("pair", "day")),
        check_vma=False,
    )
```

time: 835 us -> 206 us (0.25)
  waiting for transfers between devices: 539 us -> 67.4 us
  other arithmetic: 119 us -> 13.5 us
  blocking collectives: 102 us -> 54.7 us
  local copies, waits for them, and re-layouts: 44.3 us -> 10.5 us
  Pallas kernels: 0 us -> 29 us
  starting transfers between devices: 0.2 us -> 27.3 us
  matrix products: 15.1 us -> 0 us
  between operations: 13.9 us -> 0.75 us
    psum x4 -> x0, waiting for transfers between devices: 464 us -> none  [the longest x3 241 us: per_device(): lax.psum((jnp.sum(weight[:, :, None] * xn, axis=1), jnp.sum(weight, axis=...]
    psum x11 -> x0, blocking collectives: 102 us -> none  [the longest x3 30.9 us: per_device(): coh = lax.psum(inner, 'lag') / lags]
    reduce_sum x15 -> x0, other arithmetic: 89.6 us -> none  [the longest x1 32.5 us: per_device(): jnp.sum(xn, axis=1)]
    all_gather x1 -> x0, waiting for transfers between devices: 74.5 us -> none  [per_device(): piece = lax.all_gather(corr, 'lag', axis=2, tiled=True)]
    all_to_all x0 -> x2, waiting for transfers between devices: none -> 67.4 us  [the longest x1 67.4 us: per_device(): moved = lax.all_to_all(corr, ('day', 'lag'), 0, 0, tiled=True)]
    all_gather x0 -> x1, blocking collectives: none -> 54.7 us  [per_device(): side = lax.all_gather(side, ('day', 'lag'), axis=0, tiled=True)]
    reshape x2 -> x0, local copies, waits for them, and re-layouts: 33.5 us -> none  [the longest x1 23.7 us: per_device(): piece.reshape(pairs * days_here, count)]
    pallas_call x0 -> x1, Pallas kernels: none -> 29 us  [stack_pairs(): pl.pallas_call(functools.partial(stack_kernel, sizes), grid=(pairs // gro...]
  transfers between devices with their start and end apart: 5 -> 2, of which waited for: 5 -> 1; matrix products, arithmetic and copies ran while one was open for 3% -> 5% of each run, Pallas kernels for 0% -> 0%
where the time goes in v1:
time: 206 us; the launch traced here: 203 us
  waiting for transfers between devices  67.4 us (33%)
  blocking collectives  54.7 us (27%)
  Pallas kernels  29 us (14%)
  starting transfers between devices  27.3 us (13%)
  other arithmetic  13.5 us (7%)
  local copies, waits for them, and re-layouts  10.5 us (5%)
    all_to_all x1, waiting for transfers between devices, per_device(): moved = lax.all_to_all(corr, ('day', 'lag'), 0, 0, tiled=True)  67.4 us
    all_gather x1, blocking collectives, per_device(): side = lax.all_gather(side, ('day', 'lag'), axis=0, tiled=True)  54.7 us
    pallas_call x1, Pallas kernels, stack_pairs(): pl.pallas_call(functools.partial(stack_kernel, sizes), grid=(pairs // gro...  29 us
    all_to_all x1, starting transfers between devices, per_device(): both = lax.all_to_all(both, ('day', 'lag'), 0, 0, tiled=True)  19.8 us
    convert_element_type x1, other arithmetic, kernel_rows(): return value.astype(jnp.bfloat16)  10.2 us
    all_to_all x1, starting transfers between devices, per_device(): moved = lax.all_to_all(corr, ('day', 'lag'), 0, 0, tiled=True)  7.48 us
    slice x1, local copies, waits for them, and re-layouts, per_device(): pieces = [moved[s] for s in range(n)]  4.37 us
  transfers between devices with their start and end apart: 2, of which 1 were waited for; matrix products, arithmetic and copies ran while one was open for 5% of the time, Pallas kernels for 0%

profile of v1, /device:TPU:0, one launch (start us, length us, event | category | flops | bytes accessed | tf_op | source)
XLA Modules:
  0.0 203.2 jit_solution(17962133787345445500)
XLA Ops:
  0.6 7.5 %all-to-all-start = ((bf16[1024,4,512]{2,1,0:T(4,128)(2,1)}), bf16[1024,4,512]{2,1,0:T(4,128)(2,1)}, u32[]{:S(2)}, u32[]{:S(2)}) async-start(bf16[1024,4,512]{2,1,0:T(4,128)(2,1)} %param.1), calls=%async_computation | async-start | bytes 8388608 | tf_op jit(solution)/shard_map/all_to_all | solution.py:157
  8.1 10.2 %select_convert_fusion.top_ref = bf16[256,2048]{1,0:T(8,128)(2,1)} fusion(), kind=kLoop, calls=%fused_computation.12 | loop fusion | flops 16252928 | bytes 1048576 | tf_op jit(solution)/shard_map/convert_element_type | solution.py:22
  18.3 67.4 %all-to-all-done = bf16[1024,4,512]{2,1,0:T(4,128)(2,1)} async-done(((bf16[1024,4,512]{2,1,0:T(4,128)(2,1)}), bf16[1024,4,512]{2,1,0:T(4,128)(2,1)}, u32[]{:S(2)}, u32[]{:S(2)}) %all-to-all-start) | async-done | bytes 4194336 | tf_op jit(solution)/shard_map/all_to_all | solution.py:157
  85.7 4.4 %fusion.11 = (bf16[1,64,4,4,128]{4,3,2,1,0:T(4,128)(2,1)}, bf16[1,64,4,4,128]{4,3,2,1,0:T(4,128)(2,1)}, bf16[1,64,4,4,128]{4,3,2,1,0:T(4,128)(2,1)}, bf16[1,64,4...) fusion(bf16[16,64,4,4,128]{4,3,2,1,0:T(4,128)(2,1)} %bitcast.1), kind=kLoop, calls=%fused_computation.27 | loop fusion | bytes 8388608 | tf_op jit(solution)/shard_map/slice | solution.py:160
  90.0 29.0 %stack_pairs.1 = (f32[64,2048]{1,0:T(8,128)}, f32[64,2048]{1,0:T(8,128)}, f32[64,16]{1,0:T(8,128)}) custom-call(bf16[256,2048]{1,0:T(8,128)(2,1)} %select_convert_fusion.top_ref, bf16[1024,128]{1,0:T(8,128)(2,1)} %bitcast.56, bf16[1024,128]{1,0:T(8,128)(2,1)} %bitcast.55, bf16[1024,128]{1,0:T(8,128)(2,1)} %bitcast.54, bf16[1024,128]{1,0:T(8,128)(2,1)} %bitcast.53, ...), custom_call_target="tpu_custom_call" | custom-call | flops 8589934592 | bytes 4194304 | tf_op jit(solution)/shard_map/stack_pairs/pallas_call | solution.py:119
  119.1 0.0 copy-start
  119.1 0.0 copy-start.1
  119.1 1.5 stack.15
  120.6 1.4 stack.16
  121.9 0.0 copy-done
  122.0 0.0 copy-done.1
  122.0 0.1 fusion.8
  122.1 0.3 fusion.9
  122.5 0.2 copy.18
  122.6 1.6 broadcast_in_dim.18
  124.2 19.8 %all-to-all-start.1 = ((f16[16,2,64,512]{3,2,1,0:T(8,128)(2,1)}), f16[16,2,64,512]{3,2,1,0:T(8,128)(2,1)S(1)}, u32[]{:S(2)}, u32[]{:S(2)}) async-start(f16[16,2,64,512]{3,2,1,0:T(8,128)(2,1)} %bitcast.38), calls=%async_computation.1 | async-start | bytes 4194304 | tf_op jit(solution)/shard_map/all_to_all | solution.py:167
  144.0 0.1 copy.19
  144.1 54.7 %all-gather = f32[16,64,18]{1,2,0:T(8,128)S(1)} all-gather(f32[1,64,18]{1,2,0:T(8,128)S(1)} %maximum_bitcast_fusion), channel_id=1, replica_groups=mesh['pair'=2,'day'=4,'lag'=4] {'day','lag'}, dimensions={0}, use_global_device_ids=true | all-gather | bytes 78336 | tf_op jit(solution)/shard_map/all_gather | solution.py:169
  198.9 0.1 reshape.64
  199.0 0.6 constant_dynamic-slice_fusion
  199.6 0.0 all-to-all-done.1
  199.6 0.5 convert_bitcast_fusion
  200.1 0.7 fusion.10
  200.9 2.4 %bitcast_multiply_fusion = (f32[1024,512]{1,0:T(8,128)}, f32[1024,512]{1,0:T(8,128)}) fusion(f32[1,16,64,512]{3,2,0,1:T(8,128)S(1)} %get-tuple-element.9, f32[1024]{0:T(1024)S(1)} %bitcast.57, f32[1024]{0:T(1024)S(1)} %bitcast.58, f32[1,16,64,512]{3,2,0,1:T(8,128)S(1)} %get-tuple-element.10), kind=kLoop, calls=%fused_computation.10 | loop fusion | flops 1048576 | bytes 8396800 | tf_op jit(solution)/shard_map/mul | solution.py:175
  (6 shorter events, 0.1 us)
Async XLA Ops:
  0.6 85.0 %all-to-all-start = ((bf16[1024,4,512]{2,1,0:T(4,128)(2,1)}), bf16[1024,4,512]{2,1,0:T(4,128)(2,1)}, u32[]{:S(2)}, u32[]{:S(2)}) async-start(bf16[1024,4,512]{2,1,0:T(4,128)(2,1)} %param.1), calls=%async_computation | async-start | bytes 8388608 | tf_op jit(solution)/shard_map/all_to_all | solution.py:157
  119.1 2.9 %copy-start = (f32[64,2048]{1,0:T(8,128)S(1)}, f32[64,2048]{1,0:T(8,128)}, u32[]{:S(2)}) copy-start(f32[64,2048]{1,0:T(8,128)} %get-tuple-element.6) | copy-start | bytes 1572868
  119.1 2.9 %copy-start.1 = (f32[64,2048]{1,0:T(8,128)S(1)}, f32[64,2048]{1,0:T(8,128)}, u32[]{:S(2)}) copy-start(f32[64,2048]{1,0:T(8,128)} %get-tuple-element.7) | copy-start | bytes 1572868
  124.2 19.8 %copy-start.2 = (f32[64,16]{1,0:T(8,128)S(1)}, f32[64,16]{1,0:T(8,128)}, u32[]{:S(2)}) copy-start(f32[64,16]{1,0:T(8,128)} %get-tuple-element.8) | copy-start | bytes 12292
  124.2 75.4 %all-to-all-start.1 = ((f16[16,2,64,512]{3,2,1,0:T(8,128)(2,1)}), f16[16,2,64,512]{3,2,1,0:T(8,128)(2,1)S(1)}, u32[]{:S(2)}, u32[]{:S(2)}) async-start(f16[16,2,64,512]{3,2,1,0:T(8,128)(2,1)} %bitcast.38), calls=%async_computation.1 | async-start | bytes 4194304 | tf_op jit(solution)/shard_map/all_to_all | solution.py:167

commit v2 on v1

v2 whole, which is shorter than its diff:
```python
import functools

import jax
import jax.numpy as jnp
from jax import lax
from jax.experimental import pallas as pl
from jax.experimental.pallas import tpu as pltpu
from jax.sharding import PartitionSpec as P


ITERS = 3
LANES = 128
SUBLANES = 8
PLAN = ((32, "all", "staged"), (16, "all", "staged"), (16, "all", "all"),)
epsilon = 1e-06


def kernel_rows(rows, lags):
    row = jnp.arange(rows, dtype=jnp.int32)
    col = jnp.arange(lags, dtype=jnp.int32)
    offset = (col[None, :] - row[:, None]) % lags
    odd = offset % 2 == 1
    angle = jnp.pi * offset.astype(jnp.float32) / lags
    value = jnp.where(odd, 2.0 / lags * jnp.cos(angle) / jnp.where(odd, jnp.sin(angle), 1.0), 0.0)
    return value.astype(jnp.bfloat16)


def stack_kernel(sizes, me_ref, top_ref, *refs):
    lag_groups, days_here, group, lags, n_src = sizes
    ins = refs[:-8]
    message_ref, matrix, rows32, data, data16, quad, normed, stack = refs[-8:]
    days = n_src // lag_groups * days_here
    width = lags // lag_groups
    tiles = width // LANES
    top_rows = top_ref.shape[0]
    pitch = tiles * days_here
    chunk = min(512, width)

    @pl.when(pl.program_id(0) == 0)
    def _():
        for a in range(lags // top_rows):
            cut = a * top_rows
            if cut:
                matrix[cut:cut + top_rows, :cut] = top_ref[:, lags - cut:]
            matrix[cut:cut + top_rows, cut:] = top_ref[:, :lags - cut]

    for s in range(n_src):
        if len(ins) == 1:
            here = pl.multiple_of(pl.program_id(0) * group * pitch, group * pitch)
            rows32[...] = ins[0][s, pl.ds(here, group * pitch), :].astype(jnp.float32)
            block, part = divmod(s, lag_groups)
        else:
            rows32[...] = ins[s][...].astype(jnp.float32)
            source = me_ref[0] ^ s
            block, part = source // lag_groups, source % lag_groups
        for d in range(days_here):
            day = block * days_here + d
            row = pl.multiple_of(day * group, group)
            for t in range(tiles):
                lane = pl.ds(pl.multiple_of(part * width + t * LANES, LANES), LANES)
                x = rows32[pl.ds(t * days_here + d, group, stride=pitch), :]
                data[day, :, lane] = x
                data16[pl.ds(row, group), lane] = x.astype(jnp.bfloat16)

    quad[...] = jnp.dot(data16[...], matrix[...], preferred_element_type=jnp.float32)

    scale = []
    for day in range(days):
        x = data[day]
        norm2 = jnp.sum(x * x, axis=1, keepdims=True)
        scale.append(1.0 / jnp.sqrt(norm2 / lags + epsilon))

    for c in range(0, lags, chunk):
        linear = csum = ssum = None
        for day in range(days):
            x = data[day, :, c:c + chunk]
            q = quad[day * group:(day + 1) * group, c:c + chunk]
            inv = jnp.minimum(lax.rsqrt(x * x + q * q), 10.0 * scale[day])
            xn = x * scale[day]
            data[day, :, c:c + chunk] = xn
            if day == 0:
                linear, csum, ssum = xn, x * inv, q * inv
            else:
                linear, csum, ssum = linear + xn, csum + x * inv, ssum + q * inv
        stack[:, c:c + chunk] = linear / days * ((csum * csum + ssum * ssum) / (days * days))

    bands = group // SUBLANES
    all_bands = bands * pl.num_programs(0)

    def emit(kind, value):
        peak = jnp.maximum(jnp.max(jnp.abs(value), axis=1, keepdims=True), 1e-30)
        power = jnp.floor(jnp.log2(peak))
        value = value * jnp.exp2(9.0 - power)
        for part in range(lag_groups):
            for r in range(bands):
                for t in range(tiles):
                    place = (kind * all_bands + pl.program_id(0) * bands + r) * tiles + t
                    lane = part * width + t * LANES
                    message_ref[part, place] = value[r * SUBLANES:(r + 1) * SUBLANES, lane:lane + LANES]
        return power

    powers = [emit(0, stack[...])]
    for step in range(ITERS):
        s = stack[...]
        msq = jnp.sum(s * s, axis=1, keepdims=True) / lags
        normed[...] = s * (1.0 / jnp.sqrt(msq + epsilon))
        cohs, ress = [], []
        for day in range(days):
            cohs.append(jnp.sum(data[day] * normed[...], axis=1, keepdims=True) / lags)
        for day in range(days):
            gap = data[day] - cohs[day] * normed[...]
            ress.append(jnp.sum(gap * gap, axis=1, keepdims=True) / lags)
        rbar = sum(ress[1:], ress[0]) / days
        weights = [(0.1 + jnp.abs(c)) / (r + rbar + epsilon) for c, r in zip(cohs, ress)]
        if step == ITERS - 1:
            total = sum(weights[1:], weights[0])
            weights = [w / total for w in weights]
        for c in range(0, lags, chunk):
            acc = weights[0] * data[0, :, c:c + chunk]
            for day in range(1, days):
                acc = acc + weights[day] * data[day, :, c:c + chunk]
            stack[:, c:c + chunk] = acc
    powers.append(emit(1, stack[...]))
    side = jnp.concatenate([w * 1024.0 for w in weights] + powers, axis=1)
    per = LANES // (days + 2)
    for r in range(bands):
        band = pl.program_id(0) * bands + r
        for k in range(per):
            @pl.when(band % per == k)
            def _():
                for part in range(lag_groups):
                    message_ref[part, 2 * tiles * all_bands + band // per, :, k * (days + 2):(k + 1) * (days + 2)] = (
                        side[r * SUBLANES:(r + 1) * SUBLANES])


def stack_pairs(me, pieces, top, lag_groups, days_here, pairs, group, n_src):
    lags = top.shape[1]
    days = n_src // lag_groups * days_here
    width = lags // lag_groups
    pitch = width // LANES * days_here
    bands = pairs // SUBLANES
    tiles = 2 * bands * (width // LANES) + pl.cdiv(bands, LANES // (days + 2))
    cost = pl.CostEstimate(
        flops=2 * pairs * days * lags * lags, bytes_accessed=pairs * days * lags * 2, transcendentals=pairs * days * lags
    )
    if len(pieces) == 1:
        piece_specs = [pl.BlockSpec(memory_space=pltpu.VMEM)]
    else:
        piece_specs = [pl.BlockSpec((group * pitch, LANES), lambda i: (i, 0))] * n_src
    return pl.pallas_call(
        functools.partial(stack_kernel, (lag_groups, days_here, group, lags, n_src)),
        grid=(pairs // group,),
        in_specs=[pl.BlockSpec(memory_space=pltpu.SMEM), pl.BlockSpec(top.shape, lambda i: (0, 0))] + piece_specs,
        out_specs=pl.BlockSpec(memory_space=pltpu.VMEM),
        out_shape=jax.ShapeDtypeStruct((lag_groups, tiles, SUBLANES, LANES), jnp.float32),
        scratch_shapes=[
            pltpu.VMEM((lags, lags), jnp.bfloat16),
            pltpu.VMEM((group * pitch, LANES), jnp.float32),
            pltpu.VMEM((days, group, lags), jnp.float32),
            pltpu.VMEM((days * group, lags), jnp.bfloat16),
            pltpu.VMEM((days * group, lags), jnp.float32),
            pltpu.VMEM((group, lags), jnp.float32),
            pltpu.VMEM((group, lags), jnp.float32),
        ],
        cost_estimate=cost,
        name="stack_pairs",
    )(me, top, *pieces)


def unpack(message, pairs, width, days, days_here):
    n = message.shape[0]
    bands, tiles, per = pairs // SUBLANES, width // LANES, LANES // (days + 2)
    side = message[:, 2 * bands * tiles:].astype(jnp.float32)
    blocks = [side[:, r // per, :, r % per * (days + 2):(r % per + 1) * (days + 2)] for r in range(bands)]
    blocks = jnp.stack(blocks, axis=1)
    shares = lax.dynamic_slice_in_dim(blocks, lax.axis_index("day") * days_here, days_here, 3) / 1024.0
    outs = []
    for kind in range(2):
        scale = jnp.exp2(blocks[:, :, :, days + kind] - 9.0)
        scale = jnp.broadcast_to(scale[:, :, None, :, None], (n, bands, 1, SUBLANES, LANES))
        scale = lax.optimization_barrier(scale)
        value = message[:, kind * bands * tiles:(kind + 1) * bands * tiles].astype(jnp.float32)
        value = value.reshape(n, bands, tiles, SUBLANES, LANES) * scale
        outs.append(jnp.swapaxes(value, 2, 3).reshape(n * pairs, width))
    return outs[0], outs[1], shares.reshape(n * pairs, days_here)


AXES = ("day", "lag")


def swap(x, n, by):
    return lax.ppermute(x, AXES, [(i, i ^ by) for i in range(n)])


def spread_direct(message, day_groups, n):
    message = jnp.broadcast_to(message[None], (day_groups,) + message.shape).reshape((n,) + message.shape[1:])
    return lax.all_to_all(message, AXES, 0, 0, tiled=True)


def unswap(pieces, index):
    step = 1
    while step < len(pieces):
        odd = (index // step) % 2 == 1
        pieces = [jnp.where(odd, pieces[k ^ step], pieces[k]) for k in range(len(pieces))]
        step *= 2
    return pieces


def spread_lags(message, me, lag_groups, n):
    lag = me % lag_groups
    pieces = unswap([message[m] for m in range(lag_groups)], lag)
    got = [pieces[0]] + [swap(pieces[m], n, m) for m in range(1, lag_groups)]
    return jnp.stack(unswap(got, lag))


def spread_days(got, me, lag_groups, n):
    near, far = me // lag_groups % 2, me // (2 * lag_groups)
    got = jnp.stack(unswap([got, swap(got, n, 2 * lag_groups)], far))
    got = jnp.stack(unswap([got, swap(got, n, lag_groups)], near), axis=1)
    return got.reshape((n,) + got.shape[3:])


def per_device(corr):
    pairs, days_here, width = corr.shape
    lag_groups = lax.axis_size("lag")
    day_groups = lax.axis_size("day")
    n = lag_groups * day_groups
    me = lax.axis_index(AXES)
    lags = width * lag_groups
    days = days_here * day_groups
    tiles = width // LANES
    top = kernel_rows(min(256, lags), lags)
    mine = pairs // n
    staged = day_groups == 4 and lag_groups == 4 and mine == sum(p for p, _, _ in PLAN)
    plan = PLAN if staged else ((mine, "all", "all"),)

    def flat(piece, lead):
        piece = piece.reshape(lead + (piece.shape[-3], days_here, tiles, LANES))
        piece = jnp.swapaxes(piece, -2, -3)
        return piece.reshape(lead + (-1, LANES))

    outs = [jnp.zeros((pairs, width), jnp.float32), jnp.zeros((pairs, width), jnp.float32)]
    starts = [sum(p for p, _, _ in plan[:k]) for k in range(len(plan))]
    moved, sent = [], []

    def work(k):
        message = stack_pairs(me.reshape(1), moved[k], top, lag_groups, days_here, plan[k][0], 16 if plan[k][0] % 16 == 0 else 8, n)
        message = message.astype(jnp.float16)
        if plan[k][2] == "staged":
            message = spread_lags(message, me, lag_groups, n)
        sent.append(message)

    for k, (p, _, _) in enumerate(plan):
        if k >= 2:
            work(k - 2)
        if k == 1:
            corr, top, *outs = lax.optimization_barrier((corr, top, *outs))
        rows = corr[starts[k] * n:(starts[k] + p) * n]
        if k >= 1:
            rows, moved[k - 1] = lax.optimization_barrier((rows, moved[k - 1]))
        if k >= 2:
            rows, sent[k - 2] = lax.optimization_barrier((rows, sent[k - 2]))
        got = lax.all_to_all(rows, AXES, 0, 0, tiled=True)
        moved.append([flat(got.reshape(n, p, days_here, width), (n,))])
    for k in range(len(sent), len(plan)):
        work(k)
    outs = list(outs) + [jnp.zeros((pairs, days_here), jnp.float32)]
    for k, (p, _, how) in enumerate(plan):
        spread = spread_direct(sent[k], day_groups, n) if how == "all" else spread_days(sent[k], me, lag_groups, n)
        parts = unpack(spread, p, width, days, days_here)
        outs = [lax.dynamic_update_slice(o, v, (starts[k] * n, 0)) for o, v in zip(outs, parts)]
    return tuple(outs)


def solution(mesh):
    return jax.shard_map(
        per_device,
        mesh=mesh,
        in_specs=(P("pair", "day", "lag"),),
        out_specs=(P("pair", "lag"), P("pair", "lag"), P("pair", "day")),
        check_vma=False,
    )
```

time: 206 us -> 206 us (level)
  blocking collectives: 54.7 us -> 0 us
  waiting for transfers between devices: 67.4 us -> 85.2 us
  starting transfers between devices: 27.3 us -> 39.9 us
  local copies, waits for them, and re-layouts: 10.5 us -> 21.5 us
  other arithmetic: 13.5 us -> 23.2 us
  Pallas kernels: 29 us -> 33.7 us
    all_gather x1 -> x0, blocking collectives: 54.7 us -> none  [per_device(): side = lax.all_gather(side, ('day', 'lag'), axis=0, tiled=True)]
    ppermute x0 -> x10, waiting for transfers between devices: none -> 46.2 us  [swap(): return lax.ppermute(x, AXES, [(i, i ^ by) for i in range(n)])]
    all_to_all x2 -> x4, waiting for transfers between devices: 67.4 us -> 39 us  [the longest x3 30.8 us: per_device(): got = lax.all_to_all(rows, AXES, 0, 0, tiled=True)]
    ppermute x0 -> x10, starting transfers between devices: none -> 11.9 us  [swap(): return lax.ppermute(x, AXES, [(i, i ^ by) for i in range(n)])]
    dynamic_update_slice x0 -> x8, local copies, waits for them, and re-layouts: none -> 4.82 us  [per_device(): lax.dynamic_update_slice(o, v, (starts[k] * n, 0))]
    pallas_call x1 -> x3, Pallas kernels: 29 us -> 33.7 us  [stack_pairs(): pl.pallas_call(functools.partial(stack_kernel, (lag_groups, days_here, gr...]
    another operation x0 -> x13, other arithmetic: none -> 4.29 us  [the longest x4 1.96 us: spread_days(): got = jnp.stack(unswap([got, swap(got, n, lag_groups)], near), axis=1)]
    slice x3 -> x12, local copies, waits for them, and re-layouts: 5.08 us -> 9.09 us  [the longest x2 7.19 us: per_device(): rows = corr[starts[k] * n:(starts[k] + p) * n]]
  transfers between devices with their start and end apart: 2 -> 14, of which waited for: 1 -> 6; matrix products, arithmetic and copies ran while one was open for 5% -> 16% of each run, Pallas kernels for 0% -> 8%
where the time goes in v2:
time: 206 us; the launch traced here: 205 us
  waiting for transfers between devices  85.2 us (41%)
  starting transfers between devices  39.9 us (19%)
  Pallas kernels  33.7 us (16%)
  other arithmetic  23.2 us (11%)
  local copies, waits for them, and re-layouts  21.5 us (10%)
    ppermute x10, waiting for transfers between devices, swap(): return lax.ppermute(x, AXES, [(i, i ^ by) for i in range(n)])  46.2 us
    pallas_call x3, Pallas kernels, stack_pairs(): pl.pallas_call(functools.partial(stack_kernel, (lag_groups, days_here, gr...  33.7 us
    all_to_all x3, waiting for transfers between devices, per_device(): got = lax.all_to_all(rows, AXES, 0, 0, tiled=True)  30.8 us
    all_to_all x3, starting transfers between devices, per_device(): got = lax.all_to_all(rows, AXES, 0, 0, tiled=True)  24.1 us
    ppermute x10, starting transfers between devices, swap(): return lax.ppermute(x, AXES, [(i, i ^ by) for i in range(n)])  11.9 us
    convert_element_type x1, other arithmetic, kernel_rows(): return value.astype(jnp.bfloat16)  10.1 us
    all_to_all x1, waiting for transfers between devices, spread_direct(): return lax.all_to_all(message, AXES, 0, 0, tiled=True)  8.23 us
    slice x2, local copies, waits for them, and re-layouts, per_device(): rows = corr[starts[k] * n:(starts[k] + p) * n]  7.19 us
  transfers between devices with their start and end apart: 14, of which 6 were waited for; matrix products, arithmetic and copies ran while one was open for 16% of the time, Pallas kernels for 8%

profile of v2, /device:TPU:0, one launch (start us, length us, event | category | flops | bytes accessed | tf_op | source)
XLA Modules:
  0.0 204.7 jit_solution(13368452140104634969)
XLA Ops:
  0.6 3.6 %slice.104 = bf16[512,4,512]{2,1,0:T(4,128)(2,1)} slice(bf16[1024,4,512]{2,1,0:T(4,128)(2,1)} %param.1), slice={[0:512], [0:4], [0:512]} | slice | bytes 4194304 | tf_op jit(solution)/shard_map/slice | solution.py:258
  4.3 7.4 %all-to-all-start = ((bf16[512,4,512]{2,1,0:T(4,128)(2,1)}), bf16[512,4,512]{2,1,0:T(4,128)(2,1)S(1)}, u32[]{:S(2)}, u32[]{:S(2)}) async-start(bf16[512,4,512]{2,1,0:T(4,128)(2,1)} %slice.104), calls=%async_computation | async-start | bytes 4194304 | tf_op jit(solution)/shard_map/all_to_all | solution.py:263
  11.7 10.1 %select_convert_fusion.top_ref = bf16[256,2048]{1,0:T(8,128)(2,1)} fusion(), kind=kLoop, calls=%fused_computation.9 | loop fusion | flops 16252928 | bytes 1048576 | tf_op jit(solution)/shard_map/convert_element_type | solution.py:25
  21.8 3.6 %fusion.21 = (bf16[256,4,512]{2,1,0:T(4,128)(2,1)}, bf16[256,4,512]{2,1,0:T(4,128)(2,1)}) fusion(bf16[1024,4,512]{2,1,0:T(4,128)(2,1)} %param.1), kind=kLoop, calls=%fused_computation.108 | loop fusion | bytes 4194304 | tf_op jit(solution)/shard_map/slice | solution.py:258
  25.4 27.3 %all-to-all-done = bf16[512,4,512]{2,1,0:T(4,128)(2,1)S(1)} async-done(((bf16[512,4,512]{2,1,0:T(4,128)(2,1)}), bf16[512,4,512]{2,1,0:T(4,128)(2,1)S(1)}, u32[]{:S(2)}, u32[]{:S(2)}) %all-to-all-start) | async-done | bytes 2097184 | tf_op jit(solution)/shard_map/all_to_all | solution.py:263
  52.7 11.2 %all-to-all-start.1 = ((bf16[256,4,512]{2,1,0:T(4,128)(2,1)}), bf16[256,4,512]{2,1,0:T(4,128)(2,1)S(1)}, u32[]{:S(2)}, u32[]{:S(2)}) async-start(bf16[256,4,512]{2,1,0:T(4,128)(2,1)} %get-tuple-element.15), calls=%async_computation.1 | async-start | bytes 2097152 | tf_op jit(solution)/shard_map/all_to_all | solution.py:263
  64.3 1.3 copy.96
  65.6 16.6 %stack_pairs.3 = f32[4,33,8,128]{3,2,1,0:T(8,128)} custom-call(s32[1]{0:T(128)} %bitcast.6.me_ref, bf16[256,2048]{1,0:T(8,128)(2,1)} %select_convert_fusion.top_ref, bf16[16,512,128]{2,1,0:T(8,128)(2,1)} %bitcast.149), custom_call_target="tpu_custom_call" | custom-call | flops 4294967296 | bytes 2097152 | tf_op jit(solution)/shard_map/stack_pairs/pallas_call | solution.py:150
  83.3 3.5 %all-to-all-done.1 = bf16[256,4,512]{2,1,0:T(4,128)(2,1)S(1)} async-done(((bf16[256,4,512]{2,1,0:T(4,128)(2,1)}), bf16[256,4,512]{2,1,0:T(4,128)(2,1)S(1)}, u32[]{:S(2)}, u32[]{:S(2)}) %all-to-all-start.1) | async-done | bytes 1048608 | tf_op jit(solution)/shard_map/all_to_all | solution.py:263
  87.7 8.6 %stack_pairs.4 = f32[4,17,8,128]{3,2,1,0:T(8,128)} custom-call(s32[1]{0:T(128)} %bitcast.6.me_ref, bf16[256,2048]{1,0:T(8,128)(2,1)} %select_convert_fusion.top_ref, bf16[16,256,128]{2,1,0:T(8,128)(2,1)} %bitcast.154), custom_call_target="tpu_custom_call" | custom-call | flops 2147483648 | bytes 1048576 | tf_op jit(solution)/shard_map/stack_pairs/pallas_call | solution.py:150
  97.3 2.3 %collective-permute-start.5 = (f16[17,8,128]{2,1,0:T(8,128)(2,1)S(1)}, f16[17,8,128]{2,1,0:T(8,128)(2,1)S(1)}, u32[]{:S(2)}, u32[]{:S(2)}) collective-permute-start(f16[17,8,128]{2,1,0:T(8,128)(2,1)S(1)} %get-tuple-element.70), channel_id=1, source_target_pairs={{0,3},{1,2},{2,1},{3,0},{4,7},{5,6},{6,5},{7,4},{8,11},{9,10},{10,... | collective-permute-start | bytes 104456 | tf_op jit(solution)/shard_map/ppermute | solution.py:192
  100.0 2.0 collective-permute-start
  102.2 1.8 collective-permute-done.6
  104.1 2.8 %collective-permute-start.8 = (f16[4,17,8,128]{3,2,1,0:T(8,128)(2,1)S(1)}, f16[4,17,8,128]{3,2,1,0:T(8,128)(2,1)S(1)}, u32[]{:S(2)}, u32[]{:S(2)}) collective-permute-start(f16[4,17,8,128]{3,2,1,0:T(8,128)(2,1)S(1)} %pad_maximum_fusion.6), channel_id=1, source_target_pairs={{0,8},{1,9},{2,10},{3,11},{4,12},{5,13},{6,14},{7,15},{8,0},{9,1},... | collective-permute-start | bytes 417800 | tf_op jit(solution)/shard_map/ppermute | solution.py:192
  107.1 5.5 %all-to-all-start.2 = ((bf16[256,4,512]{2,1,0:T(4,128)(2,1)}), bf16[256,4,512]{2,1,0:T(4,128)(2,1)}, u32[]{:S(2)}, u32[]{:S(2)}) async-start(bf16[256,4,512]{2,1,0:T(4,128)(2,1)} %get-tuple-element.21), calls=%async_computation.2 | async-start | bytes 2097152 | tf_op jit(solution)/shard_map/all_to_all | solution.py:263
  112.6 2.8 %collective-permute-start.3 = (f16[4,33,8,128]{3,2,1,0:T(8,128)(2,1)S(1)}, f16[4,33,8,128]{3,2,1,0:T(8,128)(2,1)S(1)}, u32[]{:S(2)}, u32[]{:S(2)}) collective-permute-start(f16[4,33,8,128]{3,2,1,0:T(8,128)(2,1)S(1)} %pad_maximum_fusion.5), channel_id=1, source_target_pairs={{0,8},{1,9},{2,10},{3,11},{4,12},{5,13},{6,14},{7,15},{8,0},{9,1},... | collective-permute-start | bytes 811016 | tf_op jit(solution)/shard_map/ppermute | solution.py:192
  115.6 1.5 collective-permute-start.9
  117.1 33.5 %collective-permute-done.3 = f16[4,33,8,128]{3,2,1,0:T(8,128)(2,1)S(1)} collective-permute-done((f16[4,33,8,128]{3,2,1,0:T(8,128)(2,1)S(1)}, f16[4,33,8,128]{3,2,1,0:T(8,128)(2,1)S(1)}, u32[]{:S(2)}, u32[]{:S(2)}) %collective-permute-start.3) | collective-permute-done | bytes 270368 | tf_op jit(solution)/shard_map/ppermute | solution.py:192
  154.8 10.9 %collective-permute-done.4 = f16[2,4,33,8,128]{4,3,2,1,0:T(8,128)(2,1)} collective-permute-done((f16[2,4,33,8,128]{4,3,2,1,0:T(8,128)(2,1)}, f16[2,4,33,8,128]{4,3,2,1,0:T(8,128)(2,1)}, u32[]{:S(2)}, u32[]{:S(2)}) %collective-permute-start.4) | collective-permute-done | bytes 540704 | tf_op jit(solution)/shard_map/ppermute | solution.py:192
  165.7 1.4 select_bitcast_fusion.1
  168.8 1.3 fusion.13
  171.4 8.6 %stack_pairs.5 = f32[4,17,8,128]{3,2,1,0:T(8,128)} custom-call(s32[1]{0:T(128)} %bitcast.6.me_ref, bf16[256,2048]{1,0:T(8,128)(2,1)} %select_convert_fusion.top_ref, bf16[16,256,128]{2,1,0:T(8,128)(2,1)} %bitcast.45.refs_0_), custom_call_target="tpu_custom_call" | custom-call | flops 2147483648 | bytes 1048576 | tf_op jit(solution)/shard_map/stack_pairs/pallas_call | solution.py:150
  181.8 3.9 %all-to-all-start.3 = ((f16[16,17,8,128]{3,2,1,0:T(8,128)(2,1)}), f16[16,17,8,128]{3,2,1,0:T(8,128)(2,1)S(1)}, u32[]{:S(2)}, u32[]{:S(2)}) async-start(f16[16,17,8,128]{3,2,1,0:T(8,128)(2,1)} %bitcast.46), calls=%async_computation.3 | async-start | bytes 1114112 | tf_op jit(solution)/shard_map/all_to_all | solution.py:197
  192.3 8.2 %all-to-all-done.3 = f16[16,17,8,128]{3,2,1,0:T(8,128)(2,1)S(1)} async-done(((f16[16,17,8,128]{3,2,1,0:T(8,128)(2,1)}), f16[16,17,8,128]{3,2,1,0:T(8,128)(2,1)S(1)}, u32[]{:S(2)}, u32[]{:S(2)}) %all-to-all-start.3) | async-done | bytes 557088 | tf_op jit(solution)/shard_map/all_to_all | solution.py:197
  (101 shorter events, 23.8 us)
Async XLA Ops:
  4.3 48.4 %all-to-all-start = ((bf16[512,4,512]{2,1,0:T(4,128)(2,1)}), bf16[512,4,512]{2,1,0:T(4,128)(2,1)S(1)}, u32[]{:S(2)}, u32[]{:S(2)}) async-start(bf16[512,4,512]{2,1,0:T(4,128)(2,1)} %slice.104), calls=%async_computation | async-start | bytes 4194304 | tf_op jit(solution)/shard_map/all_to_all | solution.py:263
  52.7 11.4 %copy-start.3 = (bf16[512,4,512]{2,1,0:T(4,128)(2,1)}, bf16[512,4,512]{2,1,0:T(4,128)(2,1)S(1)}, u32[]{:S(2)}) copy-start(bf16[512,4,512]{2,1,0:T(4,128)(2,1)S(1)} %all-to-all-done) | copy-start | bytes 6291460
  52.7 34.1 %all-to-all-start.1 = ((bf16[256,4,512]{2,1,0:T(4,128)(2,1)}), bf16[256,4,512]{2,1,0:T(4,128)(2,1)S(1)}, u32[]{:S(2)}, u32[]{:S(2)}) async-start(bf16[256,4,512]{2,1,0:T(4,128)(2,1)} %get-tuple-element.15), calls=%async_computation.1 | async-start | bytes 2097152 | tf_op jit(solution)/shard_map/all_to_all | solution.py:263
  86.8 1.0 copy-start.5
  97.3 4.7 %collective-permute-start.5 = (f16[17,8,128]{2,1,0:T(8,128)(2,1)S(1)}, f16[17,8,128]{2,1,0:T(8,128)(2,1)S(1)}, u32[]{:S(2)}, u32[]{:S(2)}) collective-permute-start(f16[17,8,128]{2,1,0:T(8,128)(2,1)S(1)} %get-tuple-element.70), channel_id=1, source_target_pairs={{0,3},{1,2},{2,1},{3,0},{4,7},{5,6},{6,5},{7,4},{8,11},{9,10},{10,... | collective-permute-start | bytes 104456 | tf_op jit(solution)/shard_map/ppermute | solution.py:192
  99.7 4.3 %collective-permute-start.6 = (f16[17,8,128]{2,1,0:T(8,128)(2,1)S(1)}, f16[17,8,128]{2,1,0:T(8,128)(2,1)S(1)}, u32[]{:S(2)}, u32[]{:S(2)}) collective-permute-start(f16[17,8,128]{2,1,0:T(8,128)(2,1)S(1)} %get-tuple-element.23), channel_id=1, source_target_pairs={{0,2},{1,3},{2,0},{3,1},{4,6},{5,7},{6,4},{7,5},{8,10},{9,11},{10,... | collective-permute-start | bytes 104456 | tf_op jit(solution)/shard_map/ppermute | solution.py:192
  99.7 4.2 %collective-permute-start.7 = (f16[17,8,128]{2,1,0:T(8,128)(2,1)S(1)}, f16[17,8,128]{2,1,0:T(8,128)(2,1)S(1)}, u32[]{:S(2)}, u32[]{:S(2)}) collective-permute-start(f16[17,8,128]{2,1,0:T(8,128)(2,1)S(1)} %get-tuple-element.69), channel_id=1, source_target_pairs={{0,1},{1,0},{2,3},{3,2},{4,5},{5,4},{6,7},{7,6},{8,9},{9,8},{10,11... | collective-permute-start | bytes 104456 | tf_op jit(solution)/shard_map/ppermute | solution.py:192
  100.0 6.9 %collective-permute-start = (f16[33,8,128]{2,1,0:T(8,128)(2,1)S(1)}, f16[33,8,128]{2,1,0:T(8,128)(2,1)S(1)}, u32[]{:S(2)}, u32[]{:S(2)}) collective-permute-start(f16[33,8,128]{2,1,0:T(8,128)(2,1)S(1)} %get-tuple-element.60), channel_id=1, source_target_pairs={{0,3},{1,2},{2,1},{3,0},{4,7},{5,6},{6,5},{7,4},{8,11},{9,10},{10,... | collective-permute-start | bytes 202760 | tf_op jit(solution)/shard_map/ppermute | solution.py:192
  102.0 4.9 %collective-permute-start.1 = (f16[33,8,128]{2,1,0:T(8,128)(2,1)S(1)}, f16[33,8,128]{2,1,0:T(8,128)(2,1)S(1)}, u32[]{:S(2)}, u32[]{:S(2)}) collective-permute-start(f16[33,8,128]{2,1,0:T(8,128)(2,1)S(1)} %get-tuple-element.26), channel_id=1, source_target_pairs={{0,2},{1,3},{2,0},{3,1},{4,6},{5,7},{6,4},{7,5},{8,10},{9,11},{10,... | collective-permute-start | bytes 202760 | tf_op jit(solution)/shard_map/ppermute | solution.py:192
  102.1 4.8 %collective-permute-start.2 = (f16[33,8,128]{2,1,0:T(8,128)(2,1)S(1)}, f16[33,8,128]{2,1,0:T(8,128)(2,1)S(1)}, u32[]{:S(2)}, u32[]{:S(2)}) collective-permute-start(f16[33,8,128]{2,1,0:T(8,128)(2,1)S(1)} %get-tuple-element.59), channel_id=1, source_target_pairs={{0,1},{1,0},{2,3},{3,2},{4,5},{5,4},{6,7},{7,6},{8,9},{9,8},{10,11... | collective-permute-start | bytes 202760 | tf_op jit(solution)/shard_map/ppermute | solution.py:192
  104.1 11.3 %collective-permute-start.8 = (f16[4,17,8,128]{3,2,1,0:T(8,128)(2,1)S(1)}, f16[4,17,8,128]{3,2,1,0:T(8,128)(2,1)S(1)}, u32[]{:S(2)}, u32[]{:S(2)}) collective-permute-start(f16[4,17,8,128]{3,2,1,0:T(8,128)(2,1)S(1)} %pad_maximum_fusion.6), channel_id=1, source_target_pairs={{0,8},{1,9},{2,10},{3,11},{4,12},{5,13},{6,14},{7,15},{8,0},{9,1},... | collective-permute-start | bytes 417800 | tf_op jit(solution)/shard_map/ppermute | solution.py:192
  107.1 64.3 %all-to-all-start.2 = ((bf16[256,4,512]{2,1,0:T(4,128)(2,1)}), bf16[256,4,512]{2,1,0:T(4,128)(2,1)}, u32[]{:S(2)}, u32[]{:S(2)}) async-start(bf16[256,4,512]{2,1,0:T(4,128)(2,1)} %get-tuple-element.21), calls=%async_computation.2 | async-start | bytes 2097152 | tf_op jit(solution)/shard_map/all_to_all | solution.py:263
  112.6 38.0 %collective-permute-start.3 = (f16[4,33,8,128]{3,2,1,0:T(8,128)(2,1)S(1)}, f16[4,33,8,128]{3,2,1,0:T(8,128)(2,1)S(1)}, u32[]{:S(2)}, u32[]{:S(2)}) collective-permute-start(f16[4,33,8,128]{3,2,1,0:T(8,128)(2,1)S(1)} %pad_maximum_fusion.5), channel_id=1, source_target_pairs={{0,8},{1,9},{2,10},{3,11},{4,12},{5,13},{6,14},{7,15},{8,0},{9,1},... | collective-permute-start | bytes 811016 | tf_op jit(solution)/shard_map/ppermute | solution.py:192
  115.6 36.1 %collective-permute-start.9 = (f16[2,4,17,8,128]{4,3,2,1,0:T(8,128)(2,1)S(1)}, f16[2,4,17,8,128]{4,3,2,1,0:T(8,128)(2,1)S(1)}, u32[]{:S(2)}, u32[]{:S(2)}) collective-permute-start(f16[2,4,17,8,128]{4,3,2,1,0:T(8,128)(2,1)S(1)} %pad_maximum_fusion.4), channel_id=1, source_target_pairs={{0,4},{1,5},{2,6},{3,7},{4,0},{5,1},{6,2},{7,3},{8,12},{9,13},{10,... | collective-permute-start | bytes 835592 | tf_op jit(solution)/shard_map/ppermute | solution.py:192
  151.7 14.0 %collective-permute-start.4 = (f16[2,4,33,8,128]{4,3,2,1,0:T(8,128)(2,1)}, f16[2,4,33,8,128]{4,3,2,1,0:T(8,128)(2,1)}, u32[]{:S(2)}, u32[]{:S(2)}) collective-permute-start(f16[2,4,33,8,128]{4,3,2,1,0:T(8,128)(2,1)} %pad_maximum_fusion.2), channel_id=1, source_target_pairs={{0,4},{1,5},{2,6},{3,7},{4,0},{5,1},{6,2},{7,3},{8,12},{9,13},{10,... | collective-permute-start | bytes 1622024 | tf_op jit(solution)/shard_map/ppermute | solution.py:192
  152.7 14.4 %copy-start.6 = (f32[16,1,8,18]{0,2,3,1:T(8,128)}, f32[16,1,8,18]{0,2,3,1:T(8,128)S(1)}, u32[]{:S(2)}) copy-start(f32[16,1,8,18]{0,2,3,1:T(8,128)S(1)} %get-tuple-element.46) | copy-start | bytes 27652
  181.8 8.0 %copy-start.4 = (f16[16,16,8,128]{3,2,1,0:T(8,128)(2,1)S(1)}, f16[16,16,8,128]{3,2,1,0:T(8,128)(2,1)}, u32[]{:S(2)}) copy-start(f16[16,16,8,128]{3,2,1,0:T(8,128)(2,1)} %get-tuple-element.31) | copy-start | bytes 1572868
  181.8 18.7 %all-to-all-start.3 = ((f16[16,17,8,128]{3,2,1,0:T(8,128)(2,1)}), f16[16,17,8,128]{3,2,1,0:T(8,128)(2,1)S(1)}, u32[]{:S(2)}, u32[]{:S(2)}) async-start(f16[16,17,8,128]{3,2,1,0:T(8,128)(2,1)} %bitcast.46), calls=%async_computation.3 | async-start | bytes 1114112 | tf_op jit(solution)/shard_map/all_to_all | solution.py:197
  190.0 1.2 copy-start.1
  190.0 1.5 copy-start.2
  191.2 9.7 %copy-start.7 = (f32[16,1,8,18]{0,2,3,1:T(8,128)S(1)}, f32[16,1,8,18]{0,2,3,1:T(8,128)}, u32[]{:S(2)}) copy-start(f32[16,1,8,18]{0,2,3,1:T(8,128)} %copy-done.6) | copy-start | bytes 27652
  203.2 1.5 copy-start

commit v3 on v2

--- a/solution.py
+++ b/solution.py
@@ -25,10 +25,8 @@
     return value.astype(jnp.bfloat16)
 
 
-def stack_kernel(sizes, me_ref, top_ref, *refs):
+def stack_kernel(sizes, top_ref, moved_ref, message_ref, matrix, rows32, data, data16, quad, normed, stack):
     lag_groups, days_here, group, lags, n_src = sizes
-    ins = refs[:-8]
-    message_ref, matrix, rows32, data, data16, quad, normed, stack = refs[-8:]
     days = n_src // lag_groups * days_here
     width = lags // lag_groups
     tiles = width // LANES
@@ -44,23 +42,17 @@
                 matrix[cut:cut + top_rows, :cut] = top_ref[:, lags - cut:]
             matrix[cut:cut + top_rows, cut:] = top_ref[:, :lags - cut]
 
+    here = pl.multiple_of(pl.program_id(0) * group * pitch, group * pitch)
     for s in range(n_src):
-        if len(ins) == 1:
-            here = pl.multiple_of(pl.program_id(0) * group * pitch, group * pitch)
-            rows32[...] = ins[0][s, pl.ds(here, group * pitch), :].astype(jnp.float32)
-            block, part = divmod(s, lag_groups)
-        else:
-            rows32[...] = ins[s][...].astype(jnp.float32)
-            source = me_ref[0] ^ s
-            block, part = source // lag_groups, source % lag_groups
+        block, part = divmod(s, lag_groups)
+        rows32[...] = moved_ref[s, pl.ds(here, group * pitch), :].astype(jnp.float32)
         for d in range(days_here):
             day = block * days_here + d
-            row = pl.multiple_of(day * group, group)
             for t in range(tiles):
-                lane = pl.ds(pl.multiple_of(part * width + t * LANES, LANES), LANES)
+                lane = slice(part * width + t * LANES, part * width + (t + 1) * LANES)
                 x = rows32[pl.ds(t * days_here + d, group, stride=pitch), :]
                 data[day, :, lane] = x
-                data16[pl.ds(row, group), lane] = x.astype(jnp.bfloat16)
+                data16[day * group:(day + 1) * group, lane] = x.astype(jnp.bfloat16)
 
     quad[...] = jnp.dot(data16[...], matrix[...], preferred_element_type=jnp.float32)
 
@@ -96,7 +88,8 @@
                 for t in range(tiles):
                     place = (kind * all_bands + pl.program_id(0) * bands + r) * tiles + t
                     lane = part * width + t * LANES
-                    message_ref[part, place] = value[r * SUBLANES:(r + 1) * SUBLANES, lane:lane + LANES]
+                    for copy in range(part, message_ref.shape[0], lag_groups):
+                        message_ref[copy, place] = value[r * SUBLANES:(r + 1) * SUBLANES, lane:lane + LANES]
         return power
 
     powers = [emit(0, stack[...])]
@@ -128,12 +121,12 @@
         for k in range(per):
             @pl.when(band % per == k)
             def _():
-                for part in range(lag_groups):
+                for part in range(message_ref.shape[0]):
                     message_ref[part, 2 * tiles * all_bands + band // per, :, k * (days + 2):(k + 1) * (days + 2)] = (
                         side[r * SUBLANES:(r + 1) * SUBLANES])
 
 
-def stack_pairs(me, pieces, top, lag_groups, days_here, pairs, group, n_src):
+def stack_pairs(moved, top, lag_groups, days_here, pairs, group, n_src, repeats):
     lags = top.shape[1]
     days = n_src // lag_groups * days_here
     width = lags // lag_groups
@@ -143,16 +136,14 @@
     cost = pl.CostEstimate(
         flops=2 * pairs * days * lags * lags, bytes_accessed=pairs * days * lags * 2, transcendentals=pairs * days * lags
     )
-    if len(pieces) == 1:
-        piece_specs = [pl.BlockSpec(memory_space=pltpu.VMEM)]
-    else:
-        piece_specs = [pl.BlockSpec((group * pitch, LANES), lambda i: (i, 0))] * n_src
+    need = 2 * lags * lags + 10 * days * group * lags + 8 * group * lags + 2 * moved.size + 4 * top.size
+    need += 4 * repeats * lag_groups * tiles * SUBLANES * LANES
     return pl.pallas_call(
         functools.partial(stack_kernel, (lag_groups, days_here, group, lags, n_src)),
         grid=(pairs // group,),
-        in_specs=[pl.BlockSpec(memory_space=pltpu.SMEM), pl.BlockSpec(top.shape, lambda i: (0, 0))] + piece_specs,
+        in_specs=[pl.BlockSpec(top.shape, lambda i: (0, 0)), pl.BlockSpec(memory_space=pltpu.VMEM)],
         out_specs=pl.BlockSpec(memory_space=pltpu.VMEM),
-        out_shape=jax.ShapeDtypeStruct((lag_groups, tiles, SUBLANES, LANES), jnp.float32),
+        out_shape=jax.ShapeDtypeStruct((repeats * lag_groups, tiles, SUBLANES, LANES), jnp.float32),
         scratch_shapes=[
             pltpu.VMEM((lags, lags), jnp.bfloat16),
             pltpu.VMEM((group * pitch, LANES), jnp.float32),
@@ -163,26 +154,66 @@
             pltpu.VMEM((group, lags), jnp.float32),
         ],
         cost_estimate=cost,
+        compiler_params=pltpu.CompilerParams(vmem_limit_bytes=need + 6 * 2**20),
         name="stack_pairs",
-    )(me, top, *pieces)
-
-
-def unpack(message, pairs, width, days, days_here):
-    n = message.shape[0]
-    bands, tiles, per = pairs // SUBLANES, width // LANES, LANES // (days + 2)
-    side = message[:, 2 * bands * tiles:].astype(jnp.float32)
-    blocks = [side[:, r // per, :, r % per * (days + 2):(r % per + 1) * (days + 2)] for r in range(bands)]
-    blocks = jnp.stack(blocks, axis=1)
-    shares = lax.dynamic_slice_in_dim(blocks, lax.axis_index("day") * days_here, days_here, 3) / 1024.0
-    outs = []
-    for kind in range(2):
-        scale = jnp.exp2(blocks[:, :, :, days + kind] - 9.0)
-        scale = jnp.broadcast_to(scale[:, :, None, :, None], (n, bands, 1, SUBLANES, LANES))
-        scale = lax.optimization_barrier(scale)
-        value = message[:, kind * bands * tiles:(kind + 1) * bands * tiles].astype(jnp.float32)
-        value = value.reshape(n, bands, tiles, SUBLANES, LANES) * scale
-        outs.append(jnp.swapaxes(value, 2, 3).reshape(n * pairs, width))
-    return outs[0], outs[1], shares.reshape(n * pairs, days_here)
+    )(top, moved)
+
+
+def place_kernel(sizes, me_ref, *refs):
+    pairs, row, moves, n_old, lag_groups, days, days_here = sizes
+    n_blocks = len(moves)
+    blocks = refs[:n_blocks]
+    outs, buffers, sems = refs[n_blocks + n_old:-4], refs[-4:-1], refs[-1]
+    bands = pairs // SUBLANES
+    tiles = buffers[0].shape[2] // LANES
+    per = LANES // (days + 2)
+    my_day = me_ref[0] // lag_groups
+    copies = []
+    for b, (block, move) in enumerate(zip(blocks, moves)):
+        sources = block.shape[0]
+        for i in range(sources):
+            for group in range(pl.cdiv(bands, per)):
+                side = block[i, 2 * bands * tiles + group]
+                scales = jnp.exp2(side - 9.0)
+                for r in range(group * per, min(bands, (group + 1) * per)):
+                    lane = (r - group * per) * (days + 2)
+                    at = slice((i * bands + r) * SUBLANES, (i * bands + r + 1) * SUBLANES)
+                    for kind in range(2):
+                        scale = jnp.broadcast_to(scales[:, lane + days + kind:lane + days + kind + 1], (SUBLANES, LANES))
+                        for t in range(tiles):
+                            buffers[kind][b, at, t * LANES:(t + 1) * LANES] = (
+                                block[i, (kind * bands + r) * tiles + t] * scale)
+                    shift = (2 * LANES - lane - my_day * days_here) % LANES
+                    buffers[2][b, at, :] = pltpu.roll(side, shift, 1) * (1.0 / 1024.0)
+        rows = sources * pairs
+        first = row
+        if move is not None:
+            first = pl.multiple_of(row + (my_day ^ move) * rows, SUBLANES)
+        for k in range(3):
+            copy = pltpu.make_async_copy(buffers[k].at[b], outs[k].at[pl.ds(first, rows), :], sems.at[k, b])
+            copy.start()
+            copies.append(copy)
+    for copy in copies:
+        copy.wait()
+
+
+def place(outs, blocks, moves, me, shapes, row, pairs, lag_groups, days, days_here):
+    blocks = [b.astype(jnp.float32) for b in blocks]
+    rows = blocks[0].shape[0] * pairs
+    n = len(blocks)
+    old = list(outs or [])
+    return pl.pallas_call(
+        functools.partial(place_kernel, (pairs, row, moves, len(old), lag_groups, days, days_here)),
+        in_specs=[pl.BlockSpec(memory_space=pltpu.SMEM)] + [pl.BlockSpec(memory_space=pltpu.VMEM)] * n
+        + [pl.BlockSpec(memory_space=pl.ANY)] * len(old),
+        out_specs=[pl.BlockSpec(memory_space=pl.ANY)] * 3,
+        out_shape=[jax.ShapeDtypeStruct(shape, jnp.float32) for shape in shapes],
+        input_output_aliases={1 + n + k: k for k in range(len(old))},
+        scratch_shapes=[pltpu.VMEM((n, rows, shape[1]), jnp.float32) for shape in shapes] + [pltpu.SemaphoreType.DMA((3, n))],
+        cost_estimate=pl.CostEstimate(flops=4 * n * rows * shapes[0][1], bytes_accessed=16 * n * rows * shapes[0][1], transcendentals=0),
+        compiler_params=pltpu.CompilerParams(vmem_limit_bytes=20 * 2**20),
+        name="place",
+    )(me.reshape(1), *blocks, *old)
 
 
 AXES = ("day", "lag")
@@ -190,11 +221,6 @@
 
 def swap(x, n, by):
     return lax.ppermute(x, AXES, [(i, i ^ by) for i in range(n)])
-
-
-def spread_direct(message, day_groups, n):
-    message = jnp.broadcast_to(message[None], (day_groups,) + message.shape).reshape((n,) + message.shape[1:])
-    return lax.all_to_all(message, AXES, 0, 0, tiled=True)
 
 
 def unswap(pieces, index):
@@ -213,11 +239,11 @@
     return jnp.stack(unswap(got, lag))
 
 
-def spread_days(got, me, lag_groups, n):
-    near, far = me // lag_groups % 2, me // (2 * lag_groups)
-    got = jnp.stack(unswap([got, swap(got, n, 2 * lag_groups)], far))
-    got = jnp.stack(unswap([got, swap(got, n, lag_groups)], near), axis=1)
-    return got.reshape((n,) + got.shape[3:])
+def spread_days(mine, lag_groups, n):
+    far = swap(mine, n, 2 * lag_groups)
+    near = swap(mine, n, lag_groups)
+    last = swap(far, n, lag_groups)
+    return (0, 2, 1, 3), (mine, far, near, last)
 
 
 def per_device(corr):
@@ -239,12 +265,12 @@
         piece = jnp.swapaxes(piece, -2, -3)
         return piece.reshape(lead + (-1, LANES))
 
-    outs = [jnp.zeros((pairs, width), jnp.float32), jnp.zeros((pairs, width), jnp.float32)]
     starts = [sum(p for p, _, _ in plan[:k]) for k in range(len(plan))]
     moved, sent = [], []
 
     def work(k):
-        message = stack_pairs(me.reshape(1), moved[k], top, lag_groups, days_here, plan[k][0], 16 if plan[k][0] % 16 == 0 else 8, n)
+        message = stack_pairs(moved[k], top, lag_groups, days_here, plan[k][0], 16 if plan[k][0] % 16 == 0 else 8, n,
+                              1 if plan[k][2] == "staged" else day_groups)
         message = message.astype(jnp.float16)
         if plan[k][2] == "staged":
             message = spread_lags(message, me, lag_groups, n)
@@ -254,22 +280,36 @@
         if k >= 2:
             work(k - 2)
         if k == 1:
-            corr, top, *outs = lax.optimization_barrier((corr, top, *outs))
+            corr, top = lax.optimization_barrier((corr, top))
         rows = corr[starts[k] * n:(starts[k] + p) * n]
         if k >= 1:
             rows, moved[k - 1] = lax.optimization_barrier((rows, moved[k - 1]))
         if k >= 2:
             rows, sent[k - 2] = lax.optimization_barrier((rows, sent[k - 2]))
         got = lax.all_to_all(rows, AXES, 0, 0, tiled=True)
-        moved.append([flat(got.reshape(n, p, days_here, width), (n,))])
+        moved.append(flat(got.reshape(n, p, days_here, width), (n,)))
     for k in range(len(sent), len(plan)):
         work(k)
-    outs = list(outs) + [jnp.zeros((pairs, days_here), jnp.float32)]
+    shapes = ((pairs, width), (pairs, width), (pairs, LANES))
+    outs = None
+    todo = []
     for k, (p, _, how) in enumerate(plan):
-        spread = spread_direct(sent[k], day_groups, n) if how == "all" else spread_days(sent[k], me, lag_groups, n)
-        parts = unpack(spread, p, width, days, days_here)
-        outs = [lax.dynamic_update_slice(o, v, (starts[k] * n, 0)) for o, v in zip(outs, parts)]
-    return tuple(outs)
+        if how == "all":
+            turns = [((None,), (lax.all_to_all(sent[k], AXES, 0, 0, tiled=True),))]
+        else:
+            moves, blocks = spread_days(sent[k], lag_groups, n)
+            turns = [(moves[:2], blocks[:2]), (moves[2:], blocks[2:])]
+        todo.append((k, turns))
+    turns_of = {k: list(turns) for k, turns in todo}
+    last = len(plan) - 1
+    sequence = [(k, 0) for k in range(last - 1)]
+    if last:
+        sequence += [(k, 1) for k in range(last - 1)] + [(last - 1, 0), (last - 1, 1)]
+    sequence.append((last, 0))
+    for k, turn in sequence:
+        moves, blocks = turns_of[k][turn]
+        outs = place(outs, blocks, moves, me, shapes, starts[k] * n, plan[k][0], lag_groups, days, days_here)
+    return outs[0], outs[1], outs[2][:, :days_here]
 
 
 def solution(mesh):

time: 206 us -> 182 us (0.88)
  blocking collectives: 0 us -> 30 us
  waiting for transfers between devices: 85.2 us -> 59.9 us
  local copies, waits for them, and re-layouts: 21.5 us -> 9.26 us
  other arithmetic: 23.2 us -> 11.8 us
  starting transfers between devices: 39.9 us -> 36.8 us
    all_to_all x0 -> x1, blocking collectives: none -> 30 us  [per_device(): got = lax.all_to_all(rows, AXES, 0, 0, tiled=True)]
    ppermute x10 -> x12, waiting for transfers between devices: 46.2 us -> 32.7 us  [swap(): return lax.ppermute(x, AXES, [(i, i ^ by) for i in range(n)])]
    all_to_all x1, waiting for transfers between devices: 8.23 us -> 0.01 us  [per_device(): turns = [((None,), (lax.all_to_all(sent[k], AXES, 0, 0, tiled=True),))]]
    pallas_call x3, Pallas kernels: 33.7 us -> 26.6 us  [stack_pairs(): pl.pallas_call(functools.partial(stack_kernel, (lag_groups, days_here, gr...]
    pallas_call x0 -> x5, Pallas kernels: none -> 5.6 us  [place(): pl.pallas_call(functools.partial(place_kernel, (pairs, row, moves, len(ol...]
    all_to_all x3 -> x2, starting transfers between devices: 24.1 us -> 18.6 us  [per_device(): got = lax.all_to_all(rows, AXES, 0, 0, tiled=True)]
    dynamic_update_slice x8 -> x0, local copies, waits for them, and re-layouts: 4.82 us -> none  [per_device(): lax.dynamic_update_slice(o, v, (starts[k] * n, 0))]
    another operation x9 -> x0, other arithmetic: 3.98 us -> none  [the longest x4 1.96 us: spread_days(): got = jnp.stack(unswap([got, swap(got, n, lag_groups)], near), axis=1)]
  transfers between devices with their start and end apart: 14 -> 15, of which waited for: 6 -> 8; matrix products, arithmetic and copies ran while one was open for 16% -> 8% of each run, Pallas kernels for 8% -> 14%
where the time goes in v3:
time: 182 us; the launch traced here: 181 us
  waiting for transfers between devices  59.9 us (33%)
  starting transfers between devices  36.8 us (20%)
  Pallas kernels  32.2 us (18%)
  blocking collectives  30 us (16%)
  other arithmetic  11.8 us (6%)
  local copies, waits for them, and re-layouts  9.26 us (5%)
    ppermute x12, waiting for transfers between devices, swap(): return lax.ppermute(x, AXES, [(i, i ^ by) for i in range(n)])  32.7 us
    all_to_all x1, blocking collectives, per_device(): got = lax.all_to_all(rows, AXES, 0, 0, tiled=True)  30 us
    all_to_all x2, waiting for transfers between devices, per_device(): got = lax.all_to_all(rows, AXES, 0, 0, tiled=True)  27.2 us
    pallas_call x3, Pallas kernels, stack_pairs(): pl.pallas_call(functools.partial(stack_kernel, (lag_groups, days_here, gr...  26.6 us
    all_to_all x2, starting transfers between devices, per_device(): got = lax.all_to_all(rows, AXES, 0, 0, tiled=True)  18.6 us
    ppermute x12, starting transfers between devices, swap(): return lax.ppermute(x, AXES, [(i, i ^ by) for i in range(n)])  13.2 us
    convert_element_type x1, other arithmetic, kernel_rows(): return value.astype(jnp.bfloat16)  10.2 us
    slice x2, local copies, waits for them, and re-layouts, per_device(): rows = corr[starts[k] * n:(starts[k] + p) * n]  7.24 us
  transfers between devices with their start and end apart: 15, of which 8 were waited for; matrix products, arithmetic and copies ran while one was open for 8% of the time, Pallas kernels for 14%

profile of v3, /device:TPU:0, one launch (start us, length us, event | category | flops | bytes accessed | tf_op | source)
XLA Modules:
  0.0 181.0 jit_solution(8602024293753467536)
XLA Ops:
  0.6 3.6 %slice.38 = bf16[512,4,512]{2,1,0:T(4,128)(2,1)} slice(bf16[1024,4,512]{2,1,0:T(4,128)(2,1)} %param.1), slice={[0:512], [0:4], [0:512]} | slice | bytes 4194304 | tf_op jit(solution)/shard_map/slice | solution.py:284
  4.3 7.4 %all-to-all-start = ((bf16[512,4,512]{2,1,0:T(4,128)(2,1)}), bf16[512,4,512]{2,1,0:T(4,128)(2,1)S(1)}, u32[]{:S(2)}, u32[]{:S(2)}) async-start(bf16[512,4,512]{2,1,0:T(4,128)(2,1)} %slice.38), calls=%async_computation | async-start | bytes 4194304 | tf_op jit(solution)/shard_map/all_to_all | solution.py:289
  11.7 10.2 %select_convert_fusion.top_ref = bf16[256,2048]{1,0:T(8,128)(2,1)} fusion(), kind=kLoop, calls=%fused_computation.9 | loop fusion | flops 16252928 | bytes 1048576 | tf_op jit(solution)/shard_map/convert_element_type | solution.py:25
  21.8 3.6 %fusion.8 = (bf16[256,4,512]{2,1,0:T(4,128)(2,1)}, bf16[256,4,512]{2,1,0:T(4,128)(2,1)}) fusion(bf16[1024,4,512]{2,1,0:T(4,128)(2,1)} %param.1), kind=kLoop, calls=%fused_computation.49 | loop fusion | bytes 4194304 | tf_op jit(solution)/shard_map/slice | solution.py:284
  25.4 27.2 %all-to-all-done = bf16[512,4,512]{2,1,0:T(4,128)(2,1)S(1)} async-done(((bf16[512,4,512]{2,1,0:T(4,128)(2,1)}), bf16[512,4,512]{2,1,0:T(4,128)(2,1)S(1)}, u32[]{:S(2)}, u32[]{:S(2)}) %all-to-all-start) | async-done | bytes 2097184 | tf_op jit(solution)/shard_map/all_to_all | solution.py:289
  52.7 11.2 %all-to-all-start.1 = ((bf16[256,4,512]{2,1,0:T(4,128)(2,1)}), bf16[256,4,512]{2,1,0:T(4,128)(2,1)S(1)}, u32[]{:S(2)}, u32[]{:S(2)}) async-start(bf16[256,4,512]{2,1,0:T(4,128)(2,1)} %get-tuple-element.28), calls=%async_computation.1 | async-start | bytes 2097152 | tf_op jit(solution)/shard_map/all_to_all | solution.py:289
  64.0 1.2 copy-done
  65.2 13.9 %stack_pairs.3 = f32[4,33,8,128]{3,2,1,0:T(8,128)S(1)} custom-call(bf16[256,2048]{1,0:T(8,128)(2,1)S(1)} %copy-done, bf16[16,512,128]{2,1,0:T(8,128)(2,1)S(1)} %bitcast.68), custom_call_target="tpu_custom_call" | custom-call | flops 4294967296 | bytes 2097152 | tf_op jit(solution)/shard_map/stack_pairs/pallas_call | solution.py:141
  79.2 1.9 %collective-permute-start.1 = (f16[33,8,128]{2,1,0:T(8,128)(2,1)S(1)}, f16[33,8,128]{2,1,0:T(8,128)(2,1)S(1)}, u32[]{:S(2)}, u32[]{:S(2)}) collective-permute-start(f16[33,8,128]{2,1,0:T(8,128)(2,1)S(1)} %get-tuple-element.55), channel_id=1, source_target_pairs={{0,2},{1,3},{2,0},{3,1},{4,6},{5,7},{6,4},{7,5},{8,10},{9,11},{10,... | collective-permute-start | bytes 202760 | tf_op jit(solution)/shard_map/ppermute | solution.py:223
  81.4 2.2 %collective-permute-done.1 = f16[33,8,128]{2,1,0:T(8,128)(2,1)S(1)} collective-permute-done((f16[33,8,128]{2,1,0:T(8,128)(2,1)S(1)}, f16[33,8,128]{2,1,0:T(8,128)(2,1)S(1)}, u32[]{:S(2)}, u32[]{:S(2)}) %collective-permute-start.1) | collective-permute-done | bytes 67616 | tf_op jit(solution)/shard_map/ppermute | solution.py:223
  83.7 4.1 %collective-permute-done = f16[33,8,128]{2,1,0:T(8,128)(2,1)S(1)} collective-permute-done((f16[33,8,128]{2,1,0:T(8,128)(2,1)S(1)}, f16[33,8,128]{2,1,0:T(8,128)(2,1)S(1)}, u32[]{:S(2)}, u32[]{:S(2)}) %collective-permute-start) | collective-permute-done | bytes 67616 | tf_op jit(solution)/shard_map/ppermute | solution.py:223
  88.0 30.0 %all_to_all.20 = bf16[256,4,512]{2,1,0:T(4,128)(2,1)S(1)} all-to-all(bf16[256,4,512]{2,1,0:T(4,128)(2,1)S(1)} %copy-done.2), channel_id=1, replica_groups=mesh['pair'=2,'day'=4,'lag'=4] {'day','lag'}, dimensions={0} | all-to-all | bytes 2097152 | tf_op jit(solution)/shard_map/all_to_all | solution.py:289
  118.0 6.4 %stack_pairs.4 = f32[16,17,8,128]{3,2,1,0:T(8,128)S(1)} custom-call(bf16[256,2048]{1,0:T(8,128)(2,1)S(1)} %copy-done.1, bf16[16,256,128]{2,1,0:T(8,128)(2,1)S(1)} %bitcast.70), custom_call_target="tpu_custom_call" | custom-call | flops 2147483648 | bytes 1048576 | tf_op jit(solution)/shard_map/stack_pairs/pallas_call | solution.py:141
  125.3 5.0 %all-to-all-start.3 = ((f16[16,17,8,128]{3,2,1,0:T(8,128)(2,1)}), f16[16,17,8,128]{3,2,1,0:T(8,128)(2,1)S(1)}, u32[]{:S(2)}, u32[]{:S(2)}) async-start(f16[16,17,8,128]{3,2,1,0:T(8,128)(2,1)} %convert_element_type.45), calls=%async_computation.3 | async-start | bytes 1114112 | tf_op jit(solution)/shard_map/all_to_all | solution.py:298
  130.4 6.4 %stack_pairs.5 = f32[4,17,8,128]{3,2,1,0:T(8,128)S(1)} custom-call(bf16[256,2048]{1,0:T(8,128)(2,1)S(1)} %copy-done.1, bf16[16,256,128]{2,1,0:T(8,128)(2,1)S(1)} %bitcast.69), custom_call_target="tpu_custom_call" | custom-call | flops 2147483648 | bytes 1048576 | tf_op jit(solution)/shard_map/stack_pairs/pallas_call | solution.py:141
  136.8 2.0 %collective-permute-start.4 = (f16[17,8,128]{2,1,0:T(8,128)(2,1)S(1)}, f16[17,8,128]{2,1,0:T(8,128)(2,1)S(1)}, u32[]{:S(2)}, u32[]{:S(2)}) collective-permute-start(f16[17,8,128]{2,1,0:T(8,128)(2,1)S(1)} %get-tuple-element.52), channel_id=1, source_target_pairs={{0,2},{1,3},{2,0},{3,1},{4,6},{5,7},{6,4},{7,5},{8,10},{9,11},{10,... | collective-permute-start | bytes 104456 | tf_op jit(solution)/shard_map/ppermute | solution.py:223
  139.0 2.8 %collective-permute-start.10 = (f16[4,33,8,128]{3,2,1,0:T(8,128)(2,1)S(1)}, f16[4,33,8,128]{3,2,1,0:T(8,128)(2,1)S(1)}, u32[]{:S(2)}, u32[]{:S(2)}) collective-permute-start(f16[4,33,8,128]{3,2,1,0:T(8,128)(2,1)S(1)} %pad_maximum_fusion), channel_id=1, source_target_pairs={{0,8},{1,9},{2,10},{3,11},{4,12},{5,13},{6,14},{7,15},{8,0},{9,1},... | collective-permute-start | bytes 811016 | tf_op jit(solution)/shard_map/ppermute | solution.py:223
  142.3 3.3 %collective-permute-start.7 = (f16[4,17,8,128]{3,2,1,0:T(8,128)(2,1)S(1)}, f16[4,17,8,128]{3,2,1,0:T(8,128)(2,1)S(1)}, u32[]{:S(2)}, u32[]{:S(2)}) collective-permute-start(f16[4,17,8,128]{3,2,1,0:T(8,128)(2,1)S(1)} %get-tuple-element.71), channel_id=1, source_target_pairs={{0,8},{1,9},{2,10},{3,11},{4,12},{5,13},{6,14},{7,15},{8,0},{9,1},... | collective-permute-start | bytes 417800 | tf_op jit(solution)/shard_map/ppermute | solution.py:223
  146.2 15.3 %collective-permute-done.10 = f16[4,33,8,128]{3,2,1,0:T(8,128)(2,1)S(1)} collective-permute-done((f16[4,33,8,128]{3,2,1,0:T(8,128)(2,1)S(1)}, f16[4,33,8,128]{3,2,1,0:T(8,128)(2,1)S(1)}, u32[]{:S(2)}, u32[]{:S(2)}) %collective-permute-start.10) | collective-permute-done | bytes 270368 | tf_op jit(solution)/shard_map/ppermute | solution.py:223
  161.4 2.0 %collective-permute-start.6 = (f16[4,17,8,128]{3,2,1,0:T(8,128)(2,1)S(1)}, f16[4,17,8,128]{3,2,1,0:T(8,128)(2,1)S(1)}, u32[]{:S(2)}, u32[]{:S(2)}) collective-permute-start(f16[4,17,8,128]{3,2,1,0:T(8,128)(2,1)S(1)} %get-tuple-element.71), channel_id=1, source_target_pairs={{0,4},{1,5},{2,6},{3,7},{4,0},{5,1},{6,2},{7,3},{8,12},{9,13},{10,... | collective-permute-start | bytes 417800 | tf_op jit(solution)/shard_map/ppermute | solution.py:223
  164.0 9.8 %collective-permute-done.6 = f16[4,17,8,128]{3,2,1,0:T(8,128)(2,1)S(1)} collective-permute-done((f16[4,17,8,128]{3,2,1,0:T(8,128)(2,1)S(1)}, f16[4,17,8,128]{3,2,1,0:T(8,128)(2,1)S(1)}, u32[]{:S(2)}, u32[]{:S(2)}) %collective-permute-start.6) | collective-permute-done | bytes 139296 | tf_op jit(solution)/shard_map/ppermute | solution.py:223
  173.9 1.2 place.5
  175.7 1.2 place.6
  179.0 1.2 place.9
  (42 shorter events, 6.9 us)
Async XLA Ops:
  4.3 48.4 %all-to-all-start = ((bf16[512,4,512]{2,1,0:T(4,128)(2,1)}), bf16[512,4,512]{2,1,0:T(4,128)(2,1)S(1)}, u32[]{:S(2)}, u32[]{:S(2)}) async-start(bf16[512,4,512]{2,1,0:T(4,128)(2,1)} %slice.38), calls=%async_computation | async-start | bytes 4194304 | tf_op jit(solution)/shard_map/all_to_all | solution.py:289
  52.7 35.4 %all-to-all-start.1 = ((bf16[256,4,512]{2,1,0:T(4,128)(2,1)}), bf16[256,4,512]{2,1,0:T(4,128)(2,1)S(1)}, u32[]{:S(2)}, u32[]{:S(2)}) async-start(bf16[256,4,512]{2,1,0:T(4,128)(2,1)} %get-tuple-element.28), calls=%async_computation.1 | async-start | bytes 2097152 | tf_op jit(solution)/shard_map/all_to_all | solution.py:289
  63.9 1.2 copy-start
  79.1 8.9 %copy-start.2 = (bf16[256,4,512]{2,1,0:T(4,128)(2,1)S(1)}, bf16[256,4,512]{2,1,0:T(4,128)(2,1)}, u32[]{:S(2)}) copy-start(bf16[256,4,512]{2,1,0:T(4,128)(2,1)} %get-tuple-element.31) | copy-start | bytes 3145732
  79.1 38.9 %copy-start.1 = (bf16[256,2048]{1,0:T(8,128)(2,1)S(1)}, bf16[256,2048]{1,0:T(8,128)(2,1)}, u32[]{:S(2)}) copy-start(bf16[256,2048]{1,0:T(8,128)(2,1)} %select_convert_fusion.top_ref) | copy-start | bytes 3145732
  79.2 4.4 %collective-permute-start.1 = (f16[33,8,128]{2,1,0:T(8,128)(2,1)S(1)}, f16[33,8,128]{2,1,0:T(8,128)(2,1)S(1)}, u32[]{:S(2)}, u32[]{:S(2)}) collective-permute-start(f16[33,8,128]{2,1,0:T(8,128)(2,1)S(1)} %get-tuple-element.55), channel_id=1, source_target_pairs={{0,2},{1,3},{2,0},{3,1},{4,6},{5,7},{6,4},{7,5},{8,10},{9,11},{10,... | collective-permute-start | bytes 202760 | tf_op jit(solution)/shard_map/ppermute | solution.py:223
  81.1 2.5 %collective-permute-start.2 = (f16[33,8,128]{2,1,0:T(8,128)(2,1)S(1)}, f16[33,8,128]{2,1,0:T(8,128)(2,1)S(1)}, u32[]{:S(2)}, u32[]{:S(2)}) collective-permute-start(f16[33,8,128]{2,1,0:T(8,128)(2,1)S(1)} %get-tuple-element.64), channel_id=1, source_target_pairs={{0,1},{1,0},{2,3},{3,2},{4,5},{5,4},{6,7},{7,6},{8,9},{9,8},{10,11... | collective-permute-start | bytes 202760 | tf_op jit(solution)/shard_map/ppermute | solution.py:223
  81.1 6.7 %collective-permute-start = (f16[33,8,128]{2,1,0:T(8,128)(2,1)S(1)}, f16[33,8,128]{2,1,0:T(8,128)(2,1)S(1)}, u32[]{:S(2)}, u32[]{:S(2)}) collective-permute-start(f16[33,8,128]{2,1,0:T(8,128)(2,1)S(1)} %get-tuple-element.65), channel_id=1, source_target_pairs={{0,3},{1,2},{2,1},{3,0},{4,7},{5,6},{6,5},{7,4},{8,11},{9,10},{10,... | collective-permute-start | bytes 202760 | tf_op jit(solution)/shard_map/ppermute | solution.py:223
  125.3 53.6 %all-to-all-start.3 = ((f16[16,17,8,128]{3,2,1,0:T(8,128)(2,1)}), f16[16,17,8,128]{3,2,1,0:T(8,128)(2,1)S(1)}, u32[]{:S(2)}, u32[]{:S(2)}) async-start(f16[16,17,8,128]{3,2,1,0:T(8,128)(2,1)} %convert_element_type.45), calls=%async_computation.3 | async-start | bytes 1114112 | tf_op jit(solution)/shard_map/all_to_all | solution.py:298
  136.8 5.0 %collective-permute-start.4 = (f16[17,8,128]{2,1,0:T(8,128)(2,1)S(1)}, f16[17,8,128]{2,1,0:T(8,128)(2,1)S(1)}, u32[]{:S(2)}, u32[]{:S(2)}) collective-permute-start(f16[17,8,128]{2,1,0:T(8,128)(2,1)S(1)} %get-tuple-element.52), channel_id=1, source_target_pairs={{0,2},{1,3},{2,0},{3,1},{4,6},{5,7},{6,4},{7,5},{8,10},{9,11},{10,... | collective-permute-start | bytes 104456 | tf_op jit(solution)/shard_map/ppermute | solution.py:223
  138.8 3.0 %collective-permute-start.5 = (f16[17,8,128]{2,1,0:T(8,128)(2,1)S(1)}, f16[17,8,128]{2,1,0:T(8,128)(2,1)S(1)}, u32[]{:S(2)}, u32[]{:S(2)}) collective-permute-start(f16[17,8,128]{2,1,0:T(8,128)(2,1)S(1)} %get-tuple-element.72), channel_id=1, source_target_pairs={{0,1},{1,0},{2,3},{3,2},{4,5},{5,4},{6,7},{7,6},{8,9},{9,8},{10,11... | collective-permute-start | bytes 104456 | tf_op jit(solution)/shard_map/ppermute | solution.py:223
  138.8 3.4 %collective-permute-start.3 = (f16[17,8,128]{2,1,0:T(8,128)(2,1)S(1)}, f16[17,8,128]{2,1,0:T(8,128)(2,1)S(1)}, u32[]{:S(2)}, u32[]{:S(2)}) collective-permute-start(f16[17,8,128]{2,1,0:T(8,128)(2,1)S(1)} %get-tuple-element.73), channel_id=1, source_target_pairs={{0,3},{1,2},{2,1},{3,0},{4,7},{5,6},{6,5},{7,4},{8,11},{9,10},{10,... | collective-permute-start | bytes 104456 | tf_op jit(solution)/shard_map/ppermute | solution.py:223
  139.0 22.4 %collective-permute-start.10 = (f16[4,33,8,128]{3,2,1,0:T(8,128)(2,1)S(1)}, f16[4,33,8,128]{3,2,1,0:T(8,128)(2,1)S(1)}, u32[]{:S(2)}, u32[]{:S(2)}) collective-permute-start(f16[4,33,8,128]{3,2,1,0:T(8,128)(2,1)S(1)} %pad_maximum_fusion), channel_id=1, source_target_pairs={{0,8},{1,9},{2,10},{3,11},{4,12},{5,13},{6,14},{7,15},{8,0},{9,1},... | collective-permute-start | bytes 811016 | tf_op jit(solution)/shard_map/ppermute | solution.py:223
  142.3 21.7 %collective-permute-start.7 = (f16[4,17,8,128]{3,2,1,0:T(8,128)(2,1)S(1)}, f16[4,17,8,128]{3,2,1,0:T(8,128)(2,1)S(1)}, u32[]{:S(2)}, u32[]{:S(2)}) collective-permute-start(f16[4,17,8,128]{3,2,1,0:T(8,128)(2,1)S(1)} %get-tuple-element.71), channel_id=1, source_target_pairs={{0,8},{1,9},{2,10},{3,11},{4,12},{5,13},{6,14},{7,15},{8,0},{9,1},... | collective-permute-start | bytes 417800 | tf_op jit(solution)/shard_map/ppermute | solution.py:223
  145.6 28.3 %collective-permute-start.9 = (f16[4,33,8,128]{3,2,1,0:T(8,128)(2,1)S(1)}, f16[4,33,8,128]{3,2,1,0:T(8,128)(2,1)S(1)}, u32[]{:S(2)}, u32[]{:S(2)}) collective-permute-start(f16[4,33,8,128]{3,2,1,0:T(8,128)(2,1)S(1)} %pad_maximum_fusion), channel_id=1, source_target_pairs={{0,4},{1,5},{2,6},{3,7},{4,0},{5,1},{6,2},{7,3},{8,12},{9,13},{10,... | collective-permute-start | bytes 811016 | tf_op jit(solution)/shard_map/ppermute | solution.py:223
  161.4 14.2 %collective-permute-start.11 = (f16[4,33,8,128]{3,2,1,0:T(8,128)(2,1)S(1)}, f16[4,33,8,128]{3,2,1,0:T(8,128)(2,1)S(1)}, u32[]{:S(2)}, u32[]{:S(2)}) collective-permute-start(f16[4,33,8,128]{3,2,1,0:T(8,128)(2,1)S(1)} %collective-permute-done.10), channel_id=1, source_target_pairs={{0,4},{1,5},{2,6},{3,7},{4,0},{5,1},{6,2},{7,3},{8,12},{9,13},{10,... | collective-permute-start | bytes 811016 | tf_op jit(solution)/shard_map/ppermute | solution.py:223
  161.4 12.3 %collective-permute-start.6 = (f16[4,17,8,128]{3,2,1,0:T(8,128)(2,1)S(1)}, f16[4,17,8,128]{3,2,1,0:T(8,128)(2,1)S(1)}, u32[]{:S(2)}, u32[]{:S(2)}) collective-permute-start(f16[4,17,8,128]{3,2,1,0:T(8,128)(2,1)S(1)} %get-tuple-element.71), channel_id=1, source_target_pairs={{0,4},{1,5},{2,6},{3,7},{4,0},{5,1},{6,2},{7,3},{8,12},{9,13},{10,... | collective-permute-start | bytes 417800 | tf_op jit(solution)/shard_map/ppermute | solution.py:223
  163.9 11.7 %collective-permute-start.8 = (f16[4,17,8,128]{3,2,1,0:T(8,128)(2,1)S(1)}, f16[4,17,8,128]{3,2,1,0:T(8,128)(2,1)S(1)}, u32[]{:S(2)}, u32[]{:S(2)}) collective-permute-start(f16[4,17,8,128]{3,2,1,0:T(8,128)(2,1)S(1)} %collective-permute-done.7), channel_id=1, source_target_pairs={{0,4},{1,5},{2,6},{3,7},{4,0},{5,1},{6,2},{7,3},{8,12},{9,13},{10,... | collective-permute-start | bytes 417800 | tf_op jit(solution)/shard_map/ppermute | solution.py:223

commit v4 on v3

--- a/solution.py
+++ b/solution.py
@@ -11,7 +11,8 @@
 ITERS = 3
 LANES = 128
 SUBLANES = 8
-PLAN = ((32, "all", "staged"), (16, "all", "staged"), (16, "all", "all"),)
+TOP_SPACE = pltpu.HBM
+PLAN = ((16, "all", "staged"), (32, "all", "staged"), (16, "all", "all"),)
 epsilon = 1e-06
 
 
@@ -25,7 +26,7 @@
     return value.astype(jnp.bfloat16)
 
 
-def stack_kernel(sizes, top_ref, moved_ref, message_ref, matrix, rows32, data, data16, quad, normed, stack):
+def stack_kernel(sizes, top_hbm, moved_ref, message_ref, top_ref, top_sem, rows32, data, data16, quad, normed, stack):
     lag_groups, days_here, group, lags, n_src = sizes
     days = n_src // lag_groups * days_here
     width = lags // lag_groups
@@ -34,13 +35,11 @@
     pitch = tiles * days_here
     chunk = min(512, width)
 
+    fetch = pltpu.make_async_copy(top_hbm, top_ref, top_sem)
+
     @pl.when(pl.program_id(0) == 0)
     def _():
-        for a in range(lags // top_rows):
-            cut = a * top_rows
-            if cut:
-                matrix[cut:cut + top_rows, :cut] = top_ref[:, lags - cut:]
-            matrix[cut:cut + top_rows, cut:] = top_ref[:, :lags - cut]
+        fetch.start()
 
     here = pl.multiple_of(pl.program_id(0) * group * pitch, group * pitch)
     for s in range(n_src):
@@ -54,7 +53,14 @@
                 data[day, :, lane] = x
                 data16[day * group:(day + 1) * group, lane] = x.astype(jnp.bfloat16)
 
-    quad[...] = jnp.dot(data16[...], matrix[...], preferred_element_type=jnp.float32)
+    @pl.when(pl.program_id(0) == 0)
+    def _():
+        fetch.wait()
+
+    bands_of_matrix = [top_ref[...]]
+    for cut in range(top_rows, lags, top_rows):
+        bands_of_matrix.append(jnp.concatenate([top_ref[:, lags - cut:], top_ref[:, :lags - cut]], axis=1))
+    quad[...] = jnp.dot(data16[...], jnp.concatenate(bands_of_matrix, axis=0), preferred_element_type=jnp.float32)
 
     scale = []
     for day in range(days):
@@ -136,16 +142,17 @@
     cost = pl.CostEstimate(
         flops=2 * pairs * days * lags * lags, bytes_accessed=pairs * days * lags * 2, transcendentals=pairs * days * lags
     )
-    need = 2 * lags * lags + 10 * days * group * lags + 8 * group * lags + 2 * moved.size + 4 * top.size
+    need = 10 * days * group * lags + 8 * group * lags + 2 * moved.size + 4 * top.size
     need += 4 * repeats * lag_groups * tiles * SUBLANES * LANES
     return pl.pallas_call(
         functools.partial(stack_kernel, (lag_groups, days_here, group, lags, n_src)),
         grid=(pairs // group,),
-        in_specs=[pl.BlockSpec(top.shape, lambda i: (0, 0)), pl.BlockSpec(memory_space=pltpu.VMEM)],
+        in_specs=[pl.BlockSpec(memory_space=TOP_SPACE), pl.BlockSpec(memory_space=pltpu.VMEM)],
         out_specs=pl.BlockSpec(memory_space=pltpu.VMEM),
         out_shape=jax.ShapeDtypeStruct((repeats * lag_groups, tiles, SUBLANES, LANES), jnp.float32),
         scratch_shapes=[
-            pltpu.VMEM((lags, lags), jnp.bfloat16),
+            pltpu.VMEM(top.shape, top.dtype),
+            pltpu.SemaphoreType.DMA,
             pltpu.VMEM((group * pitch, LANES), jnp.float32),
             pltpu.VMEM((days, group, lags), jnp.float32),
             pltpu.VMEM((days * group, lags), jnp.bfloat16),
@@ -156,7 +163,7 @@
         cost_estimate=cost,
         compiler_params=pltpu.CompilerParams(vmem_limit_bytes=need + 6 * 2**20),
         name="stack_pairs",
-    )(top, moved)
+    )(pltpu.with_memory_space_constraint(top, pltpu.HBM), moved)
 
 
 def place_kernel(sizes, me_ref, *refs):
@@ -269,7 +276,7 @@
     moved, sent = [], []
 
     def work(k):
-        message = stack_pairs(moved[k], top, lag_groups, days_here, plan[k][0], 16 if plan[k][0] % 16 == 0 else 8, n,
+        message = stack_pairs(moved[k], top, lag_groups, days_here, plan[k][0], plan[k][0] if plan[k][0] <= 32 else (16 if plan[k][0] % 16 == 0 else 8), n,
                               1 if plan[k][2] == "staged" else day_groups)
         message = message.astype(jnp.float16)
         if plan[k][2] == "staged":

time: 182 us -> 181 us (level)
  blocking collectives: 30 us -> 0 us
  waiting for transfers between devices: 59.9 us -> 84.4 us
  starting transfers between devices: 36.8 us -> 43.9 us
  Pallas kernels: 32.2 us -> 29.8 us
    all_to_all x1 -> x0, blocking collectives: 30 us -> none  [per_device(): got = lax.all_to_all(rows, AXES, 0, 0, tiled=True)]
    all_to_all x2 -> x3, waiting for transfers between devices: 27.2 us -> 44.8 us  [per_device(): got = lax.all_to_all(rows, AXES, 0, 0, tiled=True)]
    all_to_all x2 -> x3, starting transfers between devices: 18.6 us -> 25.6 us  [per_device(): got = lax.all_to_all(rows, AXES, 0, 0, tiled=True)]
    ppermute x12, waiting for transfers between devices: 32.7 us -> 39.6 us  [swap(): return lax.ppermute(x, AXES, [(i, i ^ by) for i in range(n)])]
    pallas_call x3, Pallas kernels: 26.6 us -> 24.2 us  [stack_pairs(): pl.pallas_call(functools.partial(stack_kernel, (lag_groups, days_here, gr...]
    slice x2 -> x3, local copies, waits for them, and re-layouts: 7.24 us -> 8.78 us  [per_device(): rows = corr[starts[k] * n:(starts[k] + p) * n]]
  transfers between devices with their start and end apart: 15 -> 16, of which waited for: 8 -> 10; matrix products, arithmetic and copies ran while one was open for 8% -> 9% of each run, Pallas kernels for 14% -> 12%
where the time goes in v4:
time: 181 us; the launch traced here: 180 us
  waiting for transfers between devices  84.4 us (47%)
  starting transfers between devices  43.9 us (24%)
  Pallas kernels  29.8 us (16%)
  other arithmetic  11.8 us (7%)
  local copies, waits for them, and re-layouts  9.57 us (5%)
    all_to_all x3, waiting for transfers between devices, per_device(): got = lax.all_to_all(rows, AXES, 0, 0, tiled=True)  44.8 us
    ppermute x12, waiting for transfers between devices, swap(): return lax.ppermute(x, AXES, [(i, i ^ by) for i in range(n)])  39.6 us
    all_to_all x3, starting transfers between devices, per_device(): got = lax.all_to_all(rows, AXES, 0, 0, tiled=True)  25.6 us
    pallas_call x3, Pallas kernels, stack_pairs(): pl.pallas_call(functools.partial(stack_kernel, (lag_groups, days_here, gr...  24.2 us
    ppermute x12, starting transfers between devices, swap(): return lax.ppermute(x, AXES, [(i, i ^ by) for i in range(n)])  11.5 us
    convert_element_type x1, other arithmetic, kernel_rows(): return value.astype(jnp.bfloat16)  10.2 us
    slice x3, local copies, waits for them, and re-layouts, per_device(): rows = corr[starts[k] * n:(starts[k] + p) * n]  8.78 us
    all_to_all x1, starting transfers between devices, per_device(): turns = [((None,), (lax.all_to_all(sent[k], AXES, 0, 0, tiled=True),))]  6.79 us
  transfers between devices with their start and end apart: 16, of which 10 were waited for; matrix products, arithmetic and copies ran while one was open for 9% of the time, Pallas kernels for 12%

profile of v4, /device:TPU:0, one launch (start us, length us, event | category | flops | bytes accessed | tf_op | source)
XLA Modules:
  0.0 180.5 jit_solution(17322492468752021927)
XLA Ops:
  0.6 2.6 %slice.38 = bf16[256,4,512]{2,1,0:T(4,128)(2,1)} slice(bf16[1024,4,512]{2,1,0:T(4,128)(2,1)} %param.1), slice={[0:256], [0:4], [0:512]} | slice | bytes 2097152 | tf_op jit(solution)/shard_map/slice | solution.py:291
  3.2 7.4 %all-to-all-start = ((bf16[256,4,512]{2,1,0:T(4,128)(2,1)}), bf16[256,4,512]{2,1,0:T(4,128)(2,1)S(1)}, u32[]{:S(2)}, u32[]{:S(2)}) async-start(bf16[256,4,512]{2,1,0:T(4,128)(2,1)} %slice.38), calls=%async_computation | async-start | bytes 2097152 | tf_op jit(solution)/shard_map/all_to_all | solution.py:296
  10.6 10.2 %select_convert_fusion.top_hbm = bf16[256,2048]{1,0:T(8,128)(2,1)} fusion(), kind=kLoop, calls=%fused_computation.9 | loop fusion | flops 16252928 | bytes 1048576 | tf_op jit(solution)/shard_map/convert_element_type | solution.py:26
  20.8 3.6 %slice.37 = bf16[512,4,512]{2,1,0:T(4,128)(2,1)} slice(bf16[1024,4,512]{2,1,0:T(4,128)(2,1)} %param.1), slice={[256:768], [0:4], [0:512]} | slice | bytes 4194304 | tf_op jit(solution)/shard_map/slice | solution.py:291
  24.4 9.1 %all-to-all-done = bf16[256,4,512]{2,1,0:T(4,128)(2,1)S(1)} async-done(((bf16[256,4,512]{2,1,0:T(4,128)(2,1)}), bf16[256,4,512]{2,1,0:T(4,128)(2,1)S(1)}, u32[]{:S(2)}, u32[]{:S(2)}) %all-to-all-start) | async-done | bytes 1048608 | tf_op jit(solution)/shard_map/all_to_all | solution.py:296
  33.5 6.8 %all-to-all-start.1 = ((bf16[512,4,512]{2,1,0:T(4,128)(2,1)}), bf16[512,4,512]{2,1,0:T(4,128)(2,1)S(1)}, u32[]{:S(2)}, u32[]{:S(2)}) async-start(bf16[512,4,512]{2,1,0:T(4,128)(2,1)} %slice.37), calls=%async_computation.1 | async-start | bytes 4194304 | tf_op jit(solution)/shard_map/all_to_all | solution.py:296
  40.4 6.1 %stack_pairs.3 = f32[4,17,8,128]{3,2,1,0:T(8,128)S(1)} custom-call(bf16[256,2048]{1,0:T(8,128)(2,1)} %select_convert_fusion.top_hbm, bf16[16,256,128]{2,1,0:T(8,128)(2,1)S(1)} %bitcast.69), custom_call_target="tpu_custom_call" | custom-call | flops 2147483648 | bytes 1048576 | tf_op jit(solution)/shard_map/stack_pairs/pallas_call | solution.py:147
  46.6 1.9 %collective-permute-start.1 = (f16[17,8,128]{2,1,0:T(8,128)(2,1)S(1)}, f16[17,8,128]{2,1,0:T(8,128)(2,1)S(1)}, u32[]{:S(2)}, u32[]{:S(2)}) collective-permute-start(f16[17,8,128]{2,1,0:T(8,128)(2,1)S(1)} %get-tuple-element.55), channel_id=1, source_target_pairs={{0,2},{1,3},{2,0},{3,1},{4,6},{5,7},{6,4},{7,5},{8,10},{9,11},{10,... | collective-permute-start | bytes 104456 | tf_op jit(solution)/shard_map/ppermute | solution.py:230
  48.8 2.6 %slice.36 = bf16[256,4,512]{2,1,0:T(4,128)(2,1)} slice(bf16[1024,4,512]{2,1,0:T(4,128)(2,1)} %param.1), slice={[768:1024], [0:4], [0:512]} | slice | bytes 2097152 | tf_op jit(solution)/shard_map/slice | solution.py:291
  51.3 5.1 %collective-permute-done.1 = f16[17,8,128]{2,1,0:T(8,128)(2,1)S(1)} collective-permute-done((f16[17,8,128]{2,1,0:T(8,128)(2,1)S(1)}, f16[17,8,128]{2,1,0:T(8,128)(2,1)S(1)}, u32[]{:S(2)}, u32[]{:S(2)}) %collective-permute-start.1) | collective-permute-done | bytes 34848 | tf_op jit(solution)/shard_map/ppermute | solution.py:230
  56.5 24.8 %all-to-all-done.1 = bf16[512,4,512]{2,1,0:T(4,128)(2,1)S(1)} async-done(((bf16[512,4,512]{2,1,0:T(4,128)(2,1)}), bf16[512,4,512]{2,1,0:T(4,128)(2,1)S(1)}, u32[]{:S(2)}, u32[]{:S(2)}) %all-to-all-start.1) | async-done | bytes 2097184 | tf_op jit(solution)/shard_map/all_to_all | solution.py:296
  81.3 11.4 %all-to-all-start.2 = ((bf16[256,4,512]{2,1,0:T(4,128)(2,1)}), bf16[256,4,512]{2,1,0:T(4,128)(2,1)S(1)}, u32[]{:S(2)}, u32[]{:S(2)}) async-start(bf16[256,4,512]{2,1,0:T(4,128)(2,1)} %slice.36), calls=%async_computation.2 | async-start | bytes 2097152 | tf_op jit(solution)/shard_map/all_to_all | solution.py:296
  92.7 11.7 %stack_pairs.5 = f32[4,33,8,128]{3,2,1,0:T(8,128)S(1)} custom-call(bf16[256,2048]{1,0:T(8,128)(2,1)} %select_convert_fusion.top_hbm, bf16[16,512,128]{2,1,0:T(8,128)(2,1)S(1)} %bitcast.68), custom_call_target="tpu_custom_call" | custom-call | flops 4294967296 | bytes 2097152 | tf_op jit(solution)/shard_map/stack_pairs/pallas_call | solution.py:147
  104.5 11.0 %all-to-all-done.2 = bf16[256,4,512]{2,1,0:T(4,128)(2,1)S(1)} async-done(((bf16[256,4,512]{2,1,0:T(4,128)(2,1)}), bf16[256,4,512]{2,1,0:T(4,128)(2,1)S(1)}, u32[]{:S(2)}, u32[]{:S(2)}) %all-to-all-start.2) | async-done | bytes 1048608 | tf_op jit(solution)/shard_map/all_to_all | solution.py:296
  115.4 6.4 %stack_pairs.4 = f32[16,17,8,128]{3,2,1,0:T(8,128)S(1)} custom-call(bf16[256,2048]{1,0:T(8,128)(2,1)} %select_convert_fusion.top_hbm, bf16[16,256,128]{2,1,0:T(8,128)(2,1)S(1)} %bitcast.70), custom_call_target="tpu_custom_call" | custom-call | flops 2147483648 | bytes 1048576 | tf_op jit(solution)/shard_map/stack_pairs/pallas_call | solution.py:147
  122.7 6.8 %all-to-all-start.3 = ((f16[16,17,8,128]{3,2,1,0:T(8,128)(2,1)}), f16[16,17,8,128]{3,2,1,0:T(8,128)(2,1)S(1)}, u32[]{:S(2)}, u32[]{:S(2)}) async-start(f16[16,17,8,128]{3,2,1,0:T(8,128)(2,1)} %convert_element_type.45), calls=%async_computation.3 | async-start | bytes 1114112 | tf_op jit(solution)/shard_map/all_to_all | solution.py:305
  129.6 2.0 %collective-permute-start.4 = (f16[33,8,128]{2,1,0:T(8,128)(2,1)S(1)}, f16[33,8,128]{2,1,0:T(8,128)(2,1)S(1)}, u32[]{:S(2)}, u32[]{:S(2)}) collective-permute-start(f16[33,8,128]{2,1,0:T(8,128)(2,1)S(1)} %get-tuple-element.52), channel_id=1, source_target_pairs={{0,2},{1,3},{2,0},{3,1},{4,6},{5,7},{6,4},{7,5},{8,10},{9,11},{10,... | collective-permute-start | bytes 202760 | tf_op jit(solution)/shard_map/ppermute | solution.py:230
  131.8 6.5 %collective-permute-done.4 = f16[33,8,128]{2,1,0:T(8,128)(2,1)S(1)} collective-permute-done((f16[33,8,128]{2,1,0:T(8,128)(2,1)S(1)}, f16[33,8,128]{2,1,0:T(8,128)(2,1)S(1)}, u32[]{:S(2)}, u32[]{:S(2)}) %collective-permute-start.4) | collective-permute-done | bytes 67616 | tf_op jit(solution)/shard_map/ppermute | solution.py:230
  139.0 2.5 %collective-permute-start.7 = (f16[4,33,8,128]{3,2,1,0:T(8,128)(2,1)S(1)}, f16[4,33,8,128]{3,2,1,0:T(8,128)(2,1)S(1)}, u32[]{:S(2)}, u32[]{:S(2)}) collective-permute-start(f16[4,33,8,128]{3,2,1,0:T(8,128)(2,1)S(1)} %get-tuple-element.63), channel_id=1, source_target_pairs={{0,8},{1,9},{2,10},{3,11},{4,12},{5,13},{6,14},{7,15},{8,0},{9,1},... | collective-permute-start | bytes 811016 | tf_op jit(solution)/shard_map/ppermute | solution.py:230
  142.0 2.1 %collective-permute-start.6 = (f16[4,33,8,128]{3,2,1,0:T(8,128)(2,1)S(1)}, f16[4,33,8,128]{3,2,1,0:T(8,128)(2,1)S(1)}, u32[]{:S(2)}, u32[]{:S(2)}) collective-permute-start(f16[4,33,8,128]{3,2,1,0:T(8,128)(2,1)S(1)} %get-tuple-element.63), channel_id=1, source_target_pairs={{0,4},{1,5},{2,6},{3,7},{4,0},{5,1},{6,2},{7,3},{8,12},{9,13},{10,... | collective-permute-start | bytes 811016 | tf_op jit(solution)/shard_map/ppermute | solution.py:230
  144.1 16.5 %collective-permute-done.7 = f16[4,33,8,128]{3,2,1,0:T(8,128)(2,1)S(1)} collective-permute-done((f16[4,33,8,128]{3,2,1,0:T(8,128)(2,1)S(1)}, f16[4,33,8,128]{3,2,1,0:T(8,128)(2,1)S(1)}, u32[]{:S(2)}, u32[]{:S(2)}) %collective-permute-start.7) | collective-permute-done | bytes 270368 | tf_op jit(solution)/shard_map/ppermute | solution.py:230
  160.6 2.0 %collective-permute-start.9 = (f16[4,17,8,128]{3,2,1,0:T(8,128)(2,1)S(1)}, f16[4,17,8,128]{3,2,1,0:T(8,128)(2,1)S(1)}, u32[]{:S(2)}, u32[]{:S(2)}) collective-permute-start(f16[4,17,8,128]{3,2,1,0:T(8,128)(2,1)S(1)} %pad_maximum_fusion.1), channel_id=1, source_target_pairs={{0,4},{1,5},{2,6},{3,7},{4,0},{5,1},{6,2},{7,3},{8,12},{9,13},{10,... | collective-permute-start | bytes 417800 | tf_op jit(solution)/shard_map/ppermute | solution.py:230
  164.2 8.8 %collective-permute-done.9 = f16[4,17,8,128]{3,2,1,0:T(8,128)(2,1)S(1)} collective-permute-done((f16[4,17,8,128]{3,2,1,0:T(8,128)(2,1)S(1)}, f16[4,17,8,128]{3,2,1,0:T(8,128)(2,1)S(1)}, u32[]{:S(2)}, u32[]{:S(2)}) %collective-permute-start.9) | collective-permute-done | bytes 139296 | tf_op jit(solution)/shard_map/ppermute | solution.py:230
  173.0 1.8 %collective-permute-done.11 = f16[4,17,8,128]{3,2,1,0:T(8,128)(2,1)S(1)} collective-permute-done((f16[4,17,8,128]{3,2,1,0:T(8,128)(2,1)S(1)}, f16[4,17,8,128]{3,2,1,0:T(8,128)(2,1)S(1)}, u32[]{:S(2)}, u32[]{:S(2)}) %collective-permute-start.11) | collective-permute-done | bytes 139296 | tf_op jit(solution)/shard_map/ppermute | solution.py:230
  (38 shorter events, 10.0 us)
Async XLA Ops:
  3.2 30.3 %all-to-all-start = ((bf16[256,4,512]{2,1,0:T(4,128)(2,1)}), bf16[256,4,512]{2,1,0:T(4,128)(2,1)S(1)}, u32[]{:S(2)}, u32[]{:S(2)}) async-start(bf16[256,4,512]{2,1,0:T(4,128)(2,1)} %slice.38), calls=%async_computation | async-start | bytes 2097152 | tf_op jit(solution)/shard_map/all_to_all | solution.py:296
  33.5 47.8 %all-to-all-start.1 = ((bf16[512,4,512]{2,1,0:T(4,128)(2,1)}), bf16[512,4,512]{2,1,0:T(4,128)(2,1)S(1)}, u32[]{:S(2)}, u32[]{:S(2)}) async-start(bf16[512,4,512]{2,1,0:T(4,128)(2,1)} %slice.37), calls=%async_computation.1 | async-start | bytes 4194304 | tf_op jit(solution)/shard_map/all_to_all | solution.py:296
  46.6 9.8 %collective-permute-start.1 = (f16[17,8,128]{2,1,0:T(8,128)(2,1)S(1)}, f16[17,8,128]{2,1,0:T(8,128)(2,1)S(1)}, u32[]{:S(2)}, u32[]{:S(2)}) collective-permute-start(f16[17,8,128]{2,1,0:T(8,128)(2,1)S(1)} %get-tuple-element.55), channel_id=1, source_target_pairs={{0,2},{1,3},{2,0},{3,1},{4,6},{5,7},{6,4},{7,5},{8,10},{9,11},{10,... | collective-permute-start | bytes 104456 | tf_op jit(solution)/shard_map/ppermute | solution.py:230
  48.5 7.9 %collective-permute-start.2 = (f16[17,8,128]{2,1,0:T(8,128)(2,1)S(1)}, f16[17,8,128]{2,1,0:T(8,128)(2,1)S(1)}, u32[]{:S(2)}, u32[]{:S(2)}) collective-permute-start(f16[17,8,128]{2,1,0:T(8,128)(2,1)S(1)} %get-tuple-element.70), channel_id=1, source_target_pairs={{0,1},{1,0},{2,3},{3,2},{4,5},{5,4},{6,7},{7,6},{8,9},{9,8},{10,11... | collective-permute-start | bytes 104456 | tf_op jit(solution)/shard_map/ppermute | solution.py:230
  48.5 7.9 %collective-permute-start = (f16[17,8,128]{2,1,0:T(8,128)(2,1)S(1)}, f16[17,8,128]{2,1,0:T(8,128)(2,1)S(1)}, u32[]{:S(2)}, u32[]{:S(2)}) collective-permute-start(f16[17,8,128]{2,1,0:T(8,128)(2,1)S(1)} %get-tuple-element.71), channel_id=1, source_target_pairs={{0,3},{1,2},{2,1},{3,0},{4,7},{5,6},{6,5},{7,4},{8,11},{9,10},{10,... | collective-permute-start | bytes 104456 | tf_op jit(solution)/shard_map/ppermute | solution.py:230
  81.3 34.2 %all-to-all-start.2 = ((bf16[256,4,512]{2,1,0:T(4,128)(2,1)}), bf16[256,4,512]{2,1,0:T(4,128)(2,1)S(1)}, u32[]{:S(2)}, u32[]{:S(2)}) async-start(bf16[256,4,512]{2,1,0:T(4,128)(2,1)} %slice.36), calls=%async_computation.2 | async-start | bytes 2097152 | tf_op jit(solution)/shard_map/all_to_all | solution.py:296
  122.7 55.7 %all-to-all-start.3 = ((f16[16,17,8,128]{3,2,1,0:T(8,128)(2,1)}), f16[16,17,8,128]{3,2,1,0:T(8,128)(2,1)S(1)}, u32[]{:S(2)}, u32[]{:S(2)}) async-start(f16[16,17,8,128]{3,2,1,0:T(8,128)(2,1)} %convert_element_type.45), calls=%async_computation.3 | async-start | bytes 1114112 | tf_op jit(solution)/shard_map/all_to_all | solution.py:305
  129.6 8.7 %collective-permute-start.4 = (f16[33,8,128]{2,1,0:T(8,128)(2,1)S(1)}, f16[33,8,128]{2,1,0:T(8,128)(2,1)S(1)}, u32[]{:S(2)}, u32[]{:S(2)}) collective-permute-start(f16[33,8,128]{2,1,0:T(8,128)(2,1)S(1)} %get-tuple-element.52), channel_id=1, source_target_pairs={{0,2},{1,3},{2,0},{3,1},{4,6},{5,7},{6,4},{7,5},{8,10},{9,11},{10,... | collective-permute-start | bytes 202760 | tf_op jit(solution)/shard_map/ppermute | solution.py:230
  131.6 6.8 %collective-permute-start.5 = (f16[33,8,128]{2,1,0:T(8,128)(2,1)S(1)}, f16[33,8,128]{2,1,0:T(8,128)(2,1)S(1)}, u32[]{:S(2)}, u32[]{:S(2)}) collective-permute-start(f16[33,8,128]{2,1,0:T(8,128)(2,1)S(1)} %get-tuple-element.64), channel_id=1, source_target_pairs={{0,1},{1,0},{2,3},{3,2},{4,5},{5,4},{6,7},{7,6},{8,9},{9,8},{10,11... | collective-permute-start | bytes 202760 | tf_op jit(solution)/shard_map/ppermute | solution.py:230
  131.6 7.2 %collective-permute-start.3 = (f16[33,8,128]{2,1,0:T(8,128)(2,1)S(1)}, f16[33,8,128]{2,1,0:T(8,128)(2,1)S(1)}, u32[]{:S(2)}, u32[]{:S(2)}) collective-permute-start(f16[33,8,128]{2,1,0:T(8,128)(2,1)S(1)} %get-tuple-element.65), channel_id=1, source_target_pairs={{0,3},{1,2},{2,1},{3,0},{4,7},{5,6},{6,5},{7,4},{8,11},{9,10},{10,... | collective-permute-start | bytes 202760 | tf_op jit(solution)/shard_map/ppermute | solution.py:230
  139.0 21.6 %collective-permute-start.7 = (f16[4,33,8,128]{3,2,1,0:T(8,128)(2,1)S(1)}, f16[4,33,8,128]{3,2,1,0:T(8,128)(2,1)S(1)}, u32[]{:S(2)}, u32[]{:S(2)}) collective-permute-start(f16[4,33,8,128]{3,2,1,0:T(8,128)(2,1)S(1)} %get-tuple-element.63), channel_id=1, source_target_pairs={{0,8},{1,9},{2,10},{3,11},{4,12},{5,13},{6,14},{7,15},{8,0},{9,1},... | collective-permute-start | bytes 811016 | tf_op jit(solution)/shard_map/ppermute | solution.py:230
  141.5 21.6 %collective-permute-start.10 = (f16[4,17,8,128]{3,2,1,0:T(8,128)(2,1)S(1)}, f16[4,17,8,128]{3,2,1,0:T(8,128)(2,1)S(1)}, u32[]{:S(2)}, u32[]{:S(2)}) collective-permute-start(f16[4,17,8,128]{3,2,1,0:T(8,128)(2,1)S(1)} %pad_maximum_fusion.1), channel_id=1, source_target_pairs={{0,8},{1,9},{2,10},{3,11},{4,12},{5,13},{6,14},{7,15},{8,0},{9,1},... | collective-permute-start | bytes 417800 | tf_op jit(solution)/shard_map/ppermute | solution.py:230
  142.0 33.9 %collective-permute-start.6 = (f16[4,33,8,128]{3,2,1,0:T(8,128)(2,1)S(1)}, f16[4,33,8,128]{3,2,1,0:T(8,128)(2,1)S(1)}, u32[]{:S(2)}, u32[]{:S(2)}) collective-permute-start(f16[4,33,8,128]{3,2,1,0:T(8,128)(2,1)S(1)} %get-tuple-element.63), channel_id=1, source_target_pairs={{0,4},{1,5},{2,6},{3,7},{4,0},{5,1},{6,2},{7,3},{8,12},{9,13},{10,... | collective-permute-start | bytes 811016 | tf_op jit(solution)/shard_map/ppermute | solution.py:230
  160.6 16.5 %collective-permute-start.8 = (f16[4,33,8,128]{3,2,1,0:T(8,128)(2,1)S(1)}, f16[4,33,8,128]{3,2,1,0:T(8,128)(2,1)S(1)}, u32[]{:S(2)}, u32[]{:S(2)}) collective-permute-start(f16[4,33,8,128]{3,2,1,0:T(8,128)(2,1)S(1)} %collective-permute-done.7), channel_id=1, source_target_pairs={{0,4},{1,5},{2,6},{3,7},{4,0},{5,1},{6,2},{7,3},{8,12},{9,13},{10,... | collective-permute-start | bytes 811016 | tf_op jit(solution)/shard_map/ppermute | solution.py:230
  160.6 12.3 %collective-permute-start.9 = (f16[4,17,8,128]{3,2,1,0:T(8,128)(2,1)S(1)}, f16[4,17,8,128]{3,2,1,0:T(8,128)(2,1)S(1)}, u32[]{:S(2)}, u32[]{:S(2)}) collective-permute-start(f16[4,17,8,128]{3,2,1,0:T(8,128)(2,1)S(1)} %pad_maximum_fusion.1), channel_id=1, source_target_pairs={{0,4},{1,5},{2,6},{3,7},{4,0},{5,1},{6,2},{7,3},{8,12},{9,13},{10,... | collective-permute-start | bytes 417800 | tf_op jit(solution)/shard_map/ppermute | solution.py:230
  163.1 11.7 %collective-permute-start.11 = (f16[4,17,8,128]{3,2,1,0:T(8,128)(2,1)S(1)}, f16[4,17,8,128]{3,2,1,0:T(8,128)(2,1)S(1)}, u32[]{:S(2)}, u32[]{:S(2)}) collective-permute-start(f16[4,17,8,128]{3,2,1,0:T(8,128)(2,1)S(1)} %collective-permute-done.10), channel_id=1, source_target_pairs={{0,4},{1,5},{2,6},{3,7},{4,0},{5,1},{6,2},{7,3},{8,12},{9,13},{10,... | collective-permute-start | bytes 417800 | tf_op jit(solution)/shard_map/ppermute | solution.py:230

commit v5 on v4

--- a/solution.py
+++ b/solution.py
@@ -12,7 +12,7 @@
 LANES = 128
 SUBLANES = 8
 TOP_SPACE = pltpu.HBM
-PLAN = ((16, "all", "staged"), (32, "all", "staged"), (16, "all", "all"),)
+PLAN = ((32, "all", "staged"), (16, "swap", "staged"), (16, "all", "all"))
 epsilon = 1e-06
 
 
@@ -26,8 +26,10 @@
     return value.astype(jnp.bfloat16)
 
 
-def stack_kernel(sizes, top_hbm, moved_ref, message_ref, top_ref, top_sem, rows32, data, data16, quad, normed, stack):
+def stack_kernel(sizes, me_ref, top_hbm, *refs):
     lag_groups, days_here, group, lags, n_src = sizes
+    ins = refs[:-9]
+    message_ref, top_ref, top_sem, rows32, data, data16, quad, normed, stack = refs[-9:]
     days = n_src // lag_groups * days_here
     width = lags // lag_groups
     tiles = width // LANES
@@ -43,15 +45,21 @@
 
     here = pl.multiple_of(pl.program_id(0) * group * pitch, group * pitch)
     for s in range(n_src):
-        block, part = divmod(s, lag_groups)
-        rows32[...] = moved_ref[s, pl.ds(here, group * pitch), :].astype(jnp.float32)
+        if len(ins) == 1:
+            rows32[...] = ins[0][s, pl.ds(here, group * pitch), :].astype(jnp.float32)
+            block, part = divmod(s, lag_groups)
+        else:
+            rows32[...] = ins[s][pl.ds(here, group * pitch), :].astype(jnp.float32)
+            source = me_ref[0] ^ s
+            block, part = source // lag_groups, source % lag_groups
         for d in range(days_here):
             day = block * days_here + d
+            row = pl.multiple_of(day * group, group)
             for t in range(tiles):
-                lane = slice(part * width + t * LANES, part * width + (t + 1) * LANES)
+                lane = pl.ds(pl.multiple_of(part * width + t * LANES, LANES), LANES)
                 x = rows32[pl.ds(t * days_here + d, group, stride=pitch), :]
                 data[day, :, lane] = x
-                data16[day * group:(day + 1) * group, lane] = x.astype(jnp.bfloat16)
+                data16[pl.ds(row, group), lane] = x.astype(jnp.bfloat16)
 
     @pl.when(pl.program_id(0) == 0)
     def _():
@@ -132,7 +140,7 @@
                         side[r * SUBLANES:(r + 1) * SUBLANES])
 
 
-def stack_pairs(moved, top, lag_groups, days_here, pairs, group, n_src, repeats):
+def stack_pairs(me, moved, top, lag_groups, days_here, pairs, group, n_src, repeats):
     lags = top.shape[1]
     days = n_src // lag_groups * days_here
     width = lags // lag_groups
@@ -142,12 +150,13 @@
     cost = pl.CostEstimate(
         flops=2 * pairs * days * lags * lags, bytes_accessed=pairs * days * lags * 2, transcendentals=pairs * days * lags
     )
-    need = 10 * days * group * lags + 8 * group * lags + 2 * moved.size + 4 * top.size
+    need = 10 * days * group * lags + 8 * group * lags + 2 * sum(m.size for m in moved) + 4 * top.size
     need += 4 * repeats * lag_groups * tiles * SUBLANES * LANES
     return pl.pallas_call(
         functools.partial(stack_kernel, (lag_groups, days_here, group, lags, n_src)),
         grid=(pairs // group,),
-        in_specs=[pl.BlockSpec(memory_space=TOP_SPACE), pl.BlockSpec(memory_space=pltpu.VMEM)],
+        in_specs=[pl.BlockSpec(memory_space=pltpu.SMEM), pl.BlockSpec(memory_space=TOP_SPACE)]
+        + [pl.BlockSpec(memory_space=pltpu.VMEM)] * len(moved),
         out_specs=pl.BlockSpec(memory_space=pltpu.VMEM),
         out_shape=jax.ShapeDtypeStruct((repeats * lag_groups, tiles, SUBLANES, LANES), jnp.float32),
         scratch_shapes=[
@@ -163,7 +172,7 @@
         cost_estimate=cost,
         compiler_params=pltpu.CompilerParams(vmem_limit_bytes=need + 6 * 2**20),
         name="stack_pairs",
-    )(pltpu.with_memory_space_constraint(top, pltpu.HBM), moved)
+    )(me.reshape(1), pltpu.with_memory_space_constraint(top, pltpu.HBM), *moved)
 
 
 def place_kernel(sizes, me_ref, *refs):
@@ -276,25 +285,26 @@
     moved, sent = [], []
 
     def work(k):
-        message = stack_pairs(moved[k], top, lag_groups, days_here, plan[k][0], plan[k][0] if plan[k][0] <= 32 else (16 if plan[k][0] % 16 == 0 else 8), n,
+        message = stack_pairs(me, moved[k], top, lag_groups, days_here, plan[k][0], plan[k][0] if plan[k][0] <= 32 else (16 if plan[k][0] % 16 == 0 else 8), n,
                               1 if plan[k][2] == "staged" else day_groups)
         message = message.astype(jnp.float16)
         if plan[k][2] == "staged":
             message = spread_lags(message, me, lag_groups, n)
         sent.append(message)
 
-    for k, (p, _, _) in enumerate(plan):
-        if k >= 2:
-            work(k - 2)
+    for k, (p, how, _) in enumerate(plan):
         if k == 1:
             corr, top = lax.optimization_barrier((corr, top))
         rows = corr[starts[k] * n:(starts[k] + p) * n]
+        if how == "swap":
+            pieces = [lax.dynamic_slice_in_dim(rows, (me ^ s) * p, p, 0) for s in range(n)]
+            pieces = [pieces[0]] + [swap(pieces[s], n, s) for s in range(1, n)]
+            moved.append([flat(piece, ()) for piece in pieces])
+            continue
         if k >= 1:
-            rows, moved[k - 1] = lax.optimization_barrier((rows, moved[k - 1]))
-        if k >= 2:
-            rows, sent[k - 2] = lax.optimization_barrier((rows, sent[k - 2]))
+            rows, moved[0] = lax.optimization_barrier((rows, moved[0]))
         got = lax.all_to_all(rows, AXES, 0, 0, tiled=True)
-        moved.append(flat(got.reshape(n, p, days_here, width), (n,)))
+        moved.append([flat(got.reshape(n, p, days_here, width), (n,))])
     for k in range(len(sent), len(plan)):
         work(k)
     shapes = ((pairs, width), (pairs, width), (pairs, LANES))
@@ -305,14 +315,11 @@
             turns = [((None,), (lax.all_to_all(sent[k], AXES, 0, 0, tiled=True),))]
         else:
             moves, blocks = spread_days(sent[k], lag_groups, n)
-            turns = [(moves[:2], blocks[:2]), (moves[2:], blocks[2:])]
+            turns = [(moves[:3], blocks[:3]), (moves[3:], blocks[3:])]
         todo.append((k, turns))
     turns_of = {k: list(turns) for k, turns in todo}
     last = len(plan) - 1
-    sequence = [(k, 0) for k in range(last - 1)]
-    if last:
-        sequence += [(k, 1) for k in range(last - 1)] + [(last - 1, 0), (last - 1, 1)]
-    sequence.append((last, 0))
+    sequence = [(k, 0) for k in range(last)] + [(k, 1) for k in range(last)] + [(last, 0)]
     for k, turn in sequence:
         moves, blocks = turns_of[k][turn]
         outs = place(outs, blocks, moves, me, shapes, starts[k] * n, plan[k][0], lag_groups, days, days_here)

time: 181 us -> 210 us (1.16)
  starting transfers between devices: 43.9 us -> 65.1 us
  local copies, waits for them, and re-layouts: 9.57 us -> 17.7 us
    ppermute x12 -> x27, starting transfers between devices: 11.5 us -> 42.4 us  [swap(): return lax.ppermute(x, AXES, [(i, i ^ by) for i in range(n)])]
    all_to_all x3 -> x2, waiting for transfers between devices: 44.8 us -> 27.2 us  [per_device(): got = lax.all_to_all(rows, AXES, 0, 0, tiled=True)]
    ppermute x12 -> x27, waiting for transfers between devices: 39.6 us -> 55.5 us  [swap(): return lax.ppermute(x, AXES, [(i, i ^ by) for i in range(n)])]
    unnamed x1 -> x21, local copies, waits for them, and re-layouts: 0.79 us -> 8.08 us
    all_to_all x3 -> x2, starting transfers between devices: 25.6 us -> 18.8 us  [per_device(): got = lax.all_to_all(rows, AXES, 0, 0, tiled=True)]
    all_to_all x1, starting transfers between devices: 6.79 us -> 3.84 us  [per_device(): turns = [((None,), (lax.all_to_all(sent[k], AXES, 0, 0, tiled=True),))]]
    dynamic_slice x0 -> x1, local copies, waits for them, and re-layouts: none -> 2.43 us  [per_device(): lax.dynamic_slice_in_dim(rows, (me ^ s) * p, p, 0)]
    slice x3 -> x2, local copies, waits for them, and re-layouts: 8.78 us -> 7.23 us  [per_device(): rows = corr[starts[k] * n:(starts[k] + p) * n]]
  transfers between devices with their start and end apart: 16 -> 30, of which waited for: 10 -> 10; matrix products, arithmetic and copies ran while one was open for 9% -> 9% of each run, Pallas kernels for 12% -> 14%
where the time goes in v5:
time: 210 us; the launch traced here: 209 us
  waiting for transfers between devices  82.7 us (39%)
  starting transfers between devices  65.1 us (31%)
  Pallas kernels  30.7 us (15%)
  local copies, waits for them, and re-layouts  17.7 us (8%)
  other arithmetic  11.8 us (6%)
    ppermute x27, waiting for transfers between devices, swap(): return lax.ppermute(x, AXES, [(i, i ^ by) for i in range(n)])  55.5 us
    ppermute x27, starting transfers between devices, swap(): return lax.ppermute(x, AXES, [(i, i ^ by) for i in range(n)])  42.4 us
    all_to_all x2, waiting for transfers between devices, per_device(): got = lax.all_to_all(rows, AXES, 0, 0, tiled=True)  27.2 us
    pallas_call x3, Pallas kernels, stack_pairs(): pl.pallas_call(functools.partial(stack_kernel, (lag_groups, days_here, gr...  25.1 us
    all_to_all x2, starting transfers between devices, per_device(): got = lax.all_to_all(rows, AXES, 0, 0, tiled=True)  18.8 us
    convert_element_type x1, other arithmetic, kernel_rows(): return value.astype(jnp.bfloat16)  10.2 us
    unnamed x21, local copies, waits for them, and re-layouts  8.08 us
    slice x2, local copies, waits for them, and re-layouts, per_device(): rows = corr[starts[k] * n:(starts[k] + p) * n]  7.23 us
  transfers between devices with their start and end apart: 30, of which 10 were waited for; matrix products, arithmetic and copies ran while one was open for 9% of the time, Pallas kernels for 14%

profile of v5, /device:TPU:0, one launch (start us, length us, event | category | flops | bytes accessed | tf_op | source)
XLA Modules:
  0.0 209.0 jit_solution(6010636804516714204)
XLA Ops:
  0.6 3.6 %slice.37 = bf16[512,4,512]{2,1,0:T(4,128)(2,1)} slice(bf16[1024,4,512]{2,1,0:T(4,128)(2,1)} %param.1), slice={[0:512], [0:4], [0:512]} | slice | bytes 4194304 | tf_op jit(solution)/shard_map/slice | solution.py:298
  4.3 7.4 %all-to-all-start = ((bf16[512,4,512]{2,1,0:T(4,128)(2,1)}), bf16[512,4,512]{2,1,0:T(4,128)(2,1)S(1)}, u32[]{:S(2)}, u32[]{:S(2)}) async-start(bf16[512,4,512]{2,1,0:T(4,128)(2,1)} %slice.37), calls=%async_computation | async-start | bytes 4194304 | tf_op jit(solution)/shard_map/all_to_all | solution.py:306
  11.7 10.2 %select_convert_fusion.top_hbm = bf16[256,2048]{1,0:T(8,128)(2,1)} fusion(), kind=kLoop, calls=%fused_computation.9 | loop fusion | flops 16252928 | bytes 1048576 | tf_op jit(solution)/shard_map/convert_element_type | solution.py:26
  21.8 3.6 %fusion.9 = (bf16[256,4,512]{2,1,0:T(4,128)(2,1)}, bf16[256,4,512]{2,1,0:T(4,128)(2,1)}) fusion(bf16[1024,4,512]{2,1,0:T(4,128)(2,1)} %param.1), kind=kLoop, calls=%fused_computation.66 | loop fusion | bytes 4194304 | tf_op jit(solution)/shard_map/slice | solution.py:298
  25.4 27.2 %all-to-all-done = bf16[512,4,512]{2,1,0:T(4,128)(2,1)S(1)} async-done(((bf16[512,4,512]{2,1,0:T(4,128)(2,1)}), bf16[512,4,512]{2,1,0:T(4,128)(2,1)S(1)}, u32[]{:S(2)}, u32[]{:S(2)}) %all-to-all-start) | async-done | bytes 2097184 | tf_op jit(solution)/shard_map/all_to_all | solution.py:306
  52.7 11.4 %all-to-all-start.1 = ((bf16[256,4,512]{2,1,0:T(4,128)(2,1)}), bf16[256,4,512]{2,1,0:T(4,128)(2,1)S(1)}, u32[]{:S(2)}, u32[]{:S(2)}) async-start(bf16[256,4,512]{2,1,0:T(4,128)(2,1)} %get-tuple-element.24), calls=%async_computation.1 | async-start | bytes 2097152 | tf_op jit(solution)/shard_map/all_to_all | solution.py:306
  64.1 2.4 %constant_dynamic-slice_fusion = (bf16[16,4,512]{2,1,0:T(4,128)(2,1)S(1)}, bf16[16,4,512]{2,1,0:T(4,128)(2,1)S(1)}, bf16[16,4,512]{2,1,0:T(4,128)(2,1)S(1)}, bf1...) fusion(bf16[256,4,512]{2,1,0:T(4,128)(2,1)} %get-tuple-element., ...), kind=kLoop, calls=%fused_computation.48 | loop fusion | bytes 2097216 | tf_op jit(solution)/shard_map/dynamic_slice | solution.py:300
  66.6 4.1 %collective-permute-start.14 = (bf16[16,4,512]{2,1,0:T(4,128)(2,1)S(1)}, bf16[16,4,512]{2,1,0:T(4,128)(2,1)S(1)}, u32[]{:S(2)}, u32[]{:S(2)}) collective-permute-start(bf16[16,4,512]{2,1,0:T(4,128)(2,1)S(1)} %get-tuple-element.52), channel_id=1, source_target_pairs={{0,15},{1,14},{2,13},{3,12},{4,11},{5,10},{6,9},{7,8},{8,7},{9,6},... | collective-permute-start | bytes 196616 | tf_op jit(solution)/shard_map/ppermute | solution.py:239
  71.1 3.2 %collective-permute-start.12 = (bf16[16,4,512]{2,1,0:T(4,128)(2,1)S(1)}, bf16[16,4,512]{2,1,0:T(4,128)(2,1)S(1)}, u32[]{:S(2)}, u32[]{:S(2)}) collective-permute-start(bf16[16,4,512]{2,1,0:T(4,128)(2,1)S(1)} %get-tuple-element.54), channel_id=1, source_target_pairs={{0,13},{1,12},{2,15},{3,14},{4,9},{5,8},{6,11},{7,10},{8,5},{9,4},... | collective-permute-start | bytes 196616 | tf_op jit(solution)/shard_map/ppermute | solution.py:239
  74.6 13.0 %collective-permute-done.14 = bf16[16,4,512]{2,1,0:T(4,128)(2,1)S(1)} collective-permute-done((bf16[16,4,512]{2,1,0:T(4,128)(2,1)S(1)}, bf16[16,4,512]{2,1,0:T(4,128)(2,1)S(1)}, u32[]{:S(2)}, u32[]{:S(2)}) %collective-permute-start.14) | collective-permute-done | bytes 65568 | tf_op jit(solution)/shard_map/ppermute | solution.py:239
  87.6 12.2 %collective-permute-start.9 = (bf16[16,4,512]{2,1,0:T(4,128)(2,1)S(1)}, bf16[16,4,512]{2,1,0:T(4,128)(2,1)S(1)}, u32[]{:S(2)}, u32[]{:S(2)}) collective-permute-start(bf16[16,4,512]{2,1,0:T(4,128)(2,1)S(1)} %get-tuple-element.57), channel_id=1, source_target_pairs={{0,10},{1,11},{2,8},{3,9},{4,14},{5,15},{6,12},{7,13},{8,2},{9,3},... | collective-permute-start | bytes 196616 | tf_op jit(solution)/shard_map/ppermute | solution.py:239
  100.8 2.1 %collective-permute-start.7 = (bf16[16,4,512]{2,1,0:T(4,128)(2,1)S(1)}, bf16[16,4,512]{2,1,0:T(4,128)(2,1)S(1)}, u32[]{:S(2)}, u32[]{:S(2)}) collective-permute-start(bf16[16,4,512]{2,1,0:T(4,128)(2,1)S(1)} %get-tuple-element.59), channel_id=1, source_target_pairs={{0,8},{1,9},{2,10},{3,11},{4,12},{5,13},{6,14},{7,15},{8,0},{9,1},... | collective-permute-start | bytes 196616 | tf_op jit(solution)/shard_map/ppermute | solution.py:239
  104.6 4.2 %collective-permute-done.10 = bf16[16,4,512]{2,1,0:T(4,128)(2,1)S(1)} collective-permute-done((bf16[16,4,512]{2,1,0:T(4,128)(2,1)S(1)}, bf16[16,4,512]{2,1,0:T(4,128)(2,1)S(1)}, u32[]{:S(2)}, u32[]{:S(2)}) %collective-permute-start.10) | collective-permute-done | bytes 65568 | tf_op jit(solution)/shard_map/ppermute | solution.py:239
  108.8 2.7 %collective-permute-done.9 = bf16[16,4,512]{2,1,0:T(4,128)(2,1)S(1)} collective-permute-done((bf16[16,4,512]{2,1,0:T(4,128)(2,1)S(1)}, bf16[16,4,512]{2,1,0:T(4,128)(2,1)S(1)}, u32[]{:S(2)}, u32[]{:S(2)}) %collective-permute-start.9) | collective-permute-done | bytes 65568 | tf_op jit(solution)/shard_map/ppermute | solution.py:239
  118.2 2.7 %collective-permute-done.1 = bf16[16,4,512]{2,1,0:T(4,128)(2,1)} collective-permute-done((bf16[16,4,512]{2,1,0:T(4,128)(2,1)}, bf16[16,4,512]{2,1,0:T(4,128)(2,1)}, u32[]{:S(2)}, u32[]{:S(2)}) %collective-permute-start.1) | collective-permute-done | bytes 65568 | tf_op jit(solution)/shard_map/ppermute | solution.py:239
  125.0 7.0 %stack_pairs.4 = f32[4,17,8,128]{3,2,1,0:T(8,128)S(1)} custom-call(s32[1]{0:T(128)} %bitcast.me_ref, bf16[256,2048]{1,0:T(8,128)(2,1)} %select_convert_fusion.top_hbm, bf16[256,128]{1,0:T(8,128)(2,1)S(1)} %bitcast.145, bf16[256,128]{1,0:T(8,128)(2,1)} %bitcast.12.refs_1_, bf16[256,128]{1,0:T(8,128)(2,1)} %bitcast.15.refs_2_, ...), custom_call_target="tpu_custom_call" | custom-call | flops 2147483648 | bytes 1048576 | tf_op jit(solution)/shard_map/stack_pairs/pallas_call | solution.py:155
  132.1 11.9 %stack_pairs.5 = f32[4,33,8,128]{3,2,1,0:T(8,128)S(1)} custom-call(s32[1]{0:T(128)} %bitcast.me_ref, bf16[256,2048]{1,0:T(8,128)(2,1)} %select_convert_fusion.top_hbm, bf16[16,512,128]{2,1,0:T(8,128)(2,1)S(1)} %bitcast.143), custom_call_target="tpu_custom_call" | custom-call | flops 4294967296 | bytes 2097152 | tf_op jit(solution)/shard_map/stack_pairs/pallas_call | solution.py:155
  146.4 6.1 %stack_pairs.3 = f32[16,17,8,128]{3,2,1,0:T(8,128)S(1)} custom-call(s32[1]{0:T(128)} %bitcast.me_ref, bf16[256,2048]{1,0:T(8,128)(2,1)} %select_convert_fusion.top_hbm, bf16[16,256,128]{2,1,0:T(8,128)(2,1)S(1)} %bitcast.144), custom_call_target="tpu_custom_call" | custom-call | flops 2147483648 | bytes 1048576 | tf_op jit(solution)/shard_map/stack_pairs/pallas_call | solution.py:155
  153.5 3.8 %all-to-all-start.2 = ((f16[16,17,8,128]{3,2,1,0:T(8,128)(2,1)}), f16[16,17,8,128]{3,2,1,0:T(8,128)(2,1)S(1)}, u32[]{:S(2)}, u32[]{:S(2)}) async-start(f16[16,17,8,128]{3,2,1,0:T(8,128)(2,1)} %convert_element_type.44), calls=%async_computation.2 | async-start | bytes 1114112 | tf_op jit(solution)/shard_map/all_to_all | solution.py:315
  159.8 2.6 %collective-permute-start.23 = (f16[4,33,8,128]{3,2,1,0:T(8,128)(2,1)S(1)}, f16[4,33,8,128]{3,2,1,0:T(8,128)(2,1)S(1)}, u32[]{:S(2)}, u32[]{:S(2)}) collective-permute-start(f16[4,33,8,128]{3,2,1,0:T(8,128)(2,1)S(1)} %get-tuple-element.73), channel_id=1, source_target_pairs={{0,8},{1,9},{2,10},{3,11},{4,12},{5,13},{6,14},{7,15},{8,0},{9,1},... | collective-permute-start | bytes 811016 | tf_op jit(solution)/shard_map/ppermute | solution.py:239
  162.4 2.0 collective-permute-done.16
  166.4 3.0 %collective-permute-start.26 = (f16[4,33,8,128]{3,2,1,0:T(8,128)(2,1)S(1)}, f16[4,33,8,128]{3,2,1,0:T(8,128)(2,1)S(1)}, u32[]{:S(2)}, u32[]{:S(2)}) collective-permute-start(f16[4,33,8,128]{3,2,1,0:T(8,128)(2,1)S(1)} %get-tuple-element.73), channel_id=1, source_target_pairs={{0,4},{1,5},{2,6},{3,7},{4,0},{5,1},{6,2},{7,3},{8,12},{9,13},{10,... | collective-permute-start | bytes 811016 | tf_op jit(solution)/shard_map/ppermute | solution.py:239
  169.4 18.7 %collective-permute-done.23 = f16[4,33,8,128]{3,2,1,0:T(8,128)(2,1)S(1)} collective-permute-done((f16[4,33,8,128]{3,2,1,0:T(8,128)(2,1)S(1)}, f16[4,33,8,128]{3,2,1,0:T(8,128)(2,1)S(1)}, u32[]{:S(2)}, u32[]{:S(2)}) %collective-permute-start.23) | collective-permute-done | bytes 270368 | tf_op jit(solution)/shard_map/ppermute | solution.py:239
  190.6 9.8 %collective-permute-done.25 = f16[4,17,8,128]{3,2,1,0:T(8,128)(2,1)S(1)} collective-permute-done((f16[4,17,8,128]{3,2,1,0:T(8,128)(2,1)S(1)}, f16[4,17,8,128]{3,2,1,0:T(8,128)(2,1)S(1)}, u32[]{:S(2)}, u32[]{:S(2)}) %collective-permute-start.25) | collective-permute-done | bytes 139296 | tf_op jit(solution)/shard_map/ppermute | solution.py:239
  (85 shorter events, 32.9 us)
Async XLA Ops:
  4.3 48.4 %all-to-all-start = ((bf16[512,4,512]{2,1,0:T(4,128)(2,1)}), bf16[512,4,512]{2,1,0:T(4,128)(2,1)S(1)}, u32[]{:S(2)}, u32[]{:S(2)}) async-start(bf16[512,4,512]{2,1,0:T(4,128)(2,1)} %slice.37), calls=%async_computation | async-start | bytes 4194304 | tf_op jit(solution)/shard_map/all_to_all | solution.py:306
  52.7 93.8 %all-to-all-start.1 = ((bf16[256,4,512]{2,1,0:T(4,128)(2,1)}), bf16[256,4,512]{2,1,0:T(4,128)(2,1)S(1)}, u32[]{:S(2)}, u32[]{:S(2)}) async-start(bf16[256,4,512]{2,1,0:T(4,128)(2,1)} %get-tuple-element.24), calls=%async_computation.1 | async-start | bytes 2097152 | tf_op jit(solution)/shard_map/all_to_all | solution.py:306
  66.6 21.0 %collective-permute-start.14 = (bf16[16,4,512]{2,1,0:T(4,128)(2,1)S(1)}, bf16[16,4,512]{2,1,0:T(4,128)(2,1)S(1)}, u32[]{:S(2)}, u32[]{:S(2)}) collective-permute-start(bf16[16,4,512]{2,1,0:T(4,128)(2,1)S(1)} %get-tuple-element.52), channel_id=1, source_target_pairs={{0,15},{1,14},{2,13},{3,12},{4,11},{5,10},{6,9},{7,8},{8,7},{9,6},... | collective-permute-start | bytes 196616 | tf_op jit(solution)/shard_map/ppermute | solution.py:239
  70.7 29.1 %collective-permute-start.13 = (bf16[16,4,512]{2,1,0:T(4,128)(2,1)S(1)}, bf16[16,4,512]{2,1,0:T(4,128)(2,1)S(1)}, u32[]{:S(2)}, u32[]{:S(2)}) collective-permute-start(bf16[16,4,512]{2,1,0:T(4,128)(2,1)S(1)} %get-tuple-element.53), channel_id=1, source_target_pairs={{0,14},{1,15},{2,12},{3,13},{4,10},{5,11},{6,8},{7,9},{8,6},{9,7},... | collective-permute-start | bytes 196616 | tf_op jit(solution)/shard_map/ppermute | solution.py:239
  71.1 29.7 %collective-permute-start.12 = (bf16[16,4,512]{2,1,0:T(4,128)(2,1)S(1)}, bf16[16,4,512]{2,1,0:T(4,128)(2,1)S(1)}, u32[]{:S(2)}, u32[]{:S(2)}) collective-permute-start(bf16[16,4,512]{2,1,0:T(4,128)(2,1)S(1)} %get-tuple-element.54), channel_id=1, source_target_pairs={{0,13},{1,12},{2,15},{3,14},{4,9},{5,8},{6,11},{7,10},{8,5},{9,4},... | collective-permute-start | bytes 196616 | tf_op jit(solution)/shard_map/ppermute | solution.py:239
  74.2 28.7 %collective-permute-start.11 = (bf16[16,4,512]{2,1,0:T(4,128)(2,1)S(1)}, bf16[16,4,512]{2,1,0:T(4,128)(2,1)S(1)}, u32[]{:S(2)}, u32[]{:S(2)}) collective-permute-start(bf16[16,4,512]{2,1,0:T(4,128)(2,1)S(1)} %get-tuple-element.55), channel_id=1, source_target_pairs={{0,12},{1,13},{2,14},{3,15},{4,8},{5,9},{6,10},{7,11},{8,4},{9,5},... | collective-permute-start | bytes 196616 | tf_op jit(solution)/shard_map/ppermute | solution.py:239
  74.6 34.2 %collective-permute-start.10 = (bf16[16,4,512]{2,1,0:T(4,128)(2,1)S(1)}, bf16[16,4,512]{2,1,0:T(4,128)(2,1)S(1)}, u32[]{:S(2)}, u32[]{:S(2)}) collective-permute-start(bf16[16,4,512]{2,1,0:T(4,128)(2,1)S(1)} %get-tuple-element.56), channel_id=1, source_target_pairs={{0,11},{1,10},{2,9},{3,8},{4,15},{5,14},{6,13},{7,12},{8,3},{9,2},... | collective-permute-start | bytes 196616 | tf_op jit(solution)/shard_map/ppermute | solution.py:239
  87.6 23.9 %collective-permute-start.9 = (bf16[16,4,512]{2,1,0:T(4,128)(2,1)S(1)}, bf16[16,4,512]{2,1,0:T(4,128)(2,1)S(1)}, u32[]{:S(2)}, u32[]{:S(2)}) collective-permute-start(bf16[16,4,512]{2,1,0:T(4,128)(2,1)S(1)} %get-tuple-element.57), channel_id=1, source_target_pairs={{0,10},{1,11},{2,8},{3,9},{4,14},{5,15},{6,12},{7,13},{8,2},{9,3},... | collective-permute-start | bytes 196616 | tf_op jit(solution)/shard_map/ppermute | solution.py:239
  99.8 12.3 %collective-permute-start.8 = (bf16[16,4,512]{2,1,0:T(4,128)(2,1)S(1)}, bf16[16,4,512]{2,1,0:T(4,128)(2,1)S(1)}, u32[]{:S(2)}, u32[]{:S(2)}) collective-permute-start(bf16[16,4,512]{2,1,0:T(4,128)(2,1)S(1)} %get-tuple-element.58), channel_id=1, source_target_pairs={{0,9},{1,8},{2,11},{3,10},{4,13},{5,12},{6,15},{7,14},{8,1},{9,0},... | collective-permute-start | bytes 196616 | tf_op jit(solution)/shard_map/ppermute | solution.py:239
  100.8 12.5 %collective-permute-start.7 = (bf16[16,4,512]{2,1,0:T(4,128)(2,1)S(1)}, bf16[16,4,512]{2,1,0:T(4,128)(2,1)S(1)}, u32[]{:S(2)}, u32[]{:S(2)}) collective-permute-start(bf16[16,4,512]{2,1,0:T(4,128)(2,1)S(1)} %get-tuple-element.59), channel_id=1, source_target_pairs={{0,8},{1,9},{2,10},{3,11},{4,12},{5,13},{6,14},{7,15},{8,0},{9,1},... | collective-permute-start | bytes 196616 | tf_op jit(solution)/shard_map/ppermute | solution.py:239
  102.9 12.5 %collective-permute-start.6 = (bf16[16,4,512]{2,1,0:T(4,128)(2,1)S(1)}, bf16[16,4,512]{2,1,0:T(4,128)(2,1)S(1)}, u32[]{:S(2)}, u32[]{:S(2)}) collective-permute-start(bf16[16,4,512]{2,1,0:T(4,128)(2,1)S(1)} %get-tuple-element.60), channel_id=1, source_target_pairs={{0,7},{1,6},{2,5},{3,4},{4,3},{5,2},{6,1},{7,0},{8,15},{9,14},{10,... | collective-permute-start | bytes 196616 | tf_op jit(solution)/shard_map/ppermute | solution.py:239
  108.8 8.7 %collective-permute-start.5 = (bf16[16,4,512]{2,1,0:T(4,128)(2,1)S(1)}, bf16[16,4,512]{2,1,0:T(4,128)(2,1)S(1)}, u32[]{:S(2)}, u32[]{:S(2)}) collective-permute-start(bf16[16,4,512]{2,1,0:T(4,128)(2,1)S(1)} %get-tuple-element.61), channel_id=1, source_target_pairs={{0,6},{1,7},{2,4},{3,5},{4,2},{5,3},{6,0},{7,1},{8,14},{9,15},{10,... | collective-permute-start | bytes 196616 | tf_op jit(solution)/shard_map/ppermute | solution.py:239
  112.1 6.0 %collective-permute-start.4 = (bf16[16,4,512]{2,1,0:T(4,128)(2,1)}, bf16[16,4,512]{2,1,0:T(4,128)(2,1)}, u32[]{:S(2)}, u32[]{:S(2)}) collective-permute-start(bf16[16,4,512]{2,1,0:T(4,128)(2,1)} %get-tuple-element.62), channel_id=1, source_target_pairs={{0,5},{1,4},{2,7},{3,6},{4,1},{5,0},{6,3},{7,2},{8,13},{9,12},{10,... | collective-permute-start | bytes 196616 | tf_op jit(solution)/shard_map/ppermute | solution.py:239
  144.2 14.8 %collective-permute-start.21 = (f16[33,8,128]{2,1,0:T(8,128)(2,1)S(1)}, f16[33,8,128]{2,1,0:T(8,128)(2,1)S(1)}, u32[]{:S(2)}, u32[]{:S(2)}) collective-permute-start(f16[33,8,128]{2,1,0:T(8,128)(2,1)S(1)} %get-tuple-element.44), channel_id=1, source_target_pairs={{0,2},{1,3},{2,0},{3,1},{4,6},{5,7},{6,4},{7,5},{8,10},{9,11},{10,... | collective-permute-start | bytes 202760 | tf_op jit(solution)/shard_map/ppermute | solution.py:239
  145.5 14.0 %collective-permute-start.22 = (f16[33,8,128]{2,1,0:T(8,128)(2,1)S(1)}, f16[33,8,128]{2,1,0:T(8,128)(2,1)S(1)}, u32[]{:S(2)}, u32[]{:S(2)}) collective-permute-start(f16[33,8,128]{2,1,0:T(8,128)(2,1)S(1)} %get-tuple-element.74), channel_id=1, source_target_pairs={{0,1},{1,0},{2,3},{3,2},{4,5},{5,4},{6,7},{7,6},{8,9},{9,8},{10,11... | collective-permute-start | bytes 202760 | tf_op jit(solution)/shard_map/ppermute | solution.py:239
  145.5 14.0 %collective-permute-start.20 = (f16[33,8,128]{2,1,0:T(8,128)(2,1)S(1)}, f16[33,8,128]{2,1,0:T(8,128)(2,1)S(1)}, u32[]{:S(2)}, u32[]{:S(2)}) collective-permute-start(f16[33,8,128]{2,1,0:T(8,128)(2,1)S(1)} %get-tuple-element.75), channel_id=1, source_target_pairs={{0,3},{1,2},{2,1},{3,0},{4,7},{5,6},{6,5},{7,4},{8,11},{9,10},{10,... | collective-permute-start | bytes 202760 | tf_op jit(solution)/shard_map/ppermute | solution.py:239
  153.5 53.4 %all-to-all-start.2 = ((f16[16,17,8,128]{3,2,1,0:T(8,128)(2,1)}), f16[16,17,8,128]{3,2,1,0:T(8,128)(2,1)S(1)}, u32[]{:S(2)}, u32[]{:S(2)}) async-start(f16[16,17,8,128]{3,2,1,0:T(8,128)(2,1)} %convert_element_type.44), calls=%async_computation.2 | async-start | bytes 1114112 | tf_op jit(solution)/shard_map/all_to_all | solution.py:315
  157.4 7.1 %collective-permute-start.16 = (f16[17,8,128]{2,1,0:T(8,128)(2,1)S(1)}, f16[17,8,128]{2,1,0:T(8,128)(2,1)S(1)}, u32[]{:S(2)}, u32[]{:S(2)}) collective-permute-start(f16[17,8,128]{2,1,0:T(8,128)(2,1)S(1)} %get-tuple-element.47), channel_id=1, source_target_pairs={{0,2},{1,3},{2,0},{3,1},{4,6},{5,7},{6,4},{7,5},{8,10},{9,11},{10,... | collective-permute-start | bytes 104456 | tf_op jit(solution)/shard_map/ppermute | solution.py:239
  159.8 28.3 %collective-permute-start.23 = (f16[4,33,8,128]{3,2,1,0:T(8,128)(2,1)S(1)}, f16[4,33,8,128]{3,2,1,0:T(8,128)(2,1)S(1)}, u32[]{:S(2)}, u32[]{:S(2)}) collective-permute-start(f16[4,33,8,128]{3,2,1,0:T(8,128)(2,1)S(1)} %get-tuple-element.73), channel_id=1, source_target_pairs={{0,8},{1,9},{2,10},{3,11},{4,12},{5,13},{6,14},{7,15},{8,0},{9,1},... | collective-permute-start | bytes 811016 | tf_op jit(solution)/shard_map/ppermute | solution.py:239
  164.6 26.0 %collective-permute-start.18 = (f16[4,17,8,128]{3,2,1,0:T(8,128)(2,1)S(1)}, f16[4,17,8,128]{3,2,1,0:T(8,128)(2,1)S(1)}, u32[]{:S(2)}, u32[]{:S(2)}) collective-permute-start(f16[4,17,8,128]{3,2,1,0:T(8,128)(2,1)S(1)} %get-tuple-element.81), channel_id=1, source_target_pairs={{0,8},{1,9},{2,10},{3,11},{4,12},{5,13},{6,14},{7,15},{8,0},{9,1},... | collective-permute-start | bytes 417800 | tf_op jit(solution)/shard_map/ppermute | solution.py:239
  166.4 35.9 %collective-permute-start.26 = (f16[4,33,8,128]{3,2,1,0:T(8,128)(2,1)S(1)}, f16[4,33,8,128]{3,2,1,0:T(8,128)(2,1)S(1)}, u32[]{:S(2)}, u32[]{:S(2)}) collective-permute-start(f16[4,33,8,128]{3,2,1,0:T(8,128)(2,1)S(1)} %get-tuple-element.73), channel_id=1, source_target_pairs={{0,4},{1,5},{2,6},{3,7},{4,0},{5,1},{6,2},{7,3},{8,12},{9,13},{10,... | collective-permute-start | bytes 811016 | tf_op jit(solution)/shard_map/ppermute | solution.py:239
  188.1 16.9 %collective-permute-start.24 = (f16[4,33,8,128]{3,2,1,0:T(8,128)(2,1)S(1)}, f16[4,33,8,128]{3,2,1,0:T(8,128)(2,1)S(1)}, u32[]{:S(2)}, u32[]{:S(2)}) collective-permute-start(f16[4,33,8,128]{3,2,1,0:T(8,128)(2,1)S(1)} %collective-permute-done.23), channel_id=1, source_target_pairs={{0,4},{1,5},{2,6},{3,7},{4,0},{5,1},{6,2},{7,3},{8,12},{9,13},{10,... | collective-permute-start | bytes 811016 | tf_op jit(solution)/shard_map/ppermute | solution.py:239
  188.1 12.3 %collective-permute-start.25 = (f16[4,17,8,128]{3,2,1,0:T(8,128)(2,1)S(1)}, f16[4,17,8,128]{3,2,1,0:T(8,128)(2,1)S(1)}, u32[]{:S(2)}, u32[]{:S(2)}) collective-permute-start(f16[4,17,8,128]{3,2,1,0:T(8,128)(2,1)S(1)} %get-tuple-element.81), channel_id=1, source_target_pairs={{0,4},{1,5},{2,6},{3,7},{4,0},{5,1},{6,2},{7,3},{8,12},{9,13},{10,... | collective-permute-start | bytes 417800 | tf_op jit(solution)/shard_map/ppermute | solution.py:239
  190.6 11.7 %collective-permute-start.19 = (f16[4,17,8,128]{3,2,1,0:T(8,128)(2,1)S(1)}, f16[4,17,8,128]{3,2,1,0:T(8,128)(2,1)S(1)}, u32[]{:S(2)}, u32[]{:S(2)}) collective-permute-start(f16[4,17,8,128]{3,2,1,0:T(8,128)(2,1)S(1)} %collective-permute-done.18), channel_id=1, source_target_pairs={{0,4},{1,5},{2,6},{3,7},{4,0},{5,1},{6,2},{7,3},{8,12},{9,13},{10,... | collective-permute-start | bytes 417800 | tf_op jit(solution)/shard_map/ppermute | solution.py:239
  (16 other events, 35.0 us)

commit v6 on v5

--- a/solution.py
+++ b/solution.py
@@ -173,6 +173,31 @@
         compiler_params=pltpu.CompilerParams(vmem_limit_bytes=need + 6 * 2**20),
         name="stack_pairs",
     )(me.reshape(1), pltpu.with_memory_space_constraint(top, pltpu.HBM), *moved)
+
+
+def take_kernel(corr_ref, out_ref, sems):
+    parts = sems.shape[0]
+    step = out_ref.shape[0] // parts
+    copies = [
+        pltpu.make_async_copy(corr_ref.at[pl.ds(k * step, step)], out_ref.at[pl.ds(k * step, step)], sems.at[k])
+        for k in range(parts)
+    ]
+    for copy in copies:
+        copy.start()
+    for copy in copies:
+        copy.wait()
+
+
+def take(corr, rows):
+    return pl.pallas_call(
+        take_kernel,
+        in_specs=[pl.BlockSpec(memory_space=pltpu.HBM)],
+        out_specs=pl.BlockSpec(memory_space=pltpu.VMEM),
+        out_shape=jax.ShapeDtypeStruct((rows,) + corr.shape[1:], corr.dtype),
+        scratch_shapes=[pltpu.SemaphoreType.DMA((16,))],
+        compiler_params=pltpu.CompilerParams(vmem_limit_bytes=12 * 2**20),
+        name="take",
+    )(pltpu.with_memory_space_constraint(corr, pltpu.HBM))
 
 
 def place_kernel(sizes, me_ref, *refs):
@@ -295,7 +320,7 @@
     for k, (p, how, _) in enumerate(plan):
         if k == 1:
             corr, top = lax.optimization_barrier((corr, top))
-        rows = corr[starts[k] * n:(starts[k] + p) * n]
+        rows = corr[starts[k] * n:(starts[k] + p) * n] if k else take(corr, p * n)
         if how == "swap":
             pieces = [lax.dynamic_slice_in_dim(rows, (me ^ s) * p, p, 0) for s in range(n)]
             pieces = [pieces[0]] + [swap(pieces[s], n, s) for s in range(1, n)]

time: 210 us -> 209 us (level)
  local copies, waits for them, and re-layouts: 17.7 us -> 14.1 us
  Pallas kernels: 30.7 us -> 33.8 us
    slice x2 -> x1, local copies, waits for them, and re-layouts: 7.23 us -> 3.6 us  [per_device(): rows = corr[starts[k] * n:(starts[k] + p) * n] if k else take(corr, p * n)]
    pallas_call x0 -> x1, Pallas kernels: none -> 3.06 us  [take(): pl.pallas_call(take_kernel, in_specs=[pl.BlockSpec(memory_space=pltpu.HBM...]
where the time goes in v6:
time: 209 us; the launch traced here: 208 us
  waiting for transfers between devices  82.7 us (40%)
  starting transfers between devices  65 us (31%)
  Pallas kernels  33.8 us (16%)
  local copies, waits for them, and re-layouts  14.1 us (7%)
  other arithmetic  11.8 us (6%)
    ppermute x27, waiting for transfers between devices, swap(): return lax.ppermute(x, AXES, [(i, i ^ by) for i in range(n)])  55.5 us
    ppermute x27, starting transfers between devices, swap(): return lax.ppermute(x, AXES, [(i, i ^ by) for i in range(n)])  42.4 us
    all_to_all x2, waiting for transfers between devices, per_device(): got = lax.all_to_all(rows, AXES, 0, 0, tiled=True)  27.2 us
    pallas_call x3, Pallas kernels, stack_pairs(): pl.pallas_call(functools.partial(stack_kernel, (lag_groups, days_here, gr...  25.1 us
    all_to_all x2, starting transfers between devices, per_device(): got = lax.all_to_all(rows, AXES, 0, 0, tiled=True)  18.8 us
    convert_element_type x1, other arithmetic, kernel_rows(): return value.astype(jnp.bfloat16)  10.2 us
    unnamed x21, local copies, waits for them, and re-layouts  8.08 us
    pallas_call x5, Pallas kernels, place(): pl.pallas_call(functools.partial(place_kernel, (pairs, row, moves, len(ol...  5.6 us
  transfers between devices with their start and end apart: 30, of which 10 were waited for; matrix products, arithmetic and copies ran while one was open for 9% of the time, Pallas kernels for 14%

profile of v6, /device:TPU:0, one launch (start us, length us, event | category | flops | bytes accessed | tf_op | source)
XLA Modules:
  0.0 208.4 jit_solution(8325567557763837029)
XLA Ops:
  0.6 3.1 %take.1 = bf16[512,4,512]{2,1,0:T(4,128)(2,1)} custom-call(bf16[1024,4,512]{2,1,0:T(4,128)(2,1)} %corr_ref.1), custom_call_target="tpu_custom_call" | custom-call | tf_op jit(solution)/shard_map/take/pallas_call | solution.py:192
  3.7 7.4 %all-to-all-start = ((bf16[512,4,512]{2,1,0:T(4,128)(2,1)}), bf16[512,4,512]{2,1,0:T(4,128)(2,1)S(1)}, u32[]{:S(2)}, u32[]{:S(2)}) async-start(bf16[512,4,512]{2,1,0:T(4,128)(2,1)} %take.1), calls=%async_computation | async-start | bytes 4194304 | tf_op jit(solution)/shard_map/all_to_all | solution.py:331
  11.1 10.2 %select_convert_fusion.top_hbm = bf16[256,2048]{1,0:T(8,128)(2,1)} fusion(), kind=kLoop, calls=%fused_computation.9 | loop fusion | flops 16252928 | bytes 1048576 | tf_op jit(solution)/shard_map/convert_element_type | solution.py:26
  21.3 3.6 %fusion.9 = (bf16[256,4,512]{2,1,0:T(4,128)(2,1)}, bf16[256,4,512]{2,1,0:T(4,128)(2,1)}) fusion(bf16[1024,4,512]{2,1,0:T(4,128)(2,1)} %corr_ref.1), kind=kLoop, calls=%fused_computation.66 | loop fusion | bytes 4194304 | tf_op jit(solution)/shard_map/slice | solution.py:323
  24.9 27.2 %all-to-all-done = bf16[512,4,512]{2,1,0:T(4,128)(2,1)S(1)} async-done(((bf16[512,4,512]{2,1,0:T(4,128)(2,1)}), bf16[512,4,512]{2,1,0:T(4,128)(2,1)S(1)}, u32[]{:S(2)}, u32[]{:S(2)}) %all-to-all-start) | async-done | bytes 2097184 | tf_op jit(solution)/shard_map/all_to_all | solution.py:331
  52.1 11.4 %all-to-all-start.1 = ((bf16[256,4,512]{2,1,0:T(4,128)(2,1)}), bf16[256,4,512]{2,1,0:T(4,128)(2,1)S(1)}, u32[]{:S(2)}, u32[]{:S(2)}) async-start(bf16[256,4,512]{2,1,0:T(4,128)(2,1)} %get-tuple-element.24), calls=%async_computation.1 | async-start | bytes 2097152 | tf_op jit(solution)/shard_map/all_to_all | solution.py:331
  63.6 2.4 %constant_dynamic-slice_fusion = (bf16[16,4,512]{2,1,0:T(4,128)(2,1)S(1)}, bf16[16,4,512]{2,1,0:T(4,128)(2,1)S(1)}, bf16[16,4,512]{2,1,0:T(4,128)(2,1)S(1)}, bf1...) fusion(bf16[256,4,512]{2,1,0:T(4,128)(2,1)} %get-tuple-element., ...), kind=kLoop, calls=%fused_computation.48 | loop fusion | bytes 2097216 | tf_op jit(solution)/shard_map/dynamic_slice | solution.py:325
  66.0 4.1 %collective-permute-start.14 = (bf16[16,4,512]{2,1,0:T(4,128)(2,1)S(1)}, bf16[16,4,512]{2,1,0:T(4,128)(2,1)S(1)}, u32[]{:S(2)}, u32[]{:S(2)}) collective-permute-start(bf16[16,4,512]{2,1,0:T(4,128)(2,1)S(1)} %get-tuple-element.52), channel_id=1, source_target_pairs={{0,15},{1,14},{2,13},{3,12},{4,11},{5,10},{6,9},{7,8},{8,7},{9,6},... | collective-permute-start | bytes 196616 | tf_op jit(solution)/shard_map/ppermute | solution.py:264
  70.5 3.2 %collective-permute-start.12 = (bf16[16,4,512]{2,1,0:T(4,128)(2,1)S(1)}, bf16[16,4,512]{2,1,0:T(4,128)(2,1)S(1)}, u32[]{:S(2)}, u32[]{:S(2)}) collective-permute-start(bf16[16,4,512]{2,1,0:T(4,128)(2,1)S(1)} %get-tuple-element.54), channel_id=1, source_target_pairs={{0,13},{1,12},{2,15},{3,14},{4,9},{5,8},{6,11},{7,10},{8,5},{9,4},... | collective-permute-start | bytes 196616 | tf_op jit(solution)/shard_map/ppermute | solution.py:264
  74.1 13.0 %collective-permute-done.14 = bf16[16,4,512]{2,1,0:T(4,128)(2,1)S(1)} collective-permute-done((bf16[16,4,512]{2,1,0:T(4,128)(2,1)S(1)}, bf16[16,4,512]{2,1,0:T(4,128)(2,1)S(1)}, u32[]{:S(2)}, u32[]{:S(2)}) %collective-permute-start.14) | collective-permute-done | bytes 65568 | tf_op jit(solution)/shard_map/ppermute | solution.py:264
  87.0 12.2 %collective-permute-start.9 = (bf16[16,4,512]{2,1,0:T(4,128)(2,1)S(1)}, bf16[16,4,512]{2,1,0:T(4,128)(2,1)S(1)}, u32[]{:S(2)}, u32[]{:S(2)}) collective-permute-start(bf16[16,4,512]{2,1,0:T(4,128)(2,1)S(1)} %get-tuple-element.57), channel_id=1, source_target_pairs={{0,10},{1,11},{2,8},{3,9},{4,14},{5,15},{6,12},{7,13},{8,2},{9,3},... | collective-permute-start | bytes 196616 | tf_op jit(solution)/shard_map/ppermute | solution.py:264
  100.3 2.1 %collective-permute-start.7 = (bf16[16,4,512]{2,1,0:T(4,128)(2,1)S(1)}, bf16[16,4,512]{2,1,0:T(4,128)(2,1)S(1)}, u32[]{:S(2)}, u32[]{:S(2)}) collective-permute-start(bf16[16,4,512]{2,1,0:T(4,128)(2,1)S(1)} %get-tuple-element.59), channel_id=1, source_target_pairs={{0,8},{1,9},{2,10},{3,11},{4,12},{5,13},{6,14},{7,15},{8,0},{9,1},... | collective-permute-start | bytes 196616 | tf_op jit(solution)/shard_map/ppermute | solution.py:264
  104.1 4.2 %collective-permute-done.10 = bf16[16,4,512]{2,1,0:T(4,128)(2,1)S(1)} collective-permute-done((bf16[16,4,512]{2,1,0:T(4,128)(2,1)S(1)}, bf16[16,4,512]{2,1,0:T(4,128)(2,1)S(1)}, u32[]{:S(2)}, u32[]{:S(2)}) %collective-permute-start.10) | collective-permute-done | bytes 65568 | tf_op jit(solution)/shard_map/ppermute | solution.py:264
  108.3 2.7 %collective-permute-done.9 = bf16[16,4,512]{2,1,0:T(4,128)(2,1)S(1)} collective-permute-done((bf16[16,4,512]{2,1,0:T(4,128)(2,1)S(1)}, bf16[16,4,512]{2,1,0:T(4,128)(2,1)S(1)}, u32[]{:S(2)}, u32[]{:S(2)}) %collective-permute-start.9) | collective-permute-done | bytes 65568 | tf_op jit(solution)/shard_map/ppermute | solution.py:264
  117.6 2.7 %collective-permute-done.1 = bf16[16,4,512]{2,1,0:T(4,128)(2,1)} collective-permute-done((bf16[16,4,512]{2,1,0:T(4,128)(2,1)}, bf16[16,4,512]{2,1,0:T(4,128)(2,1)}, u32[]{:S(2)}, u32[]{:S(2)}) %collective-permute-start.1) | collective-permute-done | bytes 65568 | tf_op jit(solution)/shard_map/ppermute | solution.py:264
  124.5 7.1 %stack_pairs.4 = f32[4,17,8,128]{3,2,1,0:T(8,128)S(1)} custom-call(s32[1]{0:T(128)} %bitcast.me_ref, bf16[256,2048]{1,0:T(8,128)(2,1)} %select_convert_fusion.top_hbm, bf16[256,128]{1,0:T(8,128)(2,1)S(1)} %bitcast.145, bf16[256,128]{1,0:T(8,128)(2,1)} %bitcast.12.refs_1_, bf16[256,128]{1,0:T(8,128)(2,1)} %bitcast.15.refs_2_, ...), custom_call_target="tpu_custom_call" | custom-call | flops 2147483648 | bytes 1048576 | tf_op jit(solution)/shard_map/stack_pairs/pallas_call | solution.py:155
  131.6 11.9 %stack_pairs.5 = f32[4,33,8,128]{3,2,1,0:T(8,128)S(1)} custom-call(s32[1]{0:T(128)} %bitcast.me_ref, bf16[256,2048]{1,0:T(8,128)(2,1)} %select_convert_fusion.top_hbm, bf16[16,512,128]{2,1,0:T(8,128)(2,1)S(1)} %bitcast.143), custom_call_target="tpu_custom_call" | custom-call | flops 4294967296 | bytes 2097152 | tf_op jit(solution)/shard_map/stack_pairs/pallas_call | solution.py:155
  145.9 6.1 %stack_pairs.3 = f32[16,17,8,128]{3,2,1,0:T(8,128)S(1)} custom-call(s32[1]{0:T(128)} %bitcast.me_ref, bf16[256,2048]{1,0:T(8,128)(2,1)} %select_convert_fusion.top_hbm, bf16[16,256,128]{2,1,0:T(8,128)(2,1)S(1)} %bitcast.144), custom_call_target="tpu_custom_call" | custom-call | flops 2147483648 | bytes 1048576 | tf_op jit(solution)/shard_map/stack_pairs/pallas_call | solution.py:155
  152.9 3.8 %all-to-all-start.2 = ((f16[16,17,8,128]{3,2,1,0:T(8,128)(2,1)}), f16[16,17,8,128]{3,2,1,0:T(8,128)(2,1)S(1)}, u32[]{:S(2)}, u32[]{:S(2)}) async-start(f16[16,17,8,128]{3,2,1,0:T(8,128)(2,1)} %convert_element_type.44), calls=%async_computation.2 | async-start | bytes 1114112 | tf_op jit(solution)/shard_map/all_to_all | solution.py:340
  159.2 2.6 %collective-permute-start.23 = (f16[4,33,8,128]{3,2,1,0:T(8,128)(2,1)S(1)}, f16[4,33,8,128]{3,2,1,0:T(8,128)(2,1)S(1)}, u32[]{:S(2)}, u32[]{:S(2)}) collective-permute-start(f16[4,33,8,128]{3,2,1,0:T(8,128)(2,1)S(1)} %get-tuple-element.73), channel_id=1, source_target_pairs={{0,8},{1,9},{2,10},{3,11},{4,12},{5,13},{6,14},{7,15},{8,0},{9,1},... | collective-permute-start | bytes 811016 | tf_op jit(solution)/shard_map/ppermute | solution.py:264
  161.8 2.0 collective-permute-done.16
  165.9 3.0 %collective-permute-start.26 = (f16[4,33,8,128]{3,2,1,0:T(8,128)(2,1)S(1)}, f16[4,33,8,128]{3,2,1,0:T(8,128)(2,1)S(1)}, u32[]{:S(2)}, u32[]{:S(2)}) collective-permute-start(f16[4,33,8,128]{3,2,1,0:T(8,128)(2,1)S(1)} %get-tuple-element.73), channel_id=1, source_target_pairs={{0,4},{1,5},{2,6},{3,7},{4,0},{5,1},{6,2},{7,3},{8,12},{9,13},{10,... | collective-permute-start | bytes 811016 | tf_op jit(solution)/shard_map/ppermute | solution.py:264
  168.8 18.7 %collective-permute-done.23 = f16[4,33,8,128]{3,2,1,0:T(8,128)(2,1)S(1)} collective-permute-done((f16[4,33,8,128]{3,2,1,0:T(8,128)(2,1)S(1)}, f16[4,33,8,128]{3,2,1,0:T(8,128)(2,1)S(1)}, u32[]{:S(2)}, u32[]{:S(2)}) %collective-permute-start.23) | collective-permute-done | bytes 270368 | tf_op jit(solution)/shard_map/ppermute | solution.py:264
  190.1 9.8 %collective-permute-done.25 = f16[4,17,8,128]{3,2,1,0:T(8,128)(2,1)S(1)} collective-permute-done((f16[4,17,8,128]{3,2,1,0:T(8,128)(2,1)S(1)}, f16[4,17,8,128]{3,2,1,0:T(8,128)(2,1)S(1)}, u32[]{:S(2)}, u32[]{:S(2)}) %collective-permute-start.25) | collective-permute-done | bytes 139296 | tf_op jit(solution)/shard_map/ppermute | solution.py:264
  (85 shorter events, 32.9 us)
Async XLA Ops:
  3.7 48.4 %all-to-all-start = ((bf16[512,4,512]{2,1,0:T(4,128)(2,1)}), bf16[512,4,512]{2,1,0:T(4,128)(2,1)S(1)}, u32[]{:S(2)}, u32[]{:S(2)}) async-start(bf16[512,4,512]{2,1,0:T(4,128)(2,1)} %take.1), calls=%async_computation | async-start | bytes 4194304 | tf_op jit(solution)/shard_map/all_to_all | solution.py:331
  52.1 93.8 %all-to-all-start.1 = ((bf16[256,4,512]{2,1,0:T(4,128)(2,1)}), bf16[256,4,512]{2,1,0:T(4,128)(2,1)S(1)}, u32[]{:S(2)}, u32[]{:S(2)}) async-start(bf16[256,4,512]{2,1,0:T(4,128)(2,1)} %get-tuple-element.24), calls=%async_computation.1 | async-start | bytes 2097152 | tf_op jit(solution)/shard_map/all_to_all | solution.py:331
  66.0 21.0 %collective-permute-start.14 = (bf16[16,4,512]{2,1,0:T(4,128)(2,1)S(1)}, bf16[16,4,512]{2,1,0:T(4,128)(2,1)S(1)}, u32[]{:S(2)}, u32[]{:S(2)}) collective-permute-start(bf16[16,4,512]{2,1,0:T(4,128)(2,1)S(1)} %get-tuple-element.52), channel_id=1, source_target_pairs={{0,15},{1,14},{2,13},{3,12},{4,11},{5,10},{6,9},{7,8},{8,7},{9,6},... | collective-permute-start | bytes 196616 | tf_op jit(solution)/shard_map/ppermute | solution.py:264
  70.1 29.1 %collective-permute-start.13 = (bf16[16,4,512]{2,1,0:T(4,128)(2,1)S(1)}, bf16[16,4,512]{2,1,0:T(4,128)(2,1)S(1)}, u32[]{:S(2)}, u32[]{:S(2)}) collective-permute-start(bf16[16,4,512]{2,1,0:T(4,128)(2,1)S(1)} %get-tuple-element.53), channel_id=1, source_target_pairs={{0,14},{1,15},{2,12},{3,13},{4,10},{5,11},{6,8},{7,9},{8,6},{9,7},... | collective-permute-start | bytes 196616 | tf_op jit(solution)/shard_map/ppermute | solution.py:264
  70.5 29.7 %collective-permute-start.12 = (bf16[16,4,512]{2,1,0:T(4,128)(2,1)S(1)}, bf16[16,4,512]{2,1,0:T(4,128)(2,1)S(1)}, u32[]{:S(2)}, u32[]{:S(2)}) collective-permute-start(bf16[16,4,512]{2,1,0:T(4,128)(2,1)S(1)} %get-tuple-element.54), channel_id=1, source_target_pairs={{0,13},{1,12},{2,15},{3,14},{4,9},{5,8},{6,11},{7,10},{8,5},{9,4},... | collective-permute-start | bytes 196616 | tf_op jit(solution)/shard_map/ppermute | solution.py:264
  73.7 28.7 %collective-permute-start.11 = (bf16[16,4,512]{2,1,0:T(4,128)(2,1)S(1)}, bf16[16,4,512]{2,1,0:T(4,128)(2,1)S(1)}, u32[]{:S(2)}, u32[]{:S(2)}) collective-permute-start(bf16[16,4,512]{2,1,0:T(4,128)(2,1)S(1)} %get-tuple-element.55), channel_id=1, source_target_pairs={{0,12},{1,13},{2,14},{3,15},{4,8},{5,9},{6,10},{7,11},{8,4},{9,5},... | collective-permute-start | bytes 196616 | tf_op jit(solution)/shard_map/ppermute | solution.py:264
  74.0 34.2 %collective-permute-start.10 = (bf16[16,4,512]{2,1,0:T(4,128)(2,1)S(1)}, bf16[16,4,512]{2,1,0:T(4,128)(2,1)S(1)}, u32[]{:S(2)}, u32[]{:S(2)}) collective-permute-start(bf16[16,4,512]{2,1,0:T(4,128)(2,1)S(1)} %get-tuple-element.56), channel_id=1, source_target_pairs={{0,11},{1,10},{2,9},{3,8},{4,15},{5,14},{6,13},{7,12},{8,3},{9,2},... | collective-permute-start | bytes 196616 | tf_op jit(solution)/shard_map/ppermute | solution.py:264
  87.0 23.9 %collective-permute-start.9 = (bf16[16,4,512]{2,1,0:T(4,128)(2,1)S(1)}, bf16[16,4,512]{2,1,0:T(4,128)(2,1)S(1)}, u32[]{:S(2)}, u32[]{:S(2)}) collective-permute-start(bf16[16,4,512]{2,1,0:T(4,128)(2,1)S(1)} %get-tuple-element.57), channel_id=1, source_target_pairs={{0,10},{1,11},{2,8},{3,9},{4,14},{5,15},{6,12},{7,13},{8,2},{9,3},... | collective-permute-start | bytes 196616 | tf_op jit(solution)/shard_map/ppermute | solution.py:264
  99.3 12.3 %collective-permute-start.8 = (bf16[16,4,512]{2,1,0:T(4,128)(2,1)S(1)}, bf16[16,4,512]{2,1,0:T(4,128)(2,1)S(1)}, u32[]{:S(2)}, u32[]{:S(2)}) collective-permute-start(bf16[16,4,512]{2,1,0:T(4,128)(2,1)S(1)} %get-tuple-element.58), channel_id=1, source_target_pairs={{0,9},{1,8},{2,11},{3,10},{4,13},{5,12},{6,15},{7,14},{8,1},{9,0},... | collective-permute-start | bytes 196616 | tf_op jit(solution)/shard_map/ppermute | solution.py:264
  100.3 12.5 %collective-permute-start.7 = (bf16[16,4,512]{2,1,0:T(4,128)(2,1)S(1)}, bf16[16,4,512]{2,1,0:T(4,128)(2,1)S(1)}, u32[]{:S(2)}, u32[]{:S(2)}) collective-permute-start(bf16[16,4,512]{2,1,0:T(4,128)(2,1)S(1)} %get-tuple-element.59), channel_id=1, source_target_pairs={{0,8},{1,9},{2,10},{3,11},{4,12},{5,13},{6,14},{7,15},{8,0},{9,1},... | collective-permute-start | bytes 196616 | tf_op jit(solution)/shard_map/ppermute | solution.py:264
  102.4 12.5 %collective-permute-start.6 = (bf16[16,4,512]{2,1,0:T(4,128)(2,1)S(1)}, bf16[16,4,512]{2,1,0:T(4,128)(2,1)S(1)}, u32[]{:S(2)}, u32[]{:S(2)}) collective-permute-start(bf16[16,4,512]{2,1,0:T(4,128)(2,1)S(1)} %get-tuple-element.60), channel_id=1, source_target_pairs={{0,7},{1,6},{2,5},{3,4},{4,3},{5,2},{6,1},{7,0},{8,15},{9,14},{10,... | collective-permute-start | bytes 196616 | tf_op jit(solution)/shard_map/ppermute | solution.py:264
  108.3 8.7 %collective-permute-start.5 = (bf16[16,4,512]{2,1,0:T(4,128)(2,1)S(1)}, bf16[16,4,512]{2,1,0:T(4,128)(2,1)S(1)}, u32[]{:S(2)}, u32[]{:S(2)}) collective-permute-start(bf16[16,4,512]{2,1,0:T(4,128)(2,1)S(1)} %get-tuple-element.61), channel_id=1, source_target_pairs={{0,6},{1,7},{2,4},{3,5},{4,2},{5,3},{6,0},{7,1},{8,14},{9,15},{10,... | collective-permute-start | bytes 196616 | tf_op jit(solution)/shard_map/ppermute | solution.py:264
  111.6 6.0 %collective-permute-start.4 = (bf16[16,4,512]{2,1,0:T(4,128)(2,1)}, bf16[16,4,512]{2,1,0:T(4,128)(2,1)}, u32[]{:S(2)}, u32[]{:S(2)}) collective-permute-start(bf16[16,4,512]{2,1,0:T(4,128)(2,1)} %get-tuple-element.62), channel_id=1, source_target_pairs={{0,5},{1,4},{2,7},{3,6},{4,1},{5,0},{6,3},{7,2},{8,13},{9,12},{10,... | collective-permute-start | bytes 196616 | tf_op jit(solution)/shard_map/ppermute | solution.py:264
  143.7 14.8 %collective-permute-start.21 = (f16[33,8,128]{2,1,0:T(8,128)(2,1)S(1)}, f16[33,8,128]{2,1,0:T(8,128)(2,1)S(1)}, u32[]{:S(2)}, u32[]{:S(2)}) collective-permute-start(f16[33,8,128]{2,1,0:T(8,128)(2,1)S(1)} %get-tuple-element.44), channel_id=1, source_target_pairs={{0,2},{1,3},{2,0},{3,1},{4,6},{5,7},{6,4},{7,5},{8,10},{9,11},{10,... | collective-permute-start | bytes 202760 | tf_op jit(solution)/shard_map/ppermute | solution.py:264
  145.0 14.0 %collective-permute-start.22 = (f16[33,8,128]{2,1,0:T(8,128)(2,1)S(1)}, f16[33,8,128]{2,1,0:T(8,128)(2,1)S(1)}, u32[]{:S(2)}, u32[]{:S(2)}) collective-permute-start(f16[33,8,128]{2,1,0:T(8,128)(2,1)S(1)} %get-tuple-element.74), channel_id=1, source_target_pairs={{0,1},{1,0},{2,3},{3,2},{4,5},{5,4},{6,7},{7,6},{8,9},{9,8},{10,11... | collective-permute-start | bytes 202760 | tf_op jit(solution)/shard_map/ppermute | solution.py:264
  145.0 14.0 %collective-permute-start.20 = (f16[33,8,128]{2,1,0:T(8,128)(2,1)S(1)}, f16[33,8,128]{2,1,0:T(8,128)(2,1)S(1)}, u32[]{:S(2)}, u32[]{:S(2)}) collective-permute-start(f16[33,8,128]{2,1,0:T(8,128)(2,1)S(1)} %get-tuple-element.75), channel_id=1, source_target_pairs={{0,3},{1,2},{2,1},{3,0},{4,7},{5,6},{6,5},{7,4},{8,11},{9,10},{10,... | collective-permute-start | bytes 202760 | tf_op jit(solution)/shard_map/ppermute | solution.py:264
  152.9 53.4 %all-to-all-start.2 = ((f16[16,17,8,128]{3,2,1,0:T(8,128)(2,1)}), f16[16,17,8,128]{3,2,1,0:T(8,128)(2,1)S(1)}, u32[]{:S(2)}, u32[]{:S(2)}) async-start(f16[16,17,8,128]{3,2,1,0:T(8,128)(2,1)} %convert_element_type.44), calls=%async_computation.2 | async-start | bytes 1114112 | tf_op jit(solution)/shard_map/all_to_all | solution.py:340
  156.8 7.1 %collective-permute-start.16 = (f16[17,8,128]{2,1,0:T(8,128)(2,1)S(1)}, f16[17,8,128]{2,1,0:T(8,128)(2,1)S(1)}, u32[]{:S(2)}, u32[]{:S(2)}) collective-permute-start(f16[17,8,128]{2,1,0:T(8,128)(2,1)S(1)} %get-tuple-element.47), channel_id=1, source_target_pairs={{0,2},{1,3},{2,0},{3,1},{4,6},{5,7},{6,4},{7,5},{8,10},{9,11},{10,... | collective-permute-start | bytes 104456 | tf_op jit(solution)/shard_map/ppermute | solution.py:264
  159.2 28.3 %collective-permute-start.23 = (f16[4,33,8,128]{3,2,1,0:T(8,128)(2,1)S(1)}, f16[4,33,8,128]{3,2,1,0:T(8,128)(2,1)S(1)}, u32[]{:S(2)}, u32[]{:S(2)}) collective-permute-start(f16[4,33,8,128]{3,2,1,0:T(8,128)(2,1)S(1)} %get-tuple-element.73), channel_id=1, source_target_pairs={{0,8},{1,9},{2,10},{3,11},{4,12},{5,13},{6,14},{7,15},{8,0},{9,1},... | collective-permute-start | bytes 811016 | tf_op jit(solution)/shard_map/ppermute | solution.py:264
  164.0 26.1 %collective-permute-start.18 = (f16[4,17,8,128]{3,2,1,0:T(8,128)(2,1)S(1)}, f16[4,17,8,128]{3,2,1,0:T(8,128)(2,1)S(1)}, u32[]{:S(2)}, u32[]{:S(2)}) collective-permute-start(f16[4,17,8,128]{3,2,1,0:T(8,128)(2,1)S(1)} %get-tuple-element.81), channel_id=1, source_target_pairs={{0,8},{1,9},{2,10},{3,11},{4,12},{5,13},{6,14},{7,15},{8,0},{9,1},... | collective-permute-start | bytes 417800 | tf_op jit(solution)/shard_map/ppermute | solution.py:264
  165.9 35.9 %collective-permute-start.26 = (f16[4,33,8,128]{3,2,1,0:T(8,128)(2,1)S(1)}, f16[4,33,8,128]{3,2,1,0:T(8,128)(2,1)S(1)}, u32[]{:S(2)}, u32[]{:S(2)}) collective-permute-start(f16[4,33,8,128]{3,2,1,0:T(8,128)(2,1)S(1)} %get-tuple-element.73), channel_id=1, source_target_pairs={{0,4},{1,5},{2,6},{3,7},{4,0},{5,1},{6,2},{7,3},{8,12},{9,13},{10,... | collective-permute-start | bytes 811016 | tf_op jit(solution)/shard_map/ppermute | solution.py:264
  187.6 16.9 %collective-permute-start.24 = (f16[4,33,8,128]{3,2,1,0:T(8,128)(2,1)S(1)}, f16[4,33,8,128]{3,2,1,0:T(8,128)(2,1)S(1)}, u32[]{:S(2)}, u32[]{:S(2)}) collective-permute-start(f16[4,33,8,128]{3,2,1,0:T(8,128)(2,1)S(1)} %collective-permute-done.23), channel_id=1, source_target_pairs={{0,4},{1,5},{2,6},{3,7},{4,0},{5,1},{6,2},{7,3},{8,12},{9,13},{10,... | collective-permute-start | bytes 811016 | tf_op jit(solution)/shard_map/ppermute | solution.py:264
  187.6 12.3 %collective-permute-start.25 = (f16[4,17,8,128]{3,2,1,0:T(8,128)(2,1)S(1)}, f16[4,17,8,128]{3,2,1,0:T(8,128)(2,1)S(1)}, u32[]{:S(2)}, u32[]{:S(2)}) collective-permute-start(f16[4,17,8,128]{3,2,1,0:T(8,128)(2,1)S(1)} %get-tuple-element.81), channel_id=1, source_target_pairs={{0,4},{1,5},{2,6},{3,7},{4,0},{5,1},{6,2},{7,3},{8,12},{9,13},{10,... | collective-permute-start | bytes 417800 | tf_op jit(solution)/shard_map/ppermute | solution.py:264
  190.1 11.7 %collective-permute-start.19 = (f16[4,17,8,128]{3,2,1,0:T(8,128)(2,1)S(1)}, f16[4,17,8,128]{3,2,1,0:T(8,128)(2,1)S(1)}, u32[]{:S(2)}, u32[]{:S(2)}) collective-permute-start(f16[4,17,8,128]{3,2,1,0:T(8,128)(2,1)S(1)} %collective-permute-done.18), channel_id=1, source_target_pairs={{0,4},{1,5},{2,6},{3,7},{4,0},{5,1},{6,2},{7,3},{8,12},{9,13},{10,... | collective-permute-start | bytes 417800 | tf_op jit(solution)/shard_map/ppermute | solution.py:264
  (16 other events, 35.0 us)
